TPU v7x, 128 devices: a whole 4x4x4 slice. The times are simulated.
128 devices in a mesh: atom: 8 (over x, core), tm: 16 (over z, y).
Axes of the slice: x: 4, y: 4, z: 4, core: 2. Of those that a mesh axis runs over, the one named last changes fastest.
Arguments:
- positions: int32 [128, 3, 16384], P('tm', None, 'atom'), may hold values from 0 to 131071, as said below
- velocity: bfloat16 [128, 3, 16384], P('tm', None, 'atom'), may hold values from -5 to 5
Outputs:
- correlation: float32 [4, 16, 32768], P(None, None, ('atom', 'tm'))
Inputs may be any that keep to these rules, and one draw needn't show every extreme that they name: `positions`: along each axis an atom's coordinate changes between consecutive frames by at most 1536 lattice points, counted modulo 131072.
All inputs are finite; a program needn't handle non-finite values.
Results may differ from a plain program's by a relative error of at most 0.00075.
Values may be sent and summed in bfloat16 or wider, within the bound.
No kernel may reach another device: no remote copies, remote signals or barrier semaphores. Data moves between devices by JAX's collectives and lax.ppermute only.
A program may use at most 128 MiB of HBM per device.

v0:
```python
import math

import jax
import jax.numpy as jnp
from jax import lax
from jax.sharding import PartitionSpec as P

KX = 32
KY = 32
KZ = 32
LAGS = 16
LATTICE = 131072


def wave_numbers(number, offset, extent):
    counter = jnp.arange(number, dtype=jnp.int32) + offset
    return counter - extent // 2 + (counter >= extent // 2).astype(jnp.int32)


def phase_pair(coords, numbers):
    folded = numbers[None, :, None] * coords[:, None, :] % LATTICE
    angles = folded.astype(jnp.float32) * (2.0 * math.pi / LATTICE)
    return (jnp.cos(angles), jnp.sin(angles))


def operands(positions, velocity, kx_first, kx_number):
    frame_count, atom_count = (positions.shape[0], positions.shape[2])
    cos_x, sin_x = phase_pair(positions[:, 0], wave_numbers(kx_number, kx_first, KX))
    cos_y, sin_y = phase_pair(positions[:, 1], wave_numbers(KY, 0, KY))
    cos_z, sin_z = phase_pair(positions[:, 2], wave_numbers(KZ, 0, KZ))
    real_xy = cos_x[:, :, None] * cos_y[:, None] - sin_x[:, :, None] * sin_y[:, None]
    imag_xy = cos_x[:, :, None] * sin_y[:, None] + sin_x[:, :, None] * cos_y[:, None]
    left_side = jnp.concatenate([real_xy, imag_xy], 1)
    left_side = left_side.reshape(frame_count, 2 * kx_number * KY, atom_count).astype(jnp.bfloat16)
    weights = jnp.concatenate(
        [jnp.ones((frame_count, 1, atom_count), jnp.float32), velocity.astype(jnp.float32)], 1
    )
    right_side = jnp.stack(
        [cos_z[:, None] * weights[:, :, None], sin_z[:, None] * weights[:, :, None]], 2
    )
    right_side = right_side.reshape(frame_count, -1, atom_count).astype(jnp.bfloat16)
    return (left_side, right_side)


def finish(raw, row_count):
    frame_count = raw.shape[0]
    split = raw.reshape(frame_count, 2, row_count, -1, 2, KZ)
    real_part = split[:, 0, :, :, 0] - split[:, 1, :, :, 1]
    imag_part = split[:, 0, :, :, 1] + split[:, 1, :, :, 0]
    joined = jnp.stack([real_part, imag_part], 3)
    return jnp.transpose(joined, (1, 0, 2, 3, 4)).reshape(row_count, -1)


def mode_rows(positions, velocity, kx_first, kx_number):
    frame_count, atom_count = (positions.shape[0], positions.shape[2])
    atom_block = math.gcd(atom_count, 256)
    row_count = kx_number * KY
    channels = (velocity.shape[1] + 1) * 2 * KZ

    def accumulate(running, block_index):
        pos_block = lax.dynamic_slice_in_dim(positions, block_index * atom_block, atom_block, 2)
        vel_block = lax.dynamic_slice_in_dim(velocity, block_index * atom_block, atom_block, 2)
        left_side, right_side = operands(pos_block, vel_block, kx_first, kx_number)
        product = jnp.einsum(
            "fra,fca->frc", left_side, right_side, preferred_element_type=jnp.float32
        )
        return (running + product, None)

    initial = jnp.zeros((frame_count, 2 * row_count, channels), jnp.float32)
    running = lax.scan(accumulate, initial, jnp.arange(atom_count // atom_block, dtype=jnp.int32))[
        0
    ]
    return finish(running, row_count)


def lag_sum(anchors, partners, divisor):
    product = (anchors * partners).reshape(anchors.shape[0], anchors.shape[1], -1, 2, KZ)
    return jnp.sum(product, axis=(1, 3)) / divisor


def arrange(results):
    stacked = jnp.stack(results)
    return jnp.transpose(stacked, (2, 0, 1, 3)).reshape(stacked.shape[2], LAGS, -1)


def per_device(positions, velocity):
    atom_ways = lax.axis_size("atom")
    time_ways = lax.axis_size("tm")
    frame_count = positions.shape[0]
    atom_local = positions.shape[2]
    row_count = KX * KY // atom_ways
    channels = (velocity.shape[1] + 1) * 2 * KZ
    local_modes = lax.psum_scatter(
        mode_rows(positions, velocity, jnp.int32(0) // KY, row_count * lax.axis_size("atom") // KY),
        "atom",
        scatter_dimension=0,
        tiled=True,
    )
    local_modes = local_modes.reshape(row_count, frame_count, channels)
    total_frames = frame_count * time_ways
    atom_total = atom_local * atom_ways
    results = []
    series = lax.all_to_all(local_modes, "tm", split_axis=0, concat_axis=1, tiled=True)
    for lag_index in range(LAGS):
        divisor = atom_total * (total_frames - lag_index)
        results.append(
            lag_sum(series[:, : total_frames - lag_index], series[:, lag_index:], divisor)
        )
    return arrange(results)


def solution(mesh):
    in_specs = (P("tm", None, "atom"), P("tm", None, "atom"))
    out_specs = P(None, None, ("atom", "tm"))
    return jax.shard_map(
        per_device, mesh=mesh, in_specs=in_specs, out_specs=out_specs, check_vma=False
    )
```

profile of v0, /device:TPU:1, one launch (start us, length us, event | category | flops | bytes accessed | tf_op | source)
XLA Modules:
  0.0 439.3 jit_solution(13592355053765040569)
XLA Ops:
  6.5 271.4 %while.14 = (s32[]{:T(128)}, f32[8,2048,256]{2,1,0:T(8,128)}, s32[8]{0:T(128)S(1)}, s32[8,3,2048]{2,0,1:T(8,128)}, bf16[8,3,2048]{2,0,1:T(8,128)(2,1)}, /*index=...) while((s32[]{:T(128)}, f32[8,2048,256]{2,1,0:T(8,128)}, s32[8]{0:T(128)S(1)}, ...), condition=%wide.region_1.2_spmd.clone, body=%wide.region_0.1_spmd.clone.sunk | while | flops 2181177600 | bytes 74650080 | solution.py:70
  8.7 0.7 dynamic-slice_bitcast_fusion.4
  9.4 3.1 fusion.60
  12.9 4.5 %subtract_convert_fusion.2 = (bf16[8,32,32,256]{3,2,1,0:T(8,128)(2,1)}, bf16[8,32,32,256]{3,2,1,0:T(8,128)(2,1)}) fusion(f32[8,32,256]{2,1,0:T(8,128)S(1)} %get-tuple-element.220, f32[8,32,256]{2,1,0:T(8,128)S(1)} %get-tuple-element.221, f32[8,32,256]{2,1,0:T(8,128)S(1)} %get-tuple-element.222, f32[8,32,256]{2,1,0:T(8,128)S(1)} %get-tuple-element.223), kind=kLoop, calls=%fused_computation.3.clone.1 | loop fusion | flops 16777216 | bytes 9437184 | tf_op jit(solution)/shard_map/convert.4
  17.4 7.4 %pad_maximum_fusion.4 = bf16[8,64,32,256]{3,2,1,0:T(8,128)(2,1)} fusion(bf16[8,32,32,256]{3,2,1,0:T(8,128)(2,1)} %get-tuple-element.224, bf16[8,32,32,256]{3,2,1,0:T(8,128)(2,1)} %get-tuple-element.225), kind=kLoop, calls=%fused_computation.1.clone.1 | loop fusion | flops 4194304 | bytes 16777216 | tf_op jit(solution)/shard_map/while/body/eval_jaxpr/concatenate | solution.py:33
  24.8 11.5 %select_add_fusion.2 = f32[8,2048,256]{2,1,0:T(8,128)} fusion(f32[8,2048,256]{2,1,0:T(8,128)} %get-tuple-element.242, pred[]{:T(512)S(6)} %compare.12, bf16[8,2048,256]{2,1,0:T(8,128)(2,1)} %bitcast.119, bf16[8,256,256]{2,1,0:T(8,128)(2,1)S(1)} %bitcast.120), kind=kOutput, calls=%fused_computation.clone.1 | convolution fusion | flops 2155872256 | bytes 42991616 | tf_op jit(solution)/shard_map/while/body/eval_jaxpr/fra,fca->frc/dot_general | solution.py:64
  38.4 0.7 dynamic-slice_bitcast_fusion.4
  39.2 3.1 fusion.60
  42.7 4.5 %subtract_convert_fusion.2 = (bf16[8,32,32,256]{3,2,1,0:T(8,128)(2,1)}, bf16[8,32,32,256]{3,2,1,0:T(8,128)(2,1)}) fusion(f32[8,32,256]{2,1,0:T(8,128)S(1)} %get-tuple-element.220, f32[8,32,256]{2,1,0:T(8,128)S(1)} %get-tuple-element.221, f32[8,32,256]{2,1,0:T(8,128)S(1)} %get-tuple-element.222, f32[8,32,256]{2,1,0:T(8,128)S(1)} %get-tuple-element.223), kind=kLoop, calls=%fused_computation.3.clone.1 | loop fusion | flops 16777216 | bytes 9437184 | tf_op jit(solution)/shard_map/convert.4
  47.2 7.4 %pad_maximum_fusion.4 = bf16[8,64,32,256]{3,2,1,0:T(8,128)(2,1)} fusion(bf16[8,32,32,256]{3,2,1,0:T(8,128)(2,1)} %get-tuple-element.224, bf16[8,32,32,256]{3,2,1,0:T(8,128)(2,1)} %get-tuple-element.225), kind=kLoop, calls=%fused_computation.1.clone.1 | loop fusion | flops 4194304 | bytes 16777216 | tf_op jit(solution)/shard_map/while/body/eval_jaxpr/concatenate | solution.py:33
  54.6 16.2 %select_add_fusion.2 = f32[8,2048,256]{2,1,0:T(8,128)} fusion(f32[8,2048,256]{2,1,0:T(8,128)} %get-tuple-element.242, pred[]{:T(512)S(6)} %compare.12, bf16[8,2048,256]{2,1,0:T(8,128)(2,1)} %bitcast.119, bf16[8,256,256]{2,1,0:T(8,128)(2,1)S(1)} %bitcast.120), kind=kOutput, calls=%fused_computation.clone.1 | convolution fusion | flops 2155872256 | bytes 42991616 | tf_op jit(solution)/shard_map/while/body/eval_jaxpr/fra,fca->frc/dot_general | solution.py:64
  72.9 0.7 dynamic-slice_bitcast_fusion.4
  73.7 3.1 fusion.60
  77.2 4.5 %subtract_convert_fusion.2 = (bf16[8,32,32,256]{3,2,1,0:T(8,128)(2,1)}, bf16[8,32,32,256]{3,2,1,0:T(8,128)(2,1)}) fusion(f32[8,32,256]{2,1,0:T(8,128)S(1)} %get-tuple-element.220, f32[8,32,256]{2,1,0:T(8,128)S(1)} %get-tuple-element.221, f32[8,32,256]{2,1,0:T(8,128)S(1)} %get-tuple-element.222, f32[8,32,256]{2,1,0:T(8,128)S(1)} %get-tuple-element.223), kind=kLoop, calls=%fused_computation.3.clone.1 | loop fusion | flops 16777216 | bytes 9437184 | tf_op jit(solution)/shard_map/convert.4
  81.7 7.4 %pad_maximum_fusion.4 = bf16[8,64,32,256]{3,2,1,0:T(8,128)(2,1)} fusion(bf16[8,32,32,256]{3,2,1,0:T(8,128)(2,1)} %get-tuple-element.224, bf16[8,32,32,256]{3,2,1,0:T(8,128)(2,1)} %get-tuple-element.225), kind=kLoop, calls=%fused_computation.1.clone.1 | loop fusion | flops 4194304 | bytes 16777216 | tf_op jit(solution)/shard_map/while/body/eval_jaxpr/concatenate | solution.py:33
  89.1 16.2 %select_add_fusion.2 = f32[8,2048,256]{2,1,0:T(8,128)} fusion(f32[8,2048,256]{2,1,0:T(8,128)} %get-tuple-element.242, pred[]{:T(512)S(6)} %compare.12, bf16[8,2048,256]{2,1,0:T(8,128)(2,1)} %bitcast.119, bf16[8,256,256]{2,1,0:T(8,128)(2,1)S(1)} %bitcast.120), kind=kOutput, calls=%fused_computation.clone.1 | convolution fusion | flops 2155872256 | bytes 42991616 | tf_op jit(solution)/shard_map/while/body/eval_jaxpr/fra,fca->frc/dot_general | solution.py:64
  107.5 0.7 dynamic-slice_bitcast_fusion.4
  108.2 3.1 fusion.60
  111.7 4.5 %subtract_convert_fusion.2 = (bf16[8,32,32,256]{3,2,1,0:T(8,128)(2,1)}, bf16[8,32,32,256]{3,2,1,0:T(8,128)(2,1)}) fusion(f32[8,32,256]{2,1,0:T(8,128)S(1)} %get-tuple-element.220, f32[8,32,256]{2,1,0:T(8,128)S(1)} %get-tuple-element.221, f32[8,32,256]{2,1,0:T(8,128)S(1)} %get-tuple-element.222, f32[8,32,256]{2,1,0:T(8,128)S(1)} %get-tuple-element.223), kind=kLoop, calls=%fused_computation.3.clone.1 | loop fusion | flops 16777216 | bytes 9437184 | tf_op jit(solution)/shard_map/convert.4
  116.2 7.4 %pad_maximum_fusion.4 = bf16[8,64,32,256]{3,2,1,0:T(8,128)(2,1)} fusion(bf16[8,32,32,256]{3,2,1,0:T(8,128)(2,1)} %get-tuple-element.224, bf16[8,32,32,256]{3,2,1,0:T(8,128)(2,1)} %get-tuple-element.225), kind=kLoop, calls=%fused_computation.1.clone.1 | loop fusion | flops 4194304 | bytes 16777216 | tf_op jit(solution)/shard_map/while/body/eval_jaxpr/concatenate | solution.py:33
  123.6 16.2 %select_add_fusion.2 = f32[8,2048,256]{2,1,0:T(8,128)} fusion(f32[8,2048,256]{2,1,0:T(8,128)} %get-tuple-element.242, pred[]{:T(512)S(6)} %compare.12, bf16[8,2048,256]{2,1,0:T(8,128)(2,1)} %bitcast.119, bf16[8,256,256]{2,1,0:T(8,128)(2,1)S(1)} %bitcast.120), kind=kOutput, calls=%fused_computation.clone.1 | convolution fusion | flops 2155872256 | bytes 42991616 | tf_op jit(solution)/shard_map/while/body/eval_jaxpr/fra,fca->frc/dot_general | solution.py:64
  142.0 0.7 dynamic-slice_bitcast_fusion.4
  142.7 3.1 fusion.60
  146.2 4.5 %subtract_convert_fusion.2 = (bf16[8,32,32,256]{3,2,1,0:T(8,128)(2,1)}, bf16[8,32,32,256]{3,2,1,0:T(8,128)(2,1)}) fusion(f32[8,32,256]{2,1,0:T(8,128)S(1)} %get-tuple-element.220, f32[8,32,256]{2,1,0:T(8,128)S(1)} %get-tuple-element.221, f32[8,32,256]{2,1,0:T(8,128)S(1)} %get-tuple-element.222, f32[8,32,256]{2,1,0:T(8,128)S(1)} %get-tuple-element.223), kind=kLoop, calls=%fused_computation.3.clone.1 | loop fusion | flops 16777216 | bytes 9437184 | tf_op jit(solution)/shard_map/convert.4
  150.7 7.4 %pad_maximum_fusion.4 = bf16[8,64,32,256]{3,2,1,0:T(8,128)(2,1)} fusion(bf16[8,32,32,256]{3,2,1,0:T(8,128)(2,1)} %get-tuple-element.224, bf16[8,32,32,256]{3,2,1,0:T(8,128)(2,1)} %get-tuple-element.225), kind=kLoop, calls=%fused_computation.1.clone.1 | loop fusion | flops 4194304 | bytes 16777216 | tf_op jit(solution)/shard_map/while/body/eval_jaxpr/concatenate | solution.py:33
  158.1 16.2 %select_add_fusion.2 = f32[8,2048,256]{2,1,0:T(8,128)} fusion(f32[8,2048,256]{2,1,0:T(8,128)} %get-tuple-element.242, pred[]{:T(512)S(6)} %compare.12, bf16[8,2048,256]{2,1,0:T(8,128)(2,1)} %bitcast.119, bf16[8,256,256]{2,1,0:T(8,128)(2,1)S(1)} %bitcast.120), kind=kOutput, calls=%fused_computation.clone.1 | convolution fusion | flops 2155872256 | bytes 42991616 | tf_op jit(solution)/shard_map/while/body/eval_jaxpr/fra,fca->frc/dot_general | solution.py:64
  176.5 0.7 dynamic-slice_bitcast_fusion.4
  177.2 3.1 fusion.60
  180.8 4.5 %subtract_convert_fusion.2 = (bf16[8,32,32,256]{3,2,1,0:T(8,128)(2,1)}, bf16[8,32,32,256]{3,2,1,0:T(8,128)(2,1)}) fusion(f32[8,32,256]{2,1,0:T(8,128)S(1)} %get-tuple-element.220, f32[8,32,256]{2,1,0:T(8,128)S(1)} %get-tuple-element.221, f32[8,32,256]{2,1,0:T(8,128)S(1)} %get-tuple-element.222, f32[8,32,256]{2,1,0:T(8,128)S(1)} %get-tuple-element.223), kind=kLoop, calls=%fused_computation.3.clone.1 | loop fusion | flops 16777216 | bytes 9437184 | tf_op jit(solution)/shard_map/convert.4
  185.2 7.4 %pad_maximum_fusion.4 = bf16[8,64,32,256]{3,2,1,0:T(8,128)(2,1)} fusion(bf16[8,32,32,256]{3,2,1,0:T(8,128)(2,1)} %get-tuple-element.224, bf16[8,32,32,256]{3,2,1,0:T(8,128)(2,1)} %get-tuple-element.225), kind=kLoop, calls=%fused_computation.1.clone.1 | loop fusion | flops 4194304 | bytes 16777216 | tf_op jit(solution)/shard_map/while/body/eval_jaxpr/concatenate | solution.py:33
  192.6 16.3 %select_add_fusion.2 = f32[8,2048,256]{2,1,0:T(8,128)} fusion(f32[8,2048,256]{2,1,0:T(8,128)} %get-tuple-element.242, pred[]{:T(512)S(6)} %compare.12, bf16[8,2048,256]{2,1,0:T(8,128)(2,1)} %bitcast.119, bf16[8,256,256]{2,1,0:T(8,128)(2,1)S(1)} %bitcast.120), kind=kOutput, calls=%fused_computation.clone.1 | convolution fusion | flops 2155872256 | bytes 42991616 | tf_op jit(solution)/shard_map/while/body/eval_jaxpr/fra,fca->frc/dot_general | solution.py:64
  211.8 3.1 fusion.60
  215.3 4.5 %subtract_convert_fusion.2 = (bf16[8,32,32,256]{3,2,1,0:T(8,128)(2,1)}, bf16[8,32,32,256]{3,2,1,0:T(8,128)(2,1)}) fusion(f32[8,32,256]{2,1,0:T(8,128)S(1)} %get-tuple-element.220, f32[8,32,256]{2,1,0:T(8,128)S(1)} %get-tuple-element.221, f32[8,32,256]{2,1,0:T(8,128)S(1)} %get-tuple-element.222, f32[8,32,256]{2,1,0:T(8,128)S(1)} %get-tuple-element.223), kind=kLoop, calls=%fused_computation.3.clone.1 | loop fusion | flops 16777216 | bytes 9437184 | tf_op jit(solution)/shard_map/convert.4
  219.8 7.4 %pad_maximum_fusion.4 = bf16[8,64,32,256]{3,2,1,0:T(8,128)(2,1)} fusion(bf16[8,32,32,256]{3,2,1,0:T(8,128)(2,1)} %get-tuple-element.224, bf16[8,32,32,256]{3,2,1,0:T(8,128)(2,1)} %get-tuple-element.225), kind=kLoop, calls=%fused_computation.1.clone.1 | loop fusion | flops 4194304 | bytes 16777216 | tf_op jit(solution)/shard_map/while/body/eval_jaxpr/concatenate | solution.py:33
  227.2 16.2 %select_add_fusion.2 = f32[8,2048,256]{2,1,0:T(8,128)} fusion(f32[8,2048,256]{2,1,0:T(8,128)} %get-tuple-element.242, pred[]{:T(512)S(6)} %compare.12, bf16[8,2048,256]{2,1,0:T(8,128)(2,1)} %bitcast.119, bf16[8,256,256]{2,1,0:T(8,128)(2,1)S(1)} %bitcast.120), kind=kOutput, calls=%fused_computation.clone.1 | convolution fusion | flops 2155872256 | bytes 42991616 | tf_op jit(solution)/shard_map/while/body/eval_jaxpr/fra,fca->frc/dot_general | solution.py:64
  246.3 3.1 fusion.60
  249.8 4.5 %subtract_convert_fusion.2 = (bf16[8,32,32,256]{3,2,1,0:T(8,128)(2,1)}, bf16[8,32,32,256]{3,2,1,0:T(8,128)(2,1)}) fusion(f32[8,32,256]{2,1,0:T(8,128)S(1)} %get-tuple-element.220, f32[8,32,256]{2,1,0:T(8,128)S(1)} %get-tuple-element.221, f32[8,32,256]{2,1,0:T(8,128)S(1)} %get-tuple-element.222, f32[8,32,256]{2,1,0:T(8,128)S(1)} %get-tuple-element.223), kind=kLoop, calls=%fused_computation.3.clone.1 | loop fusion | flops 16777216 | bytes 9437184 | tf_op jit(solution)/shard_map/convert.4
  254.3 7.4 %pad_maximum_fusion.4 = bf16[8,64,32,256]{3,2,1,0:T(8,128)(2,1)} fusion(bf16[8,32,32,256]{3,2,1,0:T(8,128)(2,1)} %get-tuple-element.224, bf16[8,32,32,256]{3,2,1,0:T(8,128)(2,1)} %get-tuple-element.225), kind=kLoop, calls=%fused_computation.1.clone.1 | loop fusion | flops 4194304 | bytes 16777216 | tf_op jit(solution)/shard_map/while/body/eval_jaxpr/concatenate | solution.py:33
  261.7 16.2 %select_add_fusion.2 = f32[8,2048,256]{2,1,0:T(8,128)} fusion(f32[8,2048,256]{2,1,0:T(8,128)} %get-tuple-element.242, pred[]{:T(512)S(6)} %compare.12, bf16[8,2048,256]{2,1,0:T(8,128)(2,1)} %bitcast.119, bf16[8,256,256]{2,1,0:T(8,128)(2,1)S(1)} %bitcast.120), kind=kOutput, calls=%fused_computation.clone.1 | convolution fusion | flops 2155872256 | bytes 42991616 | tf_op jit(solution)/shard_map/while/body/eval_jaxpr/fra,fca->frc/dot_general | solution.py:64
  277.9 16.4 %copy.27 = f32[8,2048,256]{1,2,0:T(8,128)} copy(f32[8,2048,256]{2,1,0:T(8,128)} %get-tuple-element.102) | data formatting | bytes 33554432 | tf_op jit(solution)/shard_map/while | solution.py:70
  294.3 22.0 %reshape.295 = f32[8,2,1024,4,2,32]{2,1,5,4,3,0:T(2,128)} reshape(f32[8,2048,256]{1,2,0:T(8,128)} %copy.27) | data formatting | bytes 33554432 | tf_op jit(solution)/shard_map/reshape | solution.py:47
  316.3 8.1 %fusion.16 = f32[8,1024,4,1,32]{1,3,4,2,0:T(1,128)S(1)} fusion(f32[8,2,1024,4,2,32]{2,1,5,4,3,0:T(2,128)} %reshape.295), kind=kLoop, calls=%fused_computation.47 | loop fusion | flops 1048576 | bytes 12582912 | tf_op jit(solution)/shard_map/add | solution.py:49
  324.5 8.2 %fusion.18 = f32[8,1024,4,1,32]{1,3,4,2,0:T(1,128)S(1)} fusion(f32[8,2,1024,4,2,32]{2,1,5,4,3,0:T(2,128)} %reshape.295), kind=kLoop, calls=%fused_computation.50 | loop fusion | flops 1048576 | bytes 12582912 | tf_op jit(solution)/shard_map/sub | solution.py:48
  332.7 7.9 %maximum_bitcast_fusion = f32[1024,8,4,2,32]{0,3,4,2,1:T(2,128)S(1)} fusion(f32[8,1024,4,1,32]{1,3,4,2,0:T(1,128)S(1)} %fusion.16, f32[8,1024,4,1,32]{1,3,4,2,0:T(1,128)S(1)} %fusion.18), kind=kLoop, calls=%fused_computation.45 | loop fusion | flops 2097152 | bytes 16777216 | tf_op jit(solution)/shard_map/transpose | solution.py:51
  340.6 6.7 %copy.30 = f32[1024,8,4,2,32]{0,4,3,2,1:T(8,128)} copy(f32[1024,8,4,2,32]{0,3,4,2,1:T(2,128)S(1)} %maximum_bitcast_fusion) | data formatting | bytes 16777216 | tf_op jit(solution)/shard_map/transpose | solution.py:51
  347.3 55.3 %reduce-scatter.2.cloned.1.call-done = f32[128,2048]{0,1:T(8,128)} async-done(((f32[1024,2048]{0,1:T(8,128)}), f32[128,2048]{0,1:T(8,128)}) %reduce-scatter.2.cloned.1.call-update) | async-done | bytes 1048592 | tf_op jit(solution)/shard_map/reduce_scatter | solution.py:93
  402.5 1.7 copy.31
  404.2 22.3 %all_to_all.18 = f32[128,8,256]{2,1,0:T(8,128)S(1)} all-to-all(f32[128,8,256]{2,1,0:T(8,128)S(1)} %copy.31), channel_id=1, replica_groups=mesh['atom'=8,'tm'=16] {'tm'}, dimensions={0} | all-to-all | bytes 2097152 | tf_op jit(solution)/shard_map/all_to_all | solution.py:103
  (129 shorter events, 21.3 us)
Async XLA Ops:
  6.5 396.0 %reduce-scatter.2.cloned.1.call-start = ((), (), s32[]{:S(2)}) async-start(), calls=%async_computation.2 | async-start | bytes 9437184 | tf_op jit(solution)/shard_map/reduce_scatter | solution.py:93
Sparse Core Ops, SparseCore 0:
  347.4 55.1 reduce-scatter.1
where the time goes:
time: 443 us; the launch traced here: 439 us
  other arithmetic  151 us (34%)
  matrix products  125 us (28%)
  local copies, waits for them, and re-layouts  66.1 us (15%)
  waiting for transfers between devices  55.3 us (12%)
  blocking collectives  22.3 us (5%)
  between operations  13.8 us (3%)
  loops' own time  5.89 us (1%)
    dot_general x8, matrix products, accumulate(): jnp.einsum('fra,fca->frc', left_side, right_side, preferred_element_type=...  125 us
    concatenate x8, other arithmetic, operands(): left_side = jnp.concatenate([real_xy, imag_xy], 1)  59.3 us
    reduce_scatter x1, waiting for transfers between devices, per_device(): lax.psum_scatter(mode_rows(positions, velocity, jnp.int32(0) // KY, row_c...  55.3 us
    another operation x16, other arithmetic  38.1 us
    cos x8, other arithmetic, phase_pair(): return (jnp.cos(angles), jnp.sin(angles))  25 us
    all_to_all x1, blocking collectives, per_device(): lax.all_to_all(local_modes, 'tm', split_axis=0, concat_axis=1, tiled=True)  22.3 us
    reshape x1, local copies, waits for them, and re-layouts, finish(): split = raw.reshape(frame_count, 2, row_count, -1, 2, KZ)  22 us
    while x1, local copies, waits for them, and re-layouts, mode_rows(): lax.scan(accumulate, initial, jnp.arange(atom_count // atom_block, dtype=...  16.4 us
  transfers between devices with their start and end apart: 1, of which 1 were waited for; matrix products, arithmetic and copies ran while one was open for 0% of the time, Pallas kernels for 0%

commit v1 on v0

v1 whole, which is shorter than its diff:
```python
import functools
import math

import jax
import jax.numpy as jnp
from jax import lax
from jax.experimental import pallas as pl
from jax.experimental.pallas import tpu as pltpu
from jax.sharding import PartitionSpec as P

KX = 32
KY = 32
KZ = 32
LAGS = 16
LATTICE = 131072
ATOMS = 16384
FRAMES = 128
HALF = 16
ROWS = 80
SINE = (6.28318516, -41.3416550, 81.6010040, -76.5498338, 39.5367090)


def sine(u):
    square = u * u
    value = jnp.full_like(u, SINE[4])
    for factor in SINE[3::-1]:
        value = value * square + factor
    return value * u


def cos_sin(turns):
    r = turns - jnp.round(turns)
    c = sine(0.25 - jnp.abs(r))
    s = sine(jnp.maximum(jnp.minimum(r, 0.5 - r), -0.5 - r))
    return c, s


def harmonics(c, s):
    twice = c + c
    cs, ss = [c], [s]
    before_c, before_s = jnp.ones_like(c), jnp.zeros_like(s)
    for _ in range(HALF - 1):
        next_c, next_s = twice * cs[-1] - before_c, twice * ss[-1] - before_s
        before_c, before_s = cs[-1], ss[-1]
        cs.append(next_c)
        ss.append(next_s)
    return cs, ss


def build(data, first, table, left, right):
    groups = 16

    def put(row, value):
        table[pl.ds(row, groups, stride=ROWS), :] = value

    turns = [
        (data[2 * a].astype(jnp.float32) * 512.0 + data[2 * a + 1].astype(jnp.float32))
        * (1.0 / LATTICE)
        for a in range(3)
    ]
    c, s = cos_sin(turns[0] * first)
    c1, s1 = cos_sin(turns[0])
    for i in range(4):
        put(2 * i, c)
        put(2 * i + 1, s)
        if i < 3:
            c, s = c * c1 - s * s1, c * s1 + s * c1
    for axis in (1, 2):
        cs, ss = harmonics(*cos_sin(turns[axis]))
        base = 8 + 32 * (axis - 1)
        for w in range(HALF):
            put(base + w, cs[w])
            put(base + HALF + w, ss[w])
    for comp in range(3):
        put(72 + comp, data[6 + comp].astype(jnp.float32))
    for g in range(groups):
        base = g * ROWS
        lanes = slice(g * 128, (g + 1) * 128)
        yc = [table[base + 8 + 8 * b : base + 16 + 8 * b, :] for b in range(2)]
        ys = [table[base + 24 + 8 * b : base + 32 + 8 * b, :] for b in range(2)]
        for i in range(4):
            cx = table[pl.ds(base + 2 * i, 1), :]
            sx = table[pl.ds(base + 2 * i + 1, 1), :]
            for b in range(2):
                cc, sn = cx * yc[b], sx * ys[b]
                cn, sc = cx * ys[b], sx * yc[b]
                plus = jnp.concatenate([cc - sn, cn + sc], 0).astype(jnp.bfloat16)
                minus = jnp.concatenate([cc + sn, sc - cn], 0).astype(jnp.bfloat16)
                row = (i * 4 + 2 + b) * 16
                left[row : row + 16, lanes] = plus
                row = (i * 4 + 1 - b) * 16
                left[row : row + 16, lanes] = minus
        for part in range(2):
            z = table[base + 40 + 16 * part : base + 56 + 16 * part, :]
            for comp in range(4):
                value = z if comp == 0 else z * table[pl.ds(base + 71 + comp, 1), :]
                row = part * 64 + comp * 16
                right[row : row + 16, lanes] = value.astype(jnp.bfloat16)


def modes_kernel(number, first_ref, *refs):
    data, out = refs[:number], refs[number]
    table, left_a, right_a, left_b, right_b, total = refs[number + 1 :]
    first = first_ref[0]
    total[...] = jnp.zeros_like(total)
    operands = ((left_a, right_a), (left_b, right_b))

    def multiply(which):
        left, right = operands[which]
        total[...] += lax.dot_general(
            right[...], left[...], (((1,), (1,)), ((), ())), preferred_element_type=jnp.float32
        )

    for g in range(number):
        build([data[g][0, k] for k in range(9)], first, table, *operands[g % 2])
        multiply(g % 2)
    turned = jnp.transpose(total[...])
    out[...] = turned.reshape(16, 1, 16, 128)


def modes(first, blocks):
    frames = blocks[0].shape[0]
    number = len(blocks)
    spec = pl.BlockSpec((1, 9, 16, 128), lambda f: (f, 0, 0, 0))
    return pl.pallas_call(
        functools.partial(modes_kernel, number),
        grid=(frames,),
        out_shape=jax.ShapeDtypeStruct((16, frames, 16, 128), jnp.float32),
        in_specs=[pl.BlockSpec(memory_space=pltpu.SMEM)] + [spec] * number,
        out_specs=pl.BlockSpec((16, 1, 16, 128), lambda f: (0, f, 0, 0)),
        scratch_shapes=[pltpu.VMEM((16 * ROWS, 128), jnp.float32)]
        + [pltpu.VMEM((256, 2048), jnp.bfloat16), pltpu.VMEM((128, 2048), jnp.bfloat16)] * 2
        + [pltpu.VMEM((128, 256), jnp.float32)],
        compiler_params=pltpu.CompilerParams(dimension_semantics=("arbitrary",)),
        name="modes",
    )(first, *blocks)


def correlate_kernel(flip_ref, series, pick, out, d, e, rows):
    frames = FRAMES
    d[frames:, :, :] = jnp.zeros((LAGS, 8, 128), jnp.float32)
    e[frames:, :, :] = jnp.zeros((LAGS, 8, 128), jnp.float32)

    def split(t, carry):
        values = series[t].astype(jnp.float32)
        real, imag = values[:8], pltpu.roll(values[8:], 64, 1)
        d[t] = real - imag
        e[t] = real + imag
        return carry

    lax.fori_loop(0, frames, split, 0, unroll=8)

    def lags(source):
        def step(t, sums):
            here = source[t]
            return tuple(sums[lag] + here * source[t + lag] for lag in range(LAGS))

        zero = jnp.zeros((8, 128), jnp.float32)
        return lax.fori_loop(0, frames, step, (zero,) * LAGS, unroll=4)

    sums_d, sums_e = lags(d), lags(e)
    for lag in range(LAGS):
        value = (sums_d[lag] + pltpu.roll(sums_e[lag], 64, 1)) * (1.0 / (ATOMS * (frames - lag)))
        rows[lag * 8 : lag * 8 + 8, :] = value
    rows[...] = jnp.dot(
        rows[...], pick[...], precision=lax.Precision.HIGHEST, preferred_element_type=jnp.float32
    )
    flip = flip_ref[0] == 1
    lane = lax.broadcasted_iota(jnp.int32, (LAGS, 128), 1) // 32
    for half in range(2):
        totals = [jnp.zeros((LAGS, 128), jnp.float32) for _ in range(4)]
        for part in range(4):
            w = half * 4 + part
            ahead = rows[pl.ds(w, LAGS, stride=8), :]
            back = rows[pl.ds(7 - w, LAGS, stride=8), :]
            value = jnp.where(flip, back, ahead)
            for comp in range(4):
                shift = (32 * (part - comp)) % 128
                moved = pltpu.roll(value, shift, 1) if shift else value
                totals[comp] = jnp.where(lane == part, moved, totals[comp])
        for comp in range(4):
            out[comp, :, half * 128 : half * 128 + 128] = totals[comp]


def correlate(flip, series):
    lane = jnp.arange(128)
    comp, q = lane // 32, lane % 32
    source = jnp.where(q < 16, 64 + comp * 16 + 15 - q, comp * 16 + q - 16)
    pick = (lane[:, None] == source[None, :]).astype(jnp.float32)
    vmem = pl.BlockSpec(memory_space=pltpu.VMEM)
    return pl.pallas_call(
        correlate_kernel,
        out_shape=jax.ShapeDtypeStruct((4, LAGS, 256), jnp.float32),
        in_specs=[pl.BlockSpec(memory_space=pltpu.SMEM), vmem, vmem],
        out_specs=vmem,
        scratch_shapes=[
            pltpu.VMEM((FRAMES + LAGS, 8, 128), jnp.float32),
            pltpu.VMEM((FRAMES + LAGS, 8, 128), jnp.float32),
            pltpu.VMEM((128, 128), jnp.float32),
        ],
        name="correlate",
    )(flip, series, pick)


def gather_atoms(own):
    sibling = [(i, i ^ 1) for i in range(8)]
    blocks = [own, lax.ppermute(own, "atom", sibling)]
    for step in (1, 3, 2):
        there = lax.ppermute(own, "atom", [(i, (i + 2 * step) % 8) for i in range(8)])
        blocks += [there, lax.ppermute(there, "atom", sibling)]
    return blocks


def per_device(positions, velocity):
    a = lax.axis_index("atom")
    t = lax.axis_index("tm")
    frames = positions.shape[0]
    low = ((positions + 256) & 511) - 256
    high = (positions - low) >> 9
    parts = jnp.stack([high, low], 2).reshape(frames, 6, 16, 128).astype(jnp.bfloat16)
    own = jnp.concatenate([parts, velocity.reshape(frames, 3, 16, 128)], 1)
    first = (4 * a - 16 + (a >= 4)).astype(jnp.float32).reshape(1)
    local = modes(first, gather_atoms(own))
    series = lax.all_to_all(local, "tm", split_axis=0, concat_axis=0, tiled=True)
    flip = (t % 4 < 2).astype(jnp.int32).reshape(1)
    return correlate(flip, series.reshape(FRAMES, 16, 128))


def solution(mesh):
    in_specs = (P("tm", None, "atom"), P("tm", None, "atom"))
    out_specs = P(None, None, ("atom", "tm"))
    return jax.shard_map(
        per_device, mesh=mesh, in_specs=in_specs, out_specs=out_specs, check_vma=False
    )
```

time: 443 us -> 116 us (0.26)
  other arithmetic: 151 us -> 1.64 us
  matrix products: 125 us -> 0 us
  Pallas kernels: 0 us -> 66.6 us
  local copies, waits for them, and re-layouts: 66.1 us -> 2.91 us
  waiting for transfers between devices: 55.3 us -> 24.3 us
  blocking collectives: 22.3 us -> 0 us
  starting transfers between devices: 0.01 us -> 19.1 us
  between operations: 13.8 us -> 0.15 us
  loops' own time: 5.89 us -> 0 us
    dot_general x8 -> x0, matrix products: 125 us -> none  [accumulate(): jnp.einsum('fra,fca->frc', left_side, right_side, preferred_element_type=...]
    pallas_call x0 -> x2, Pallas kernels: none -> 66.6 us  [the longest x1 61.7 us: modes(): pl.pallas_call(functools.partial(modes_kernel, number), grid=(frames,), o...]
    concatenate x16 -> x0, other arithmetic: 59.4 us -> none  [the longest x8 59.3 us: operands(): left_side = jnp.concatenate([real_xy, imag_xy], 1)]
    reduce_scatter x1 -> x0, waiting for transfers between devices: 55.3 us -> none  [per_device(): lax.psum_scatter(mode_rows(positions, velocity, jnp.int32(0) // KY, row_c...]
    another operation x25 -> x2, other arithmetic: 38.9 us -> 1 us  [per_device(): jnp.stack([high, low], 2).reshape(frames, 6, 16, 128).astype(jnp.bfloat16)]
    cos x8 -> x0, other arithmetic: 25 us -> none  [phase_pair(): return (jnp.cos(angles), jnp.sin(angles))]
    reshape x4 -> x0, local copies, waits for them, and re-layouts: 24.5 us -> none  [the longest x1 22 us: finish(): split = raw.reshape(frame_count, 2, row_count, -1, 2, KZ)]
    all_to_all x1 -> x0, blocking collectives: 22.3 us -> none  [per_device(): lax.all_to_all(local_modes, 'tm', split_axis=0, concat_axis=1, tiled=True)]
  transfers between devices with their start and end apart: 1 -> 8, of which waited for: 1 -> 4; matrix products, arithmetic and copies ran while one was open for 0% -> 1% of each run, Pallas kernels for 0% -> 0%
where the time goes in v1:
time: 116 us; the launch traced here: 115 us
  Pallas kernels  66.6 us (57%)
  waiting for transfers between devices  24.3 us (21%)
  starting transfers between devices  19.1 us (16%)
  local copies, waits for them, and re-layouts  2.91 us (3%)
  other arithmetic  1.64 us (1%)
    pallas_call x1, Pallas kernels, modes(): pl.pallas_call(functools.partial(modes_kernel, number), grid=(frames,), o...  61.7 us
    all_to_all x1, waiting for transfers between devices, per_device(): lax.all_to_all(local, 'tm', split_axis=0, concat_axis=0, tiled=True)  15.7 us
    all_to_all x1, starting transfers between devices, per_device(): lax.all_to_all(local, 'tm', split_axis=0, concat_axis=0, tiled=True)  7.77 us
    ppermute x3, waiting for transfers between devices, gather_atoms(): lax.ppermute(own, 'atom', [(i, (i + 2 * step) % 8) for i in range(8)])  7.46 us
    ppermute x3, starting transfers between devices, gather_atoms(): lax.ppermute(own, 'atom', [(i, (i + 2 * step) % 8) for i in range(8)])  5.1 us
    pallas_call x1, Pallas kernels, correlate(): pl.pallas_call(correlate_kernel, out_shape=jax.ShapeDtypeStruct((4, LAGS,...  4.94 us
    ppermute x3, starting transfers between devices, gather_atoms(): blocks += [there, lax.ppermute(there, 'atom', sibling)]  4.74 us
    unnamed x21, local copies, waits for them, and re-layouts  2.55 us
  transfers between devices with their start and end apart: 8, of which 4 were waited for; matrix products, arithmetic and copies ran while one was open for 1% of the time, Pallas kernels for 0%

profile of v1, /device:TPU:1, one launch (start us, length us, event | category | flops | bytes accessed | tf_op | source)
XLA Modules:
  0.0 114.8 jit_solution(6569070003212385443)
XLA Ops:
  0.0 1.0 fusion.2
  1.0 0.2 copy.5
  1.2 0.1 convert_element_type.16
  1.4 0.0 copy-start.9
  1.4 0.9 copy-done.9
  2.3 0.0 copy-start.1
  2.3 2.1 %collective-permute-start.1 = (bf16[8,9,16,128]{3,2,1,0:T(8,128)(2,1)S(1)}, bf16[8,9,16,128]{3,2,1,0:T(8,128)(2,1)S(1)}, u32[]{:S(2)}, u32[]{:S(2)}) collective-permute-start(bf16[8,9,16,128]{3,2,1,0:T(8,128)(2,1)S(1)} %copy_dynamic-update-slice_fusion.refs_0_), channel_id=1, source_target_pairs={{0,32},{16,48},{32,64},{48,80},{64,96},{80,112},{96,0},{112,16},{1... | collective-permute-start | bytes 884744 | tf_op jit(solution)/shard_map/ppermute | solution.py:209
  4.4 1.3 %collective-permute-start.3 = (bf16[8,9,16,128]{3,2,1,0:T(8,128)(2,1)S(1)}, bf16[8,9,16,128]{3,2,1,0:T(8,128)(2,1)S(1)}, u32[]{:S(2)}, u32[]{:S(2)}) collective-permute-start(bf16[8,9,16,128]{3,2,1,0:T(8,128)(2,1)S(1)} %copy_dynamic-update-slice_fusion.refs_0_), channel_id=1, source_target_pairs={{0,96},{16,112},{32,0},{48,16},{64,32},{80,48},{96,64},{112,80},{1... | collective-permute-start | bytes 884744 | tf_op jit(solution)/shard_map/ppermute | solution.py:209
  5.7 1.6 %collective-permute-start.5 = (bf16[8,9,16,128]{3,2,1,0:T(8,128)(2,1)S(1)}, bf16[8,9,16,128]{3,2,1,0:T(8,128)(2,1)S(1)}, u32[]{:S(2)}, u32[]{:S(2)}) collective-permute-start(bf16[8,9,16,128]{3,2,1,0:T(8,128)(2,1)S(1)} %copy_dynamic-update-slice_fusion.refs_0_), channel_id=1, source_target_pairs={{0,64},{16,80},{32,96},{48,112},{64,0},{80,16},{96,32},{112,48},{1... | collective-permute-start | bytes 884744 | tf_op jit(solution)/shard_map/ppermute | solution.py:209
  7.4 1.5 %collective-permute-start = (bf16[8,9,16,128]{3,2,1,0:T(8,128)(2,1)S(1)}, bf16[8,9,16,128]{3,2,1,0:T(8,128)(2,1)S(1)}, u32[]{:S(2)}, u32[]{:S(2)}) collective-permute-start(bf16[8,9,16,128]{3,2,1,0:T(8,128)(2,1)S(1)} %copy_dynamic-update-slice_fusion.refs_0_), channel_id=1, source_target_pairs={{0,16},{16,0},{32,48},{48,32},{64,80},{80,64},{96,112},{112,96},{1... | collective-permute-start | bytes 884744 | tf_op jit(solution)/shard_map/ppermute | solution.py:207
  8.9 3.1 %collective-permute-done.1.refs_2_ = bf16[8,9,16,128]{3,2,1,0:T(8,128)(2,1)S(1)} collective-permute-done((bf16[8,9,16,128]{3,2,1,0:T(8,128)(2,1)S(1)}, bf16[8,9,16,128]{3,2,1,0:T(8,128)(2,1)S(1)}, u32[]{:S(2)}, u32[]{:S(2)}) %collective-permute-start.1) | collective-permute-done | bytes 294944 | tf_op jit(solution)/shard_map/ppermute | solution.py:209
  12.0 0.0 copy-start.2
  12.0 1.6 %collective-permute-start.2 = (bf16[8,9,16,128]{3,2,1,0:T(8,128)(2,1)S(1)}, bf16[8,9,16,128]{3,2,1,0:T(8,128)(2,1)S(1)}, u32[]{:S(2)}, u32[]{:S(2)}) collective-permute-start(bf16[8,9,16,128]{3,2,1,0:T(8,128)(2,1)S(1)} %collective-permute-done.1.refs_2_), channel_id=1, source_target_pairs={{0,16},{16,0},{32,48},{48,32},{64,80},{80,64},{96,112},{112,96},{1... | collective-permute-start | bytes 884744 | tf_op jit(solution)/shard_map/ppermute | solution.py:210
  13.6 0.0 collective-permute-done.3.refs_4_
  13.6 0.0 copy-start.3
  13.6 1.6 %collective-permute-start.4 = (bf16[8,9,16,128]{3,2,1,0:T(8,128)(2,1)S(1)}, bf16[8,9,16,128]{3,2,1,0:T(8,128)(2,1)S(1)}, u32[]{:S(2)}, u32[]{:S(2)}) collective-permute-start(bf16[8,9,16,128]{3,2,1,0:T(8,128)(2,1)S(1)} %collective-permute-done.3.refs_4_), channel_id=1, source_target_pairs={{0,16},{16,0},{32,48},{48,32},{64,80},{80,64},{96,112},{112,96},{1... | collective-permute-start | bytes 884744 | tf_op jit(solution)/shard_map/ppermute | solution.py:210
  15.2 4.4 %collective-permute-done.5.refs_6_ = bf16[8,9,16,128]{3,2,1,0:T(8,128)(2,1)S(1)} collective-permute-done((bf16[8,9,16,128]{3,2,1,0:T(8,128)(2,1)S(1)}, bf16[8,9,16,128]{3,2,1,0:T(8,128)(2,1)S(1)}, u32[]{:S(2)}, u32[]{:S(2)}) %collective-permute-start.5) | collective-permute-done | bytes 294944 | tf_op jit(solution)/shard_map/ppermute | solution.py:209
  19.6 0.0 copy-start.4
  19.6 1.5 %collective-permute-start.6 = (bf16[8,9,16,128]{3,2,1,0:T(8,128)(2,1)S(1)}, bf16[8,9,16,128]{3,2,1,0:T(8,128)(2,1)S(1)}, u32[]{:S(2)}, u32[]{:S(2)}) collective-permute-start(bf16[8,9,16,128]{3,2,1,0:T(8,128)(2,1)S(1)} %collective-permute-done.5.refs_6_), channel_id=1, source_target_pairs={{0,16},{16,0},{32,48},{48,32},{64,80},{80,64},{96,112},{112,96},{1... | collective-permute-start | bytes 884744 | tf_op jit(solution)/shard_map/ppermute | solution.py:210
  21.1 0.0 collective-permute-done.refs_1_
  21.1 0.0 copy-start.5
  21.1 0.0 collective-permute-done.2.refs_3_
  21.1 0.0 copy-start.6
  21.1 0.0 collective-permute-done.4.refs_5_
  21.2 0.0 copy-start.7
  21.2 1.2 %collective-permute-done.6.refs_7_ = bf16[8,9,16,128]{3,2,1,0:T(8,128)(2,1)S(1)} collective-permute-done((bf16[8,9,16,128]{3,2,1,0:T(8,128)(2,1)S(1)}, bf16[8,9,16,128]{3,2,1,0:T(8,128)(2,1)S(1)}, u32[]{:S(2)}, u32[]{:S(2)}) %collective-permute-start.6) | collective-permute-done | bytes 294944 | tf_op jit(solution)/shard_map/ppermute | solution.py:210
  22.3 0.0 copy-start.8
  22.3 0.0 copy-done.1
  22.3 0.0 copy-done.2
  22.3 0.0 copy-done.3
  22.3 0.0 copy-done.4
  22.4 0.0 copy-done.5
  22.4 0.0 copy-done.6
  22.4 0.0 copy-done.7
  22.4 0.7 copy-done.8
  23.1 61.7 %modes.1 = f32[16,8,16,128]{3,2,1,0:T(8,128)} custom-call(f32[1]{0:T(128)} %bitcast.1.first_ref, bf16[8,9,16,128]{3,2,1,0:T(8,128)(2,1)} %copy-done.1, bf16[8,9,16,128]{3,2,1,0:T(8,128)(2,1)} %copy-done.5, bf16[8,9,16,128]{3,2,1,0:T(8,128)(2,1)} %copy-done.2, bf16[8,9,16,128]{3,2,1,0:T(8,128)(2,1)} %copy-done.6, bf16[8,9,16,128]{3,2,1,0:T(8,128)(2,1)} %copy-done.3, ...), custom_call_target="tpu_custom_call" | custom-call | tf_op jit(solution)/shard_map/modes/pallas_call | solution.py:125
  84.7 7.8 %all-to-all-start = ((f32[16,8,16,128]{3,2,1,0:T(8,128)}), f32[16,8,16,128]{3,2,1,0:T(8,128)S(1)}, u32[]{:S(2)}, u32[]{:S(2)}) async-start(f32[16,8,16,128]{3,2,1,0:T(8,128)} %modes.1), calls=%async_computation | async-start | bytes 2097152 | tf_op jit(solution)/shard_map/all_to_all | solution.py:224
  92.5 0.6 fusion.3.pick
  93.2 15.7 %all-to-all-done = f32[16,8,16,128]{3,2,1,0:T(8,128)S(1)} async-done(((f32[16,8,16,128]{3,2,1,0:T(8,128)}), f32[16,8,16,128]{3,2,1,0:T(8,128)S(1)}, u32[]{:S(2)}, u32[]{:S(2)}) %all-to-all-start) | async-done | bytes 1048608 | tf_op jit(solution)/shard_map/all_to_all | solution.py:224
  108.9 0.0 copy-start
  108.9 1.0 copy-done
  109.8 4.9 %correlate.1 = f32[4,16,256]{2,1,0:T(8,128)} custom-call(s32[1]{0:T(128)} %bitcast.flip_ref, f32[128,16,128]{2,1,0:T(8,128)} %bitcast.15, f32[128,128]{1,0:T(8,128)} %fusion.3.pick), custom_call_target="tpu_custom_call" | custom-call | tf_op jit(solution)/shard_map/correlate/pallas_call | solution.py:191
  (4 shorter events, 0.1 us)
Async XLA Ops:
  1.4 0.9 copy-start.9
  2.3 20.1 %copy-start.1 = (bf16[8,9,16,128]{3,2,1,0:T(8,128)(2,1)}, bf16[8,9,16,128]{3,2,1,0:T(8,128)(2,1)S(1)}, u32[]{:S(2)}) copy-start(bf16[8,9,16,128]{3,2,1,0:T(8,128)(2,1)S(1)} %copy_dynamic-update-slice_fusion.refs_0_) | copy-start | bytes 884740
  2.3 9.7 %collective-permute-start.1 = (bf16[8,9,16,128]{3,2,1,0:T(8,128)(2,1)S(1)}, bf16[8,9,16,128]{3,2,1,0:T(8,128)(2,1)S(1)}, u32[]{:S(2)}, u32[]{:S(2)}) collective-permute-start(bf16[8,9,16,128]{3,2,1,0:T(8,128)(2,1)S(1)} %copy_dynamic-update-slice_fusion.refs_0_), channel_id=1, source_target_pairs={{0,32},{16,48},{32,64},{48,80},{64,96},{80,112},{96,0},{112,16},{1... | collective-permute-start | bytes 884744 | tf_op jit(solution)/shard_map/ppermute | solution.py:209
  4.4 9.2 %collective-permute-start.3 = (bf16[8,9,16,128]{3,2,1,0:T(8,128)(2,1)S(1)}, bf16[8,9,16,128]{3,2,1,0:T(8,128)(2,1)S(1)}, u32[]{:S(2)}, u32[]{:S(2)}) collective-permute-start(bf16[8,9,16,128]{3,2,1,0:T(8,128)(2,1)S(1)} %copy_dynamic-update-slice_fusion.refs_0_), channel_id=1, source_target_pairs={{0,96},{16,112},{32,0},{48,16},{64,32},{80,48},{96,64},{112,80},{1... | collective-permute-start | bytes 884744 | tf_op jit(solution)/shard_map/ppermute | solution.py:209
  5.7 13.8 %collective-permute-start.5 = (bf16[8,9,16,128]{3,2,1,0:T(8,128)(2,1)S(1)}, bf16[8,9,16,128]{3,2,1,0:T(8,128)(2,1)S(1)}, u32[]{:S(2)}, u32[]{:S(2)}) collective-permute-start(bf16[8,9,16,128]{3,2,1,0:T(8,128)(2,1)S(1)} %copy_dynamic-update-slice_fusion.refs_0_), channel_id=1, source_target_pairs={{0,64},{16,80},{32,96},{48,112},{64,0},{80,16},{96,32},{112,48},{1... | collective-permute-start | bytes 884744 | tf_op jit(solution)/shard_map/ppermute | solution.py:209
  7.4 13.7 %collective-permute-start = (bf16[8,9,16,128]{3,2,1,0:T(8,128)(2,1)S(1)}, bf16[8,9,16,128]{3,2,1,0:T(8,128)(2,1)S(1)}, u32[]{:S(2)}, u32[]{:S(2)}) collective-permute-start(bf16[8,9,16,128]{3,2,1,0:T(8,128)(2,1)S(1)} %copy_dynamic-update-slice_fusion.refs_0_), channel_id=1, source_target_pairs={{0,16},{16,0},{32,48},{48,32},{64,80},{80,64},{96,112},{112,96},{1... | collective-permute-start | bytes 884744 | tf_op jit(solution)/shard_map/ppermute | solution.py:207
  12.0 10.3 %copy-start.2 = (bf16[8,9,16,128]{3,2,1,0:T(8,128)(2,1)}, bf16[8,9,16,128]{3,2,1,0:T(8,128)(2,1)S(1)}, u32[]{:S(2)}) copy-start(bf16[8,9,16,128]{3,2,1,0:T(8,128)(2,1)S(1)} %collective-permute-done.1.refs_2_) | copy-start | bytes 884740
  12.0 9.1 %collective-permute-start.2 = (bf16[8,9,16,128]{3,2,1,0:T(8,128)(2,1)S(1)}, bf16[8,9,16,128]{3,2,1,0:T(8,128)(2,1)S(1)}, u32[]{:S(2)}, u32[]{:S(2)}) collective-permute-start(bf16[8,9,16,128]{3,2,1,0:T(8,128)(2,1)S(1)} %collective-permute-done.1.refs_2_), channel_id=1, source_target_pairs={{0,16},{16,0},{32,48},{48,32},{64,80},{80,64},{96,112},{112,96},{1... | collective-permute-start | bytes 884744 | tf_op jit(solution)/shard_map/ppermute | solution.py:210
  13.6 8.7 %copy-start.3 = (bf16[8,9,16,128]{3,2,1,0:T(8,128)(2,1)}, bf16[8,9,16,128]{3,2,1,0:T(8,128)(2,1)S(1)}, u32[]{:S(2)}) copy-start(bf16[8,9,16,128]{3,2,1,0:T(8,128)(2,1)S(1)} %collective-permute-done.3.refs_4_) | copy-start | bytes 884740
  13.6 7.5 %collective-permute-start.4 = (bf16[8,9,16,128]{3,2,1,0:T(8,128)(2,1)S(1)}, bf16[8,9,16,128]{3,2,1,0:T(8,128)(2,1)S(1)}, u32[]{:S(2)}, u32[]{:S(2)}) collective-permute-start(bf16[8,9,16,128]{3,2,1,0:T(8,128)(2,1)S(1)} %collective-permute-done.3.refs_4_), channel_id=1, source_target_pairs={{0,16},{16,0},{32,48},{48,32},{64,80},{80,64},{96,112},{112,96},{1... | collective-permute-start | bytes 884744 | tf_op jit(solution)/shard_map/ppermute | solution.py:210
  19.6 2.8 %copy-start.4 = (bf16[8,9,16,128]{3,2,1,0:T(8,128)(2,1)}, bf16[8,9,16,128]{3,2,1,0:T(8,128)(2,1)S(1)}, u32[]{:S(2)}) copy-start(bf16[8,9,16,128]{3,2,1,0:T(8,128)(2,1)S(1)} %collective-permute-done.5.refs_6_) | copy-start | bytes 884740
  19.6 2.7 %collective-permute-start.6 = (bf16[8,9,16,128]{3,2,1,0:T(8,128)(2,1)S(1)}, bf16[8,9,16,128]{3,2,1,0:T(8,128)(2,1)S(1)}, u32[]{:S(2)}, u32[]{:S(2)}) collective-permute-start(bf16[8,9,16,128]{3,2,1,0:T(8,128)(2,1)S(1)} %collective-permute-done.5.refs_6_), channel_id=1, source_target_pairs={{0,16},{16,0},{32,48},{48,32},{64,80},{80,64},{96,112},{112,96},{1... | collective-permute-start | bytes 884744 | tf_op jit(solution)/shard_map/ppermute | solution.py:210
  21.1 1.2 %copy-start.5 = (bf16[8,9,16,128]{3,2,1,0:T(8,128)(2,1)}, bf16[8,9,16,128]{3,2,1,0:T(8,128)(2,1)S(1)}, u32[]{:S(2)}) copy-start(bf16[8,9,16,128]{3,2,1,0:T(8,128)(2,1)S(1)} %collective-permute-done.refs_1_) | copy-start | bytes 884740
  21.1 1.2 %copy-start.6 = (bf16[8,9,16,128]{3,2,1,0:T(8,128)(2,1)}, bf16[8,9,16,128]{3,2,1,0:T(8,128)(2,1)S(1)}, u32[]{:S(2)}) copy-start(bf16[8,9,16,128]{3,2,1,0:T(8,128)(2,1)S(1)} %collective-permute-done.2.refs_3_) | copy-start | bytes 884740
  21.2 1.2 %copy-start.7 = (bf16[8,9,16,128]{3,2,1,0:T(8,128)(2,1)}, bf16[8,9,16,128]{3,2,1,0:T(8,128)(2,1)S(1)}, u32[]{:S(2)}) copy-start(bf16[8,9,16,128]{3,2,1,0:T(8,128)(2,1)S(1)} %collective-permute-done.4.refs_5_) | copy-start | bytes 884740
  22.3 0.7 copy-start.8
  84.7 24.1 %all-to-all-start = ((f32[16,8,16,128]{3,2,1,0:T(8,128)}), f32[16,8,16,128]{3,2,1,0:T(8,128)S(1)}, u32[]{:S(2)}, u32[]{:S(2)}) async-start(f32[16,8,16,128]{3,2,1,0:T(8,128)} %modes.1), calls=%async_computation | async-start | bytes 2097152 | tf_op jit(solution)/shard_map/all_to_all | solution.py:224
  108.9 1.0 copy-start

commit v2 on v1

v2 whole, which is shorter than its diff:
```python
import functools
import math

import jax
import jax.numpy as jnp
from jax import lax
from jax.experimental import pallas as pl
from jax.experimental.pallas import tpu as pltpu
from jax.sharding import PartitionSpec as P

KX = 32
KY = 32
KZ = 32
LAGS = 16
LATTICE = 131072
ATOMS = 16384
FRAMES = 128
HALF = 16
REAL = False
ROWS = 81
SINE = (6.28318516, -41.3416550, 81.6010040, -76.5498338, 39.5367090)


def sine(u):
    square = u * u
    value = jnp.full_like(u, SINE[4])
    for factor in SINE[3::-1]:
        value = value * square + factor
    return value * u


def cos_sin(turns):
    r = turns - jnp.round(turns)
    c = sine(0.25 - jnp.abs(r))
    s = sine(jnp.maximum(jnp.minimum(r, 0.5 - r), -0.5 - r))
    return c, s


def harmonics(c, s):
    twice = c + c
    cs, ss = [c], [s]
    before_c, before_s = jnp.ones_like(c), jnp.zeros_like(s)
    for _ in range(HALF - 1):
        next_c, next_s = twice * cs[-1] - before_c, twice * ss[-1] - before_s
        before_c, before_s = cs[-1], ss[-1]
        cs.append(next_c)
        ss.append(next_s)
    return cs, ss


def fill(data, first, table):
    def put(row, value):
        table[pl.ds(row, 16, stride=ROWS), :] = value

    turns = [
        (data[2 * a].astype(jnp.float32) * 512.0 + data[2 * a + 1].astype(jnp.float32))
        * (1.0 / LATTICE)
        for a in range(3)
    ]
    c, s = cos_sin(turns[0] * first)
    c1, s1 = cos_sin(turns[0])
    for i in range(4):
        put(2 * i, c)
        put(2 * i + 1, s)
        if i < 3:
            c, s = c * c1 - s * s1, c * s1 + s * c1
    for axis in (1, 2):
        cs, ss = harmonics(*cos_sin(turns[axis]))
        base = 8 + 32 * (axis - 1)
        for w in range(HALF):
            put(base + w, cs[w])
            put(base + HALF + w, ss[w])
    for comp in range(3):
        put(72 + comp, data[6 + comp].astype(jnp.float32))


def multiply(table, total):
    for pair in range(8):
        bases = [(2 * pair + k) * ROWS for k in range(2)]

        def rows(start, number):
            return [table[pl.ds(base + start, number), :] for base in bases]

        def wide(parts):
            return jnp.concatenate([p.astype(jnp.bfloat16) for p in parts], 1)

        yc = [rows(8 + 8 * b, 8) for b in range(2)]
        ys = [rows(24 + 8 * b, 8) for b in range(2)]
        left = []
        for i in range(4):
            cx, sx = rows(2 * i, 1), rows(2 * i + 1, 1)
            for b in range(2):
                one, two = [], []
                for k in range(2):
                    cc, sn = cx[k] * yc[b][k], sx[k] * ys[b][k]
                    cn, sc = cx[k] * ys[b][k], sx[k] * yc[b][k]
                    if REAL:
                        one.append(jnp.concatenate([cc, sn], 0))
                        two.append(jnp.concatenate([cn, sc], 0))
                    else:
                        one.append(jnp.concatenate([cc - sn, cn + sc], 0))
                        two.append(jnp.concatenate([cc + sn, sc - cn], 0))
                left += [wide(one), wide(two)]
        right = []
        for part in range(2):
            z = rows(40 + 16 * part, 16)
            right.append(wide(z))
            for comp in range(3):
                u = rows(72 + comp, 1)
                right.append(wide([z[k] * u[k] for k in range(2)]))
        left, right = jnp.concatenate(left, 0), jnp.concatenate(right, 0)
        total = total + lax.dot_general(
            right, left, (((1,), (1,)), ((), ())), preferred_element_type=jnp.float32
        )
    return total


def modes_kernel(number, frames, more, last, first_ref, *refs):
    if more:
        before, refs = refs[0], refs[1:]
    data, out = refs[:number], refs[number]
    table_a, table_b, blocks, *rest = refs[number + 1 :]
    totals = rest[0] if last else out
    first = first_ref[0]
    steps = number * frames
    for g in range(number):
        for f in range(frames):
            blocks[f * number + g] = data[g][f]

    def block(index):
        return [blocks[index, k] for k in range(9)]

    totals[...] = before[...] if more else jnp.zeros_like(totals)
    fill(block(0), first, table_a)

    def step(half, carry):
        now = 2 * half
        frame = now // number
        fill(block(now + 1), first, table_b)
        total = multiply(table_a, totals[frame])
        fill(block(jnp.minimum(now + 2, steps - 1)), first, table_a)
        totals[frame] = multiply(table_b, total)
        return carry

    lax.fori_loop(0, steps // 2, step, 0)
    if not last:
        return
    for f in range(frames):
        total = jnp.transpose(totals[f])
        for i in range(4):
            for b in range(2):
                part = total[64 * i + 32 * b : 64 * i + 32 * b + 32]
                if REAL:
                    cc, sn, cn, sc = part[:8], part[8:16], part[16:24], part[24:]
                    part = jnp.concatenate([cc - sn, cn + sc, cc + sn, sc - cn], 0)
                out[i * 4 + 2 + b, f] = part[:16]
                out[i * 4 + 1 - b, f] = part[16:]


def modes(first, blocks, before=None, part=0, parts=1, last=False):
    frames = blocks[0].shape[0] // parts
    number, more = len(blocks), before is not None
    smem = pl.BlockSpec(memory_space=pltpu.SMEM)
    data = pl.BlockSpec((frames, 9, 16, 128), lambda _: (part, 0, 0, 0))
    sums = pl.BlockSpec((frames, 128, 256), lambda _: (part, 0, 0))
    owned = (16, frames, 16, 128)
    scratch = [
        pltpu.VMEM((16 * ROWS, 128), jnp.float32),
        pltpu.VMEM((16 * ROWS, 128), jnp.float32),
        pltpu.VMEM((number * frames, 9, 16, 128), jnp.bfloat16),
    ]
    work = number * frames * 2048
    return pl.pallas_call(
        functools.partial(modes_kernel, number, frames, more, last),
        grid=(1,),
        out_shape=jax.ShapeDtypeStruct(owned if last else (frames, 128, 256), jnp.float32),
        in_specs=[smem] + [sums] * more + [data] * number,
        out_specs=pl.BlockSpec(owned, lambda _: (0, 0, 0, 0)) if last else sums,
        scratch_shapes=scratch + [pltpu.VMEM((frames, 128, 256), jnp.float32)] * last,
        cost_estimate=pl.CostEstimate(
            flops=work * 256 * 128 * 2, bytes_accessed=work * 18, transcendentals=0
        ),
        name=f"last{part}" if last else f"nearby{int(more)}",
    )(first, *([before] * more), *blocks)


def correlate_kernel(flip_ref, early, late, pick, out, d, e, rows):
    frames = FRAMES
    d[frames:, :, :] = jnp.zeros((LAGS, 8, 128), jnp.float32)
    e[frames:, :, :] = jnp.zeros((LAGS, 8, 128), jnp.float32)

    def split(source, carry):
        for part, series in enumerate((early, late)):
            for f in range(series.shape[1]):
                values = series[source, f].astype(jnp.float32)
                real, imag = values[:8], pltpu.roll(values[8:], 64, 1)
                t = source * 8 + part * early.shape[1] + f
                d[t] = real - imag
                e[t] = real + imag
        return carry

    lax.fori_loop(0, 16, split, 0)

    def lags(source):
        def step(t, sums):
            here = source[t]
            return tuple(sums[lag] + here * source[t + lag] for lag in range(LAGS))

        zero = jnp.zeros((8, 128), jnp.float32)
        return lax.fori_loop(0, frames, step, (zero,) * LAGS, unroll=4)

    sums_d, sums_e = lags(d), lags(e)
    for lag in range(LAGS):
        value = (sums_d[lag] + pltpu.roll(sums_e[lag], 64, 1)) * (1.0 / (ATOMS * (frames - lag)))
        rows[lag * 8 : lag * 8 + 8, :] = value
    rows[...] = jnp.dot(
        rows[...], pick[...], precision=lax.Precision.HIGHEST, preferred_element_type=jnp.float32
    )
    flip = flip_ref[0] == 1
    lane = lax.broadcasted_iota(jnp.int32, (LAGS, 128), 1) // 32
    for half in range(2):
        totals = [jnp.zeros((LAGS, 128), jnp.float32) for _ in range(4)]
        for part in range(4):
            w = half * 4 + part
            ahead = rows[pl.ds(w, LAGS, stride=8), :]
            back = rows[pl.ds(7 - w, LAGS, stride=8), :]
            value = jnp.where(flip, back, ahead)
            for comp in range(4):
                shift = (32 * (part - comp)) % 128
                moved = pltpu.roll(value, shift, 1) if shift else value
                totals[comp] = jnp.where(lane == part, moved, totals[comp])
        for comp in range(4):
            out[comp, :, half * 128 : half * 128 + 128] = totals[comp]


def correlate(flip, early, late):
    lane = jnp.arange(128)
    comp, q = lane // 32, lane % 32
    source = jnp.where(q < 16, 64 + comp * 16 + 15 - q, comp * 16 + q - 16)
    pick = (lane[:, None] == source[None, :]).astype(jnp.float32)
    vmem = pl.BlockSpec(memory_space=pltpu.VMEM)
    return pl.pallas_call(
        correlate_kernel,
        out_shape=jax.ShapeDtypeStruct((4, LAGS, 256), jnp.float32),
        in_specs=[pl.BlockSpec(memory_space=pltpu.SMEM), vmem, vmem, vmem],
        out_specs=vmem,
        scratch_shapes=[
            pltpu.VMEM((FRAMES + LAGS, 8, 128), jnp.float32),
            pltpu.VMEM((FRAMES + LAGS, 8, 128), jnp.float32),
            pltpu.VMEM((128, 128), jnp.float32),
        ],
        name="correlate",
    )(flip, early, late, pick)


def shift(block, by):
    return lax.ppermute(block, "atom", [(i, (i + by) % 8) for i in range(8)])


def swap(block):
    return lax.ppermute(block, "atom", [(i, i ^ 1) for i in range(8)])


def per_device(positions, velocity):
    a = lax.axis_index("atom")
    t = lax.axis_index("tm")
    frames = positions.shape[0]
    low = ((positions + 256) & 511) - 256
    high = (positions - low) >> 9
    parts = jnp.stack([high, low], 2).reshape(frames, 6, 16, 128).astype(jnp.bfloat16)
    own = jnp.concatenate([parts, velocity.reshape(frames, 3, 16, 128)], 1)
    first = (4 * a - 16 + (a >= 4)).astype(jnp.float32).reshape(1)
    left, right, across = shift(own, 2), shift(own, 6), shift(own, 4)
    sums = modes(first, [own, swap(own)])
    left, right, sums = lax.optimization_barrier((left, right, sums))
    far = [swap(left), swap(right)]
    sums = modes(first, [left, right], sums)
    across, sums, *far = lax.optimization_barrier((across, sums, *far))
    far += [across, swap(across)]
    series = []
    for part in range(2):
        local = modes(first, far, sums, part, 2, True)
        series.append(lax.all_to_all(local, "tm", split_axis=0, concat_axis=0, tiled=True))
    flip = (t % 4 < 2).astype(jnp.int32).reshape(1)
    return correlate(flip, *series)


def solution(mesh):
    in_specs = (P("tm", None, "atom"), P("tm", None, "atom"))
    out_specs = P(None, None, ("atom", "tm"))
    return jax.shard_map(
        per_device, mesh=mesh, in_specs=in_specs, out_specs=out_specs, check_vma=False
    )
```

time: 116 us -> 85.1 us (0.73)
  the two profiles are of different devices: /device:TPU:1 before, /device:TPU:6 now
where the time goes in v2:
time: 85.1 us; the launch traced here: 84.6 us
  Pallas kernels  43.1 us (51%)
  waiting for transfers between devices  17.9 us (21%)
  starting transfers between devices  17.3 us (20%)
  local copies, waits for them, and re-layouts  4.48 us (5%)
  other arithmetic  1.65 us (2%)
    pallas_call x4, Pallas kernels, modes(): pl.pallas_call(functools.partial(modes_kernel, number, frames, more, last...  38.2 us
    all_to_all x2, starting transfers between devices, per_device(): lax.all_to_all(local, 'tm', split_axis=0, concat_axis=0, tiled=True)  13.1 us
    all_to_all x2, waiting for transfers between devices, per_device(): lax.all_to_all(local, 'tm', split_axis=0, concat_axis=0, tiled=True)  12.9 us
    pallas_call x1, Pallas kernels, correlate(): pl.pallas_call(correlate_kernel, out_shape=jax.ShapeDtypeStruct((4, LAGS,...  4.91 us
    unnamed x23, local copies, waits for them, and re-layouts  4.12 us
    ppermute x3, starting transfers between devices, shift(): return lax.ppermute(block, 'atom', [(i, (i + by) % 8) for i in range(8)])  3.5 us
    ppermute x3, waiting for transfers between devices, shift(): return lax.ppermute(block, 'atom', [(i, (i + by) % 8) for i in range(8)])  3.47 us
  transfers between devices with their start and end apart: 9, of which 4 were waited for; matrix products, arithmetic and copies ran while one was open for 1% of the time, Pallas kernels for 34%

profile of v2, /device:TPU:6, one launch (start us, length us, event | category | flops | bytes accessed | tf_op | source)
XLA Modules:
  0.0 84.6 jit_solution(6324238740292162639)
XLA Ops:
  0.0 1.0 %fusion.2 = (bf16[8,3,1,2048]{3,0,1,2:T(8,128)(2,1)S(1)}, bf16[8,3,1,2048]{3,0,1,2:T(8,128)(2,1)S(1)}) fusion(s32[8,3,2048]{2,0,1:T(8,128)} %param.2), kind=kLoop, calls=%fused_computation.5 | loop fusion | flops 344064 | bytes 393216 | tf_op jit(solution)/shard_map/stack | solution.py:270
  1.0 0.2 copy.5
  1.2 0.1 convert_element_type.16
  1.4 0.0 copy-start.3
  1.4 0.9 %copy-done.3 = bf16[8,3,2048]{2,0,1:T(8,128)(2,1)S(1)} copy-done((bf16[8,3,2048]{2,0,1:T(8,128)(2,1)S(1)}, bf16[8,3,2048]{2,0,1:T(8,128)(2,1)}, u32[]{:S(2)}) %copy-start.3) | copy-done | bytes 98328
  2.3 0.0 copy-start.2
  2.3 0.1 collective-permute-start.3
  2.4 0.4 collective-permute-start.1
  2.8 1.7 %collective-permute-start.2 = (bf16[8,9,16,128]{3,2,1,0:T(8,128)(2,1)S(1)}, bf16[8,9,16,128]{3,2,1,0:T(8,128)(2,1)S(1)}, u32[]{:S(2)}, u32[]{:S(2)}) collective-permute-start(bf16[8,9,16,128]{3,2,1,0:T(8,128)(2,1)S(1)} %copy_dynamic-update-slice_fusion.refs_0_), channel_id=1, source_target_pairs={{0,96},{16,112},{32,0},{48,16},{64,32},{80,48},{96,64},{112,80},{1... | collective-permute-start | bytes 884744 | tf_op jit(solution)/shard_map/ppermute | solution.py:257
  4.5 1.4 %collective-permute-start = (bf16[8,9,16,128]{3,2,1,0:T(8,128)(2,1)S(1)}, bf16[8,9,16,128]{3,2,1,0:T(8,128)(2,1)S(1)}, u32[]{:S(2)}, u32[]{:S(2)}) collective-permute-start(bf16[8,9,16,128]{3,2,1,0:T(8,128)(2,1)S(1)} %copy_dynamic-update-slice_fusion.refs_0_), channel_id=1, source_target_pairs={{0,64},{16,80},{32,96},{48,112},{64,0},{80,16},{96,32},{112,48},{1... | collective-permute-start | bytes 884744 | tf_op jit(solution)/shard_map/ppermute | solution.py:257
  5.9 0.0 collective-permute-done.3.refs_1_
  5.9 0.0 copy-start.7
  5.9 0.0 copy-done.2
  5.9 0.7 copy-done.7
  6.6 9.3 %nearby0.1.refs_0_ = f32[8,128,256]{2,1,0:T(8,128)} custom-call(f32[1]{0:T(128)} %bitcast.1.first_ref, bf16[8,9,16,128]{3,2,1,0:T(8,128)(2,1)} %copy-done.2, bf16[8,9,16,128]{3,2,1,0:T(8,128)(2,1)} %copy-done.7), custom_call_target="tpu_custom_call" | custom-call | flops 2147483648 | bytes 589824 | tf_op jit(solution)/shard_map/nearby0/pallas_call | solution.py:173
  15.9 0.0 collective-permute-done.1.refs_1_
  16.0 0.0 copy-start.5
  16.0 3.5 %collective-permute-done.2.refs_2_ = bf16[8,9,16,128]{3,2,1,0:T(8,128)(2,1)S(1)} collective-permute-done((bf16[8,9,16,128]{3,2,1,0:T(8,128)(2,1)S(1)}, bf16[8,9,16,128]{3,2,1,0:T(8,128)(2,1)S(1)}, u32[]{:S(2)}, u32[]{:S(2)}) %collective-permute-start.2) | collective-permute-done | bytes 294944 | tf_op jit(solution)/shard_map/ppermute | solution.py:257
  19.4 0.0 copy-start.6
  19.4 0.0 collective-permute-start.4
  19.4 0.5 collective-permute-start.5
  19.9 0.0 copy-done.5
  19.9 0.2 copy-done.6
  20.1 9.7 %nearby1.1.refs_0_ = f32[8,128,256]{2,1,0:T(8,128)} custom-call(f32[1]{0:T(128)} %bitcast.1.first_ref, f32[8,128,256]{2,1,0:T(8,128)} %nearby0.1.refs_0_, bf16[8,9,16,128]{3,2,1,0:T(8,128)(2,1)} %copy-done.5, bf16[8,9,16,128]{3,2,1,0:T(8,128)(2,1)} %copy-done.6), custom_call_target="tpu_custom_call" | custom-call | flops 2147483648 | bytes 589824 | tf_op jit(solution)/shard_map/nearby1/pallas_call | solution.py:173
  29.8 0.0 collective-permute-done.refs_3_
  29.8 0.0 copy-start.4
  29.8 0.0 collective-permute-done.4.refs_1_
  29.8 0.0 copy-start.8
  29.9 0.0 collective-permute-done.5.refs_2_
  29.9 0.0 copy-start.9
  29.9 0.1 collective-permute-start.6
  30.0 1.6 %collective-permute-done.6.refs_4_ = bf16[8,9,16,128]{3,2,1,0:T(8,128)(2,1)S(1)} collective-permute-done((bf16[8,9,16,128]{3,2,1,0:T(8,128)(2,1)S(1)}, bf16[8,9,16,128]{3,2,1,0:T(8,128)(2,1)S(1)}, u32[]{:S(2)}, u32[]{:S(2)}) %collective-permute-start.6) | collective-permute-done | bytes 294944 | tf_op jit(solution)/shard_map/ppermute | solution.py:261
  31.5 0.0 copy-done.4
  31.5 0.0 copy-done.8
  31.5 0.0 copy-done.9
  31.5 0.0 copy-start.10
  31.6 0.7 copy-done.10
  32.3 9.6 %last1.1 = f32[16,4,16,128]{3,2,1,0:T(8,128)} custom-call(f32[1]{0:T(128)} %bitcast.1.first_ref, f32[8,128,256]{2,1,0:T(8,128)} %nearby1.1.refs_0_, bf16[8,9,16,128]{3,2,1,0:T(8,128)(2,1)} %copy-done.8, bf16[8,9,16,128]{3,2,1,0:T(8,128)(2,1)} %copy-done.9, bf16[8,9,16,128]{3,2,1,0:T(8,128)(2,1)} %copy-done.4, bf16[8,9,16,128]{3,2,1,0:T(8,128)(2,1)} %copy-done.10), custom_call_target="tpu_custom_call" | custom-call | flops 2147483648 | bytes 589824 | tf_op jit(solution)/shard_map/last1/pallas_call | solution.py:173
  41.8 8.2 %all-to-all-start.1 = ((f32[16,4,16,128]{3,2,1,0:T(8,128)}), f32[16,4,16,128]{3,2,1,0:T(8,128)S(1)}, u32[]{:S(2)}, u32[]{:S(2)}) async-start(f32[16,4,16,128]{3,2,1,0:T(8,128)} %last1.1), calls=%async_computation.1 | async-start | bytes 1048576 | tf_op jit(solution)/shard_map/all_to_all | solution.py:283
  50.0 9.6 %last0.1 = f32[16,4,16,128]{3,2,1,0:T(8,128)} custom-call(f32[1]{0:T(128)} %bitcast.1.first_ref, f32[8,128,256]{2,1,0:T(8,128)} %nearby1.1.refs_0_, bf16[8,9,16,128]{3,2,1,0:T(8,128)(2,1)} %copy-done.8, bf16[8,9,16,128]{3,2,1,0:T(8,128)(2,1)} %copy-done.9, bf16[8,9,16,128]{3,2,1,0:T(8,128)(2,1)} %copy-done.4, bf16[8,9,16,128]{3,2,1,0:T(8,128)(2,1)} %copy-done.10), custom_call_target="tpu_custom_call" | custom-call | flops 2147483648 | bytes 589824 | tf_op jit(solution)/shard_map/last0/pallas_call | solution.py:173
  59.6 2.3 %all-to-all-done.1.late = f32[16,4,16,128]{3,2,1,0:T(8,128)S(1)} async-done(((f32[16,4,16,128]{3,2,1,0:T(8,128)}), f32[16,4,16,128]{3,2,1,0:T(8,128)S(1)}, u32[]{:S(2)}, u32[]{:S(2)}) %all-to-all-start.1) | async-done | bytes 524320 | tf_op jit(solution)/shard_map/all_to_all | solution.py:283
  61.8 0.0 copy-start
  61.8 0.8 copy-done
  62.6 4.9 %all-to-all-start = ((f32[16,4,16,128]{3,2,1,0:T(8,128)}), f32[16,4,16,128]{3,2,1,0:T(8,128)S(1)}, u32[]{:S(2)}, u32[]{:S(2)}) async-start(f32[16,4,16,128]{3,2,1,0:T(8,128)} %last0.1), calls=%async_computation | async-start | bytes 1048576 | tf_op jit(solution)/shard_map/all_to_all | solution.py:283
  67.6 0.6 fusion.3.pick
  68.3 10.6 %all-to-all-done.early = f32[16,4,16,128]{3,2,1,0:T(8,128)S(1)} async-done(((f32[16,4,16,128]{3,2,1,0:T(8,128)}), f32[16,4,16,128]{3,2,1,0:T(8,128)S(1)}, u32[]{:S(2)}, u32[]{:S(2)}) %all-to-all-start) | async-done | bytes 524320 | tf_op jit(solution)/shard_map/all_to_all | solution.py:283
  78.9 0.8 copy-done.1
  79.7 4.9 %correlate.1 = f32[4,16,256]{2,1,0:T(8,128)} custom-call(s32[1]{0:T(128)} %bitcast.flip_ref, f32[16,4,16,128]{3,2,1,0:T(8,128)} %copy-done.1, f32[16,4,16,128]{3,2,1,0:T(8,128)} %copy-done, f32[128,128]{1,0:T(8,128)} %fusion.3.pick), custom_call_target="tpu_custom_call" | custom-call | tf_op jit(solution)/shard_map/correlate/pallas_call | solution.py:242
  (5 shorter events, 0.1 us)
Async XLA Ops:
  1.4 0.9 %copy-start.3 = (bf16[8,3,2048]{2,0,1:T(8,128)(2,1)S(1)}, bf16[8,3,2048]{2,0,1:T(8,128)(2,1)}, u32[]{:S(2)}) copy-start(bf16[8,3,2048]{2,0,1:T(8,128)(2,1)} %param.3) | copy-start | bytes 294916
  2.3 3.6 %copy-start.2 = (bf16[8,9,16,128]{3,2,1,0:T(8,128)(2,1)}, bf16[8,9,16,128]{3,2,1,0:T(8,128)(2,1)S(1)}, u32[]{:S(2)}) copy-start(bf16[8,9,16,128]{3,2,1,0:T(8,128)(2,1)S(1)} %copy_dynamic-update-slice_fusion.refs_0_) | copy-start | bytes 884740
  2.3 3.6 %collective-permute-start.3 = (bf16[8,9,16,128]{3,2,1,0:T(8,128)(2,1)S(1)}, bf16[8,9,16,128]{3,2,1,0:T(8,128)(2,1)S(1)}, u32[]{:S(2)}, u32[]{:S(2)}) collective-permute-start(bf16[8,9,16,128]{3,2,1,0:T(8,128)(2,1)S(1)} %copy_dynamic-update-slice_fusion.refs_0_), channel_id=1, source_target_pairs={{0,16},{16,0},{32,48},{48,32},{64,80},{80,64},{96,112},{112,96},{1... | collective-permute-start | bytes 884744 | tf_op jit(solution)/shard_map/ppermute | solution.py:261
  2.4 13.6 %collective-permute-start.1 = (bf16[8,9,16,128]{3,2,1,0:T(8,128)(2,1)S(1)}, bf16[8,9,16,128]{3,2,1,0:T(8,128)(2,1)S(1)}, u32[]{:S(2)}, u32[]{:S(2)}) collective-permute-start(bf16[8,9,16,128]{3,2,1,0:T(8,128)(2,1)S(1)} %copy_dynamic-update-slice_fusion.refs_0_), channel_id=1, source_target_pairs={{0,32},{16,48},{32,64},{48,80},{64,96},{80,112},{96,0},{112,16},{1... | collective-permute-start | bytes 884744 | tf_op jit(solution)/shard_map/ppermute | solution.py:257
  2.8 16.6 %collective-permute-start.2 = (bf16[8,9,16,128]{3,2,1,0:T(8,128)(2,1)S(1)}, bf16[8,9,16,128]{3,2,1,0:T(8,128)(2,1)S(1)}, u32[]{:S(2)}, u32[]{:S(2)}) collective-permute-start(bf16[8,9,16,128]{3,2,1,0:T(8,128)(2,1)S(1)} %copy_dynamic-update-slice_fusion.refs_0_), channel_id=1, source_target_pairs={{0,96},{16,112},{32,0},{48,16},{64,32},{80,48},{96,64},{112,80},{1... | collective-permute-start | bytes 884744 | tf_op jit(solution)/shard_map/ppermute | solution.py:257
  4.5 25.4 %collective-permute-start = (bf16[8,9,16,128]{3,2,1,0:T(8,128)(2,1)S(1)}, bf16[8,9,16,128]{3,2,1,0:T(8,128)(2,1)S(1)}, u32[]{:S(2)}, u32[]{:S(2)}) collective-permute-start(bf16[8,9,16,128]{3,2,1,0:T(8,128)(2,1)S(1)} %copy_dynamic-update-slice_fusion.refs_0_), channel_id=1, source_target_pairs={{0,64},{16,80},{32,96},{48,112},{64,0},{80,16},{96,32},{112,48},{1... | collective-permute-start | bytes 884744 | tf_op jit(solution)/shard_map/ppermute | solution.py:257
  5.9 0.7 copy-start.7
  16.0 4.0 %copy-start.5 = (bf16[8,9,16,128]{3,2,1,0:T(8,128)(2,1)}, bf16[8,9,16,128]{3,2,1,0:T(8,128)(2,1)S(1)}, u32[]{:S(2)}) copy-start(bf16[8,9,16,128]{3,2,1,0:T(8,128)(2,1)S(1)} %collective-permute-done.1.refs_1_) | copy-start | bytes 884740
  19.4 0.7 copy-start.6
  19.4 10.4 %collective-permute-start.4 = (bf16[8,9,16,128]{3,2,1,0:T(8,128)(2,1)S(1)}, bf16[8,9,16,128]{3,2,1,0:T(8,128)(2,1)S(1)}, u32[]{:S(2)}, u32[]{:S(2)}) collective-permute-start(bf16[8,9,16,128]{3,2,1,0:T(8,128)(2,1)S(1)} %collective-permute-done.1.refs_1_), channel_id=1, source_target_pairs={{0,16},{16,0},{32,48},{48,32},{64,80},{80,64},{96,112},{112,96},{1... | collective-permute-start | bytes 884744 | tf_op jit(solution)/shard_map/ppermute | solution.py:261
  19.4 10.4 %collective-permute-start.5 = (bf16[8,9,16,128]{3,2,1,0:T(8,128)(2,1)S(1)}, bf16[8,9,16,128]{3,2,1,0:T(8,128)(2,1)S(1)}, u32[]{:S(2)}, u32[]{:S(2)}) collective-permute-start(bf16[8,9,16,128]{3,2,1,0:T(8,128)(2,1)S(1)} %collective-permute-done.2.refs_2_), channel_id=1, source_target_pairs={{0,16},{16,0},{32,48},{48,32},{64,80},{80,64},{96,112},{112,96},{1... | collective-permute-start | bytes 884744 | tf_op jit(solution)/shard_map/ppermute | solution.py:261
  29.8 1.7 %copy-start.4 = (bf16[8,9,16,128]{3,2,1,0:T(8,128)(2,1)}, bf16[8,9,16,128]{3,2,1,0:T(8,128)(2,1)S(1)}, u32[]{:S(2)}) copy-start(bf16[8,9,16,128]{3,2,1,0:T(8,128)(2,1)S(1)} %collective-permute-done.refs_3_) | copy-start | bytes 884740
  29.8 1.7 %copy-start.8 = (bf16[8,9,16,128]{3,2,1,0:T(8,128)(2,1)}, bf16[8,9,16,128]{3,2,1,0:T(8,128)(2,1)S(1)}, u32[]{:S(2)}) copy-start(bf16[8,9,16,128]{3,2,1,0:T(8,128)(2,1)S(1)} %collective-permute-done.4.refs_1_) | copy-start | bytes 884740
  29.9 1.7 %copy-start.9 = (bf16[8,9,16,128]{3,2,1,0:T(8,128)(2,1)}, bf16[8,9,16,128]{3,2,1,0:T(8,128)(2,1)S(1)}, u32[]{:S(2)}) copy-start(bf16[8,9,16,128]{3,2,1,0:T(8,128)(2,1)S(1)} %collective-permute-done.5.refs_2_) | copy-start | bytes 884740
  29.9 1.7 %collective-permute-start.6 = (bf16[8,9,16,128]{3,2,1,0:T(8,128)(2,1)S(1)}, bf16[8,9,16,128]{3,2,1,0:T(8,128)(2,1)S(1)}, u32[]{:S(2)}, u32[]{:S(2)}) collective-permute-start(bf16[8,9,16,128]{3,2,1,0:T(8,128)(2,1)S(1)} %collective-permute-done.refs_3_), channel_id=1, source_target_pairs={{0,16},{16,0},{32,48},{48,32},{64,80},{80,64},{96,112},{112,96},{1... | collective-permute-start | bytes 884744 | tf_op jit(solution)/shard_map/ppermute | solution.py:261
  31.5 0.7 copy-start.10
  41.8 20.0 %all-to-all-start.1 = ((f32[16,4,16,128]{3,2,1,0:T(8,128)}), f32[16,4,16,128]{3,2,1,0:T(8,128)S(1)}, u32[]{:S(2)}, u32[]{:S(2)}) async-start(f32[16,4,16,128]{3,2,1,0:T(8,128)} %last1.1), calls=%async_computation.1 | async-start | bytes 1048576 | tf_op jit(solution)/shard_map/all_to_all | solution.py:283
  61.8 0.8 copy-start
  62.6 16.2 %all-to-all-start = ((f32[16,4,16,128]{3,2,1,0:T(8,128)}), f32[16,4,16,128]{3,2,1,0:T(8,128)S(1)}, u32[]{:S(2)}, u32[]{:S(2)}) async-start(f32[16,4,16,128]{3,2,1,0:T(8,128)} %last0.1), calls=%async_computation | async-start | bytes 1048576 | tf_op jit(solution)/shard_map/all_to_all | solution.py:283
  78.9 0.8 copy-start.1

commit v3 on v2

v3 whole, which is shorter than its diff:
```python
import functools
import math

import jax
import jax.numpy as jnp
from jax import lax
from jax.experimental import pallas as pl
from jax.experimental.pallas import tpu as pltpu
from jax.sharding import PartitionSpec as P

KX = 32
KY = 32
KZ = 32
LAGS = 16
LATTICE = 131072
ATOMS = 16384
FRAMES = 128
HALF = 16
ROWS = 59
SINE = (6.28318516, -41.3416550, 81.6010040, -76.5498338, 39.5367090)


def sine(u):
    square = u * u
    value = jnp.full_like(u, SINE[4])
    for factor in SINE[3::-1]:
        value = value * square + factor
    return value * u


def cos_sin(turns):
    r = turns - jnp.round(turns)
    c = sine(0.25 - jnp.abs(r))
    s = sine(jnp.maximum(jnp.minimum(r, 0.5 - r), -0.5 - r))
    return c, s


def double(c, s):
    return 2.0 * c * c - 1.0, 2.0 * s * c


def harmonics(here, before, twice, number):
    values = [here]
    for _ in range(number - 1):
        values.append(twice * values[-1] - before)
        before = values[-2]
    return values


def fill(data, first, odd, table):
    def put(row, values):
        for k, value in enumerate(values):
            table[pl.ds(row + k, 16, stride=ROWS), :] = value

    x, y, z = (
        (data[2 * a].astype(jnp.float32) * 512.0 + data[2 * a + 1].astype(jnp.float32))
        * (1.0 / LATTICE)
        for a in range(3)
    )
    c, s = cos_sin(x * first)
    c1, s1 = cos_sin(x)
    for i in range(4):
        put(2 * i, [c, s])
        if i < 3:
            c, s = c * c1 - s * s1, c * s1 + s * c1
    c1, s1 = cos_sin(y)
    c2, s2 = double(c1, s1)
    even = 1.0 - odd
    put(8, harmonics(odd * c1 + even * c2, odd * c1 + even, c2 + c2, 8))
    put(16, harmonics(odd * s1 + even * s2, -odd * s1, c2 + c2, 8))
    c1, s1 = cos_sin(z)
    put(24, harmonics(c1, jnp.ones_like(c1), c1 + c1, HALF))
    put(40, harmonics(s1, jnp.zeros_like(s1), c1 + c1, HALF))
    put(56, [data[6 + comp].astype(jnp.float32) for comp in range(3)])


def multiply(table, total):
    for pair in range(8):
        bases = [(2 * pair + k) * ROWS for k in range(2)]

        def rows(start, number):
            return [table[pl.ds(base + start, number), :] for base in bases]

        def wide(parts):
            return jnp.concatenate([p.astype(jnp.bfloat16) for p in parts], 1)

        yc, ys = rows(8, 8), rows(16, 8)
        left = []
        for i in range(4):
            cx, sx = rows(2 * i, 1), rows(2 * i + 1, 1)
            plus, minus = [], []
            for k in range(2):
                cc, sn = cx[k] * yc[k], sx[k] * ys[k]
                cn, sc = cx[k] * ys[k], sx[k] * yc[k]
                plus.append(jnp.concatenate([cc - sn, cn + sc], 0))
                minus.append(jnp.concatenate([cc + sn, sc - cn], 0))
            left += [wide(plus), wide(minus)]
        right = []
        for part in range(2):
            z = rows(24 + 16 * part, 16)
            right.append(wide(z))
            for comp in range(3):
                u = rows(56 + comp, 1)
                right.append(wide([z[k] * u[k] for k in range(2)]))
        total = total + lax.dot_general(
            jnp.concatenate(left, 0),
            jnp.concatenate(right, 0),
            (((1,), (1,)), ((), ())),
            preferred_element_type=jnp.float32,
        )
    return total


def modes_kernel(number, frames, more, last, waves, *refs):
    if more:
        before, refs = refs[0], refs[1:]
    data, out = refs[:number], refs[number]
    table_a, table_b, blocks, *rest = refs[number + 1 :]
    totals = rest[0] if last else out
    first, odd = waves[0], waves[1]
    steps = number * frames
    for g in range(number):
        for f in range(frames):
            blocks[f * number + g] = data[g][f]

    def block(index):
        return [blocks[index, k] for k in range(9)]

    totals[...] = before[...] if more else jnp.zeros_like(totals)
    fill(block(0), first, odd, table_a)

    def step(half, carry):
        now = 2 * half
        frame = now // number
        fill(block(now + 1), first, odd, table_b)
        total = multiply(table_a, totals[frame])
        fill(block(jnp.minimum(now + 2, steps - 1)), first, odd, table_a)
        totals[frame] = multiply(table_b, total)
        return carry

    lax.fori_loop(0, steps // 2, step, 0)
    if not last:
        return
    for f in range(frames):
        total = totals[f]
        for i in range(4):
            for b in range(4):
                minus, upper = b < 2, b in (0, 3)
                here = 32 * i + 16 * minus + 4 * upper
                there = 32 * (3 - i) + 16 * (not minus) + 4 * upper
                out[i * 4 + b, f] = jnp.concatenate(
                    [total[at + k : at + k + 4] for k in (0, 8) for at in (here, there)], 0
                )


def modes(waves, blocks, before=None, last=False):
    frames = blocks[0].shape[0]
    number, more = len(blocks), before is not None
    smem = pl.BlockSpec(memory_space=pltpu.SMEM)
    data = pl.BlockSpec((frames, 9, 16, 128), lambda _: (0, 0, 0, 0))
    sums = pl.BlockSpec((frames, 128, 128), lambda _: (0, 0, 0))
    owned = (16, frames, 16, 128)
    scratch = [
        pltpu.VMEM((16 * ROWS, 128), jnp.float32),
        pltpu.VMEM((16 * ROWS, 128), jnp.float32),
        pltpu.VMEM((number * frames, 9, 16, 128), jnp.bfloat16),
    ]
    work = number * frames * 2048
    return pl.pallas_call(
        functools.partial(modes_kernel, number, frames, more, last),
        grid=(1,),
        out_shape=jax.ShapeDtypeStruct(owned if last else (frames, 128, 128), jnp.float32),
        in_specs=[smem] + [sums] * more + [data] * number,
        out_specs=pl.BlockSpec(owned, lambda _: (0, 0, 0, 0)) if last else sums,
        scratch_shapes=scratch + [pltpu.VMEM((frames, 128, 128), jnp.float32)] * last,
        cost_estimate=pl.CostEstimate(
            flops=work * 128 * 128 * 2, bytes_accessed=work * 18, transcendentals=0
        ),
        name="last" if last else f"nearby{int(more)}",
    )(waves, *([before] * more), *blocks)


def correlate_kernel(flags, series, keep, send, d, e):
    frames = FRAMES
    d[frames:, :, :] = jnp.zeros((LAGS, 8, 128), jnp.float32)
    e[frames:, :, :] = jnp.zeros((LAGS, 8, 128), jnp.float32)

    def split(t, carry):
        values = series[t].astype(jnp.float32)
        real, imag = values[:8], pltpu.roll(values[8:], 64, 1)
        d[t] = real - imag
        e[t] = real + imag
        return carry

    lax.fori_loop(0, frames, split, 0, unroll=8)

    def lags(source):
        def step(t, sums):
            here = source[t]
            return tuple(sums[lag] + here * source[t + lag] for lag in range(LAGS))

        zero = jnp.zeros((8, 128), jnp.float32)
        return lax.fori_loop(0, frames, step, (zero,) * LAGS, unroll=4)

    sums_d, sums_e = lags(d), lags(e)
    mirrored = flags[1] == 1
    for lag in range(LAGS):
        value = (sums_d[lag] + pltpu.roll(sums_e[lag], 64, 1)) * (1.0 / (ATOMS * (frames - lag)))
        value = jnp.where(mirrored, pltpu.roll(value, 4, 0), value)
        keep[lag * 4 : lag * 4 + 4, :] = value[:4]
        send[lag * 4 : lag * 4 + 4, :] = value[4:]


def correlate(flags, series):
    vmem = pl.BlockSpec(memory_space=pltpu.VMEM)
    return pl.pallas_call(
        correlate_kernel,
        out_shape=[jax.ShapeDtypeStruct((4 * LAGS, 128), jnp.float32)] * 2,
        in_specs=[pl.BlockSpec(memory_space=pltpu.SMEM), vmem],
        out_specs=[vmem, vmem],
        scratch_shapes=[pltpu.VMEM((FRAMES + LAGS, 8, 128), jnp.float32)] * 2,
        name="correlate",
    )(flags, series)


def arrange_kernel(flags, keep, received, pick, out, rows):
    mirrored = flags[1] == 1
    kept, other = keep[...], received[...]
    rows[:64, :] = jnp.where(mirrored, other, kept)
    rows[64:, :] = jnp.where(mirrored, kept, other)
    rows[...] = jnp.dot(
        rows[...], pick[...], precision=lax.Precision.HIGHEST, preferred_element_type=jnp.float32
    )
    flip = flags[0] == 1
    lane = lax.broadcasted_iota(jnp.int32, (LAGS, 128), 1) // 32

    def wave(w):
        return rows[pl.ds(64 * (w % 2) + w // 2, LAGS, stride=4), :]

    for half in range(2):
        totals = [jnp.zeros((LAGS, 128), jnp.float32) for _ in range(4)]
        for part in range(4):
            w = half * 4 + part
            value = jnp.where(flip, wave(7 - w), wave(w))
            for comp in range(4):
                by = (32 * (part - comp)) % 128
                moved = pltpu.roll(value, by, 1) if by else value
                totals[comp] = jnp.where(lane == part, moved, totals[comp])
        for comp in range(4):
            out[comp, :, half * 128 : half * 128 + 128] = totals[comp]


def arrange(flags, keep, received):
    lane = jnp.arange(128)
    comp, q = lane // 32, lane % 32
    falling, rising = comp * 16 + 15 - q, comp * 16 + q - 16
    side = 64 * flags[1]
    source = jnp.where(q < 16, 64 - side + falling, side + rising)
    pick = (lane[:, None] == source[None, :]).astype(jnp.float32)
    vmem = pl.BlockSpec(memory_space=pltpu.VMEM)
    return pl.pallas_call(
        arrange_kernel,
        out_shape=jax.ShapeDtypeStruct((4, LAGS, 256), jnp.float32),
        in_specs=[pl.BlockSpec(memory_space=pltpu.SMEM), vmem, vmem, vmem],
        out_specs=vmem,
        scratch_shapes=[pltpu.VMEM((128, 128), jnp.float32)],
        name="arrange",
    )(flags, keep, received, pick)


def shift(block, by):
    return lax.ppermute(block, "atom", [(i, (i + by) % 8) for i in range(8)])


def swap(block):
    return lax.ppermute(block, "atom", [(i, i ^ 1) for i in range(8)])


def per_device(positions, velocity):
    a = lax.axis_index("atom")
    t = lax.axis_index("tm")
    frames = positions.shape[0]
    low = ((positions + 256) & 511) - 256
    high = (positions - low) >> 9
    parts = jnp.stack([high, low], 2).reshape(frames, 6, 16, 128).astype(jnp.bfloat16)
    own = jnp.concatenate([parts, velocity.reshape(frames, 3, 16, 128)], 1)
    positive = a >= 4
    first = 4 * jnp.maximum(a, 7 - a) - 15
    waves = jnp.stack([first, positive.astype(jnp.int32)]).astype(jnp.float32)
    left, right, across = shift(own, 2), shift(own, 6), shift(own, 4)
    sums = modes(waves, [own, swap(own)])
    left, right, sums = lax.optimization_barrier((left, right, sums))
    far = [swap(left), swap(right)]
    sums = modes(waves, [left, right], sums)
    across, sums, *far = lax.optimization_barrier((across, sums, *far))
    local = modes(waves, far + [across, swap(across)], sums, True)
    series = lax.all_to_all(local, "tm", split_axis=0, concat_axis=0, tiled=True)
    flags = jnp.stack([t % 4 < 2, ~positive]).astype(jnp.int32)
    keep, send = correlate(flags, series.reshape(FRAMES, 16, 128))
    received = lax.ppermute(send, "atom", [(i, 7 - i) for i in range(8)])
    return arrange(flags, keep, received)


def solution(mesh):
    in_specs = (P("tm", None, "atom"), P("tm", None, "atom"))
    out_specs = P(None, None, ("atom", "tm"))
    return jax.shard_map(
        per_device, mesh=mesh, in_specs=in_specs, out_specs=out_specs, check_vma=False
    )
```

time: 85.1 us -> 82 us (0.964)
  the two profiles are of different devices: /device:TPU:6 before, /device:TPU:1 now
where the time goes in v3:
time: 82 us; the launch traced here: 81.6 us
  Pallas kernels  32.7 us (40%)
  starting transfers between devices  23.6 us (29%)
  waiting for transfers between devices  17.4 us (21%)
  local copies, waits for them, and re-layouts  4.9 us (6%)
  other arithmetic  2.26 us (3%)
    pallas_call x3, Pallas kernels, modes(): pl.pallas_call(functools.partial(modes_kernel, number, frames, more, last...  26.3 us
    all_to_all x1, waiting for transfers between devices, per_device(): lax.all_to_all(local, 'tm', split_axis=0, concat_axis=0, tiled=True)  15 us
    all_to_all x1, starting transfers between devices, per_device(): lax.all_to_all(local, 'tm', split_axis=0, concat_axis=0, tiled=True)  10.6 us
    ppermute x1, starting transfers between devices, per_device(): received = lax.ppermute(send, 'atom', [(i, 7 - i) for i in range(8)])  5.38 us
    pallas_call x1, Pallas kernels, correlate(): pl.pallas_call(correlate_kernel, out_shape=[jax.ShapeDtypeStruct((4 * LAG...  4.6 us
    ppermute x3, starting transfers between devices, shift(): return lax.ppermute(block, 'atom', [(i, (i + by) % 8) for i in range(8)])  4.32 us
    unnamed x25, local copies, waits for them, and re-layouts  3.95 us
    ppermute x4, starting transfers between devices, swap(): return lax.ppermute(block, 'atom', [(i, i ^ 1) for i in range(8)])  3.24 us
  transfers between devices with their start and end apart: 9, of which 3 were waited for; matrix products, arithmetic and copies ran while one was open for 2% of the time, Pallas kernels for 17%

profile of v3, /device:TPU:1, one launch (start us, length us, event | category | flops | bytes accessed | tf_op | source)
XLA Modules:
  0.0 81.6 jit_solution(14836553194415308399)
XLA Ops:
  0.0 1.0 %fusion.2 = (bf16[8,3,1,2048]{3,0,1,2:T(8,128)(2,1)S(1)}, bf16[8,3,1,2048]{3,0,1,2:T(8,128)(2,1)S(1)}) fusion(s32[8,3,2048]{2,0,1:T(8,128)} %param.2), kind=kLoop, calls=%fused_computation.5 | loop fusion | flops 344064 | bytes 393216 | tf_op jit(solution)/shard_map/stack | solution.py:285
  1.0 0.2 copy.5
  1.2 0.1 convert_element_type.16
  1.4 0.0 copy-start.2
  1.4 0.9 %copy-done.2 = bf16[8,3,2048]{2,0,1:T(8,128)(2,1)S(1)} copy-done((bf16[8,3,2048]{2,0,1:T(8,128)(2,1)S(1)}, bf16[8,3,2048]{2,0,1:T(8,128)(2,1)}, u32[]{:S(2)}) %copy-start.2) | copy-done | bytes 98328
  2.3 0.0 copy-start.1
  2.3 1.5 %collective-permute-start.3 = (bf16[8,9,16,128]{3,2,1,0:T(8,128)(2,1)S(1)}, bf16[8,9,16,128]{3,2,1,0:T(8,128)(2,1)S(1)}, u32[]{:S(2)}, u32[]{:S(2)}) collective-permute-start(bf16[8,9,16,128]{3,2,1,0:T(8,128)(2,1)S(1)} %copy_dynamic-update-slice_fusion.refs_0_), channel_id=1, source_target_pairs={{0,16},{16,0},{32,48},{48,32},{64,80},{80,64},{96,112},{112,96},{1... | collective-permute-start | bytes 884744 | tf_op jit(solution)/shard_map/ppermute | solution.py:276
  3.8 1.3 %collective-permute-start.1 = (bf16[8,9,16,128]{3,2,1,0:T(8,128)(2,1)S(1)}, bf16[8,9,16,128]{3,2,1,0:T(8,128)(2,1)S(1)}, u32[]{:S(2)}, u32[]{:S(2)}) collective-permute-start(bf16[8,9,16,128]{3,2,1,0:T(8,128)(2,1)S(1)} %copy_dynamic-update-slice_fusion.refs_0_), channel_id=1, source_target_pairs={{0,32},{16,48},{32,64},{48,80},{64,96},{80,112},{96,0},{112,16},{1... | collective-permute-start | bytes 884744 | tf_op jit(solution)/shard_map/ppermute | solution.py:272
  5.1 1.4 %collective-permute-start.2 = (bf16[8,9,16,128]{3,2,1,0:T(8,128)(2,1)S(1)}, bf16[8,9,16,128]{3,2,1,0:T(8,128)(2,1)S(1)}, u32[]{:S(2)}, u32[]{:S(2)}) collective-permute-start(bf16[8,9,16,128]{3,2,1,0:T(8,128)(2,1)S(1)} %copy_dynamic-update-slice_fusion.refs_0_), channel_id=1, source_target_pairs={{0,96},{16,112},{32,0},{48,16},{64,32},{80,48},{96,64},{112,80},{1... | collective-permute-start | bytes 884744 | tf_op jit(solution)/shard_map/ppermute | solution.py:272
  6.4 1.6 %collective-permute-start = (bf16[8,9,16,128]{3,2,1,0:T(8,128)(2,1)S(1)}, bf16[8,9,16,128]{3,2,1,0:T(8,128)(2,1)S(1)}, u32[]{:S(2)}, u32[]{:S(2)}) collective-permute-start(bf16[8,9,16,128]{3,2,1,0:T(8,128)(2,1)S(1)} %copy_dynamic-update-slice_fusion.refs_0_), channel_id=1, source_target_pairs={{0,64},{16,80},{32,96},{48,112},{64,0},{80,16},{96,32},{112,48},{1... | collective-permute-start | bytes 884744 | tf_op jit(solution)/shard_map/ppermute | solution.py:272
  8.1 0.6 add_convert_fusion.1.waves
  8.6 0.0 collective-permute-done.3.refs_1_
  8.6 0.0 copy-done.1
  8.6 0.0 copy-start.8
  8.6 0.7 copy-done.8
  9.4 6.9 %nearby0.1.refs_0_ = f32[8,128,128]{2,1,0:T(8,128)} custom-call(f32[2]{0:T(128)} %add_convert_fusion.1.waves, bf16[8,9,16,128]{3,2,1,0:T(8,128)(2,1)} %copy-done.1, bf16[8,9,16,128]{3,2,1,0:T(8,128)(2,1)} %copy-done.8), custom_call_target="tpu_custom_call" | custom-call | flops 1073741824 | bytes 589824 | tf_op jit(solution)/shard_map/nearby0/pallas_call | solution.py:169
  16.2 0.0 collective-permute-done.1.refs_1_
  16.2 0.0 collective-permute-done.2.refs_2_
  16.2 0.0 copy-start.7
  16.3 1.0 %collective-permute-start.4 = (bf16[8,9,16,128]{3,2,1,0:T(8,128)(2,1)S(1)}, bf16[8,9,16,128]{3,2,1,0:T(8,128)(2,1)S(1)}, u32[]{:S(2)}, u32[]{:S(2)}) collective-permute-start(bf16[8,9,16,128]{3,2,1,0:T(8,128)(2,1)S(1)} %collective-permute-done.1.refs_1_), channel_id=1, source_target_pairs={{0,16},{16,0},{32,48},{48,32},{64,80},{80,64},{96,112},{112,96},{1... | collective-permute-start | bytes 884744 | tf_op jit(solution)/shard_map/ppermute | solution.py:276
  17.3 0.1 collective-permute-start.5
  17.3 0.0 copy-done.6
  17.4 0.0 copy-done.7
  17.4 7.0 %nearby1.1.refs_0_ = f32[8,128,128]{2,1,0:T(8,128)} custom-call(f32[2]{0:T(128)} %add_convert_fusion.1.waves, f32[8,128,128]{2,1,0:T(8,128)} %nearby0.1.refs_0_, bf16[8,9,16,128]{3,2,1,0:T(8,128)(2,1)} %copy-done.6, bf16[8,9,16,128]{3,2,1,0:T(8,128)(2,1)} %copy-done.7), custom_call_target="tpu_custom_call" | custom-call | flops 1073741824 | bytes 589824 | tf_op jit(solution)/shard_map/nearby1/pallas_call | solution.py:169
  24.4 0.0 collective-permute-done.refs_3_
  24.4 0.0 collective-permute-done.4.refs_1_
  24.4 0.0 copy-start.9
  24.4 0.0 collective-permute-done.5.refs_2_
  24.4 0.0 copy-start.10
  24.4 0.7 collective-permute-start.6
  25.1 1.2 %collective-permute-done.6.refs_4_ = bf16[8,9,16,128]{3,2,1,0:T(8,128)(2,1)S(1)} collective-permute-done((bf16[8,9,16,128]{3,2,1,0:T(8,128)(2,1)S(1)}, bf16[8,9,16,128]{3,2,1,0:T(8,128)(2,1)S(1)}, u32[]{:S(2)}, u32[]{:S(2)}) %collective-permute-start.6) | collective-permute-done | bytes 294944 | tf_op jit(solution)/shard_map/ppermute | solution.py:276
  26.3 0.0 copy-done.5
  26.3 0.0 copy-done.9
  26.3 0.0 copy-done.10
  26.3 0.7 copy-done.11
  27.1 12.4 %last.1 = f32[16,8,16,128]{3,2,1,0:T(8,128)} custom-call(f32[2]{0:T(128)} %add_convert_fusion.1.waves, f32[8,128,128]{2,1,0:T(8,128)} %nearby1.1.refs_0_, bf16[8,9,16,128]{3,2,1,0:T(8,128)(2,1)} %copy-done.9, bf16[8,9,16,128]{3,2,1,0:T(8,128)(2,1)} %copy-done.10, bf16[8,9,16,128]{3,2,1,0:T(8,128)(2,1)} %copy-done.5, bf16[8,9,16,128]{3,2,1,0:T(8,128)(2,1)} %copy-done.11), custom_call_target="tpu_custom_call" | custom-call | flops 2147483648 | bytes 1179648 | tf_op jit(solution)/shard_map/last/pallas_call | solution.py:169
  39.4 10.6 %all-to-all-start = ((f32[16,8,16,128]{3,2,1,0:T(8,128)}), f32[16,8,16,128]{3,2,1,0:T(8,128)S(1)}, u32[]{:S(2)}, u32[]{:S(2)}) async-start(f32[16,8,16,128]{3,2,1,0:T(8,128)} %last.1), calls=%async_computation | async-start | bytes 2097152 | tf_op jit(solution)/shard_map/all_to_all | solution.py:297
  50.1 0.1 add_convert_fusion.flags
  50.2 0.6 slice.3
  50.7 0.0 copy-done.4
  51.4 15.0 %all-to-all-done = f32[16,8,16,128]{3,2,1,0:T(8,128)S(1)} async-done(((f32[16,8,16,128]{3,2,1,0:T(8,128)}), f32[16,8,16,128]{3,2,1,0:T(8,128)S(1)}, u32[]{:S(2)}, u32[]{:S(2)}) %all-to-all-start) | async-done | bytes 1048608 | tf_op jit(solution)/shard_map/all_to_all | solution.py:297
  66.4 1.0 %copy-done = f32[16,8,16,128]{3,2,1,0:T(8,128)} copy-done((f32[16,8,16,128]{3,2,1,0:T(8,128)}, f32[16,8,16,128]{3,2,1,0:T(8,128)S(1)}, u32[]{:S(2)}) %copy-start) | copy-done | bytes 1048600
  67.4 4.6 %correlate.1 = (f32[64,128]{1,0:T(8,128)}, f32[64,128]{1,0:T(8,128)}) custom-call(s32[2]{0:T(128)} %copy-done.4, f32[128,16,128]{2,1,0:T(8,128)} %bitcast.18), custom_call_target="tpu_custom_call" | custom-call | tf_op jit(solution)/shard_map/correlate/pallas_call | solution.py:216
  72.0 5.4 %collective-permute-start.7 = (f32[64,128]{1,0:T(8,128)}, f32[64,128]{1,0:T(8,128)S(1)}, u32[]{:S(2)}, u32[]{:S(2)}) collective-permute-start(f32[64,128]{1,0:T(8,128)} %get-tuple-element.22), channel_id=1, source_target_pairs={{0,112},{16,96},{32,80},{48,64},{64,48},{80,32},{96,16},{112,0},{1... | collective-permute-start | bytes 98312 | tf_op jit(solution)/shard_map/ppermute | solution.py:300
  77.4 0.6 fusion.3.pick
  78.0 1.2 %collective-permute-done.7.received = f32[64,128]{1,0:T(8,128)S(1)} collective-permute-done((f32[64,128]{1,0:T(8,128)}, f32[64,128]{1,0:T(8,128)S(1)}, u32[]{:S(2)}, u32[]{:S(2)}) %collective-permute-start.7) | collective-permute-done | bytes 32800 | tf_op jit(solution)/shard_map/ppermute | solution.py:300
  79.2 0.6 copy-done.3
  79.8 1.8 %arrange.1 = f32[4,16,256]{2,1,0:T(8,128)} custom-call(s32[2]{0:T(128)} %copy-done.4, f32[64,128]{1,0:T(8,128)} %get-tuple-element.21.keep, f32[64,128]{1,0:T(8,128)} %copy-done.3, f32[128,128]{1,0:T(8,128)} %fusion.3.pick), custom_call_target="tpu_custom_call" | custom-call | tf_op jit(solution)/shard_map/arrange/pallas_call | solution.py:261
  (10 shorter events, 0.1 us)
Async XLA Ops:
  1.4 0.9 %copy-start.2 = (bf16[8,3,2048]{2,0,1:T(8,128)(2,1)S(1)}, bf16[8,3,2048]{2,0,1:T(8,128)(2,1)}, u32[]{:S(2)}) copy-start(bf16[8,3,2048]{2,0,1:T(8,128)(2,1)} %param.3) | copy-start | bytes 294916
  2.3 6.4 %copy-start.1 = (bf16[8,9,16,128]{3,2,1,0:T(8,128)(2,1)}, bf16[8,9,16,128]{3,2,1,0:T(8,128)(2,1)S(1)}, u32[]{:S(2)}) copy-start(bf16[8,9,16,128]{3,2,1,0:T(8,128)(2,1)S(1)} %copy_dynamic-update-slice_fusion.refs_0_) | copy-start | bytes 884740
  2.3 6.3 %collective-permute-start.3 = (bf16[8,9,16,128]{3,2,1,0:T(8,128)(2,1)S(1)}, bf16[8,9,16,128]{3,2,1,0:T(8,128)(2,1)S(1)}, u32[]{:S(2)}, u32[]{:S(2)}) collective-permute-start(bf16[8,9,16,128]{3,2,1,0:T(8,128)(2,1)S(1)} %copy_dynamic-update-slice_fusion.refs_0_), channel_id=1, source_target_pairs={{0,16},{16,0},{32,48},{48,32},{64,80},{80,64},{96,112},{112,96},{1... | collective-permute-start | bytes 884744 | tf_op jit(solution)/shard_map/ppermute | solution.py:276
  3.8 12.5 %collective-permute-start.1 = (bf16[8,9,16,128]{3,2,1,0:T(8,128)(2,1)S(1)}, bf16[8,9,16,128]{3,2,1,0:T(8,128)(2,1)S(1)}, u32[]{:S(2)}, u32[]{:S(2)}) collective-permute-start(bf16[8,9,16,128]{3,2,1,0:T(8,128)(2,1)S(1)} %copy_dynamic-update-slice_fusion.refs_0_), channel_id=1, source_target_pairs={{0,32},{16,48},{32,64},{48,80},{64,96},{80,112},{96,0},{112,16},{1... | collective-permute-start | bytes 884744 | tf_op jit(solution)/shard_map/ppermute | solution.py:272
  5.1 11.2 %collective-permute-start.2 = (bf16[8,9,16,128]{3,2,1,0:T(8,128)(2,1)S(1)}, bf16[8,9,16,128]{3,2,1,0:T(8,128)(2,1)S(1)}, u32[]{:S(2)}, u32[]{:S(2)}) collective-permute-start(bf16[8,9,16,128]{3,2,1,0:T(8,128)(2,1)S(1)} %copy_dynamic-update-slice_fusion.refs_0_), channel_id=1, source_target_pairs={{0,96},{16,112},{32,0},{48,16},{64,32},{80,48},{96,64},{112,80},{1... | collective-permute-start | bytes 884744 | tf_op jit(solution)/shard_map/ppermute | solution.py:272
  6.4 18.0 %collective-permute-start = (bf16[8,9,16,128]{3,2,1,0:T(8,128)(2,1)S(1)}, bf16[8,9,16,128]{3,2,1,0:T(8,128)(2,1)S(1)}, u32[]{:S(2)}, u32[]{:S(2)}) collective-permute-start(bf16[8,9,16,128]{3,2,1,0:T(8,128)(2,1)S(1)} %copy_dynamic-update-slice_fusion.refs_0_), channel_id=1, source_target_pairs={{0,64},{16,80},{32,96},{48,112},{64,0},{80,16},{96,32},{112,48},{1... | collective-permute-start | bytes 884744 | tf_op jit(solution)/shard_map/ppermute | solution.py:272
  8.6 0.7 copy-start.8
  16.2 1.1 %copy-start.6 = (bf16[8,9,16,128]{3,2,1,0:T(8,128)(2,1)}, bf16[8,9,16,128]{3,2,1,0:T(8,128)(2,1)S(1)}, u32[]{:S(2)}) copy-start(bf16[8,9,16,128]{3,2,1,0:T(8,128)(2,1)S(1)} %collective-permute-done.1.refs_1_) | copy-start | bytes 884740
  16.2 1.1 %copy-start.7 = (bf16[8,9,16,128]{3,2,1,0:T(8,128)(2,1)}, bf16[8,9,16,128]{3,2,1,0:T(8,128)(2,1)S(1)}, u32[]{:S(2)}) copy-start(bf16[8,9,16,128]{3,2,1,0:T(8,128)(2,1)S(1)} %collective-permute-done.2.refs_2_) | copy-start | bytes 884740
  16.3 8.1 %collective-permute-start.4 = (bf16[8,9,16,128]{3,2,1,0:T(8,128)(2,1)S(1)}, bf16[8,9,16,128]{3,2,1,0:T(8,128)(2,1)S(1)}, u32[]{:S(2)}, u32[]{:S(2)}) collective-permute-start(bf16[8,9,16,128]{3,2,1,0:T(8,128)(2,1)S(1)} %collective-permute-done.1.refs_1_), channel_id=1, source_target_pairs={{0,16},{16,0},{32,48},{48,32},{64,80},{80,64},{96,112},{112,96},{1... | collective-permute-start | bytes 884744 | tf_op jit(solution)/shard_map/ppermute | solution.py:276
  17.3 7.2 %collective-permute-start.5 = (bf16[8,9,16,128]{3,2,1,0:T(8,128)(2,1)S(1)}, bf16[8,9,16,128]{3,2,1,0:T(8,128)(2,1)S(1)}, u32[]{:S(2)}, u32[]{:S(2)}) collective-permute-start(bf16[8,9,16,128]{3,2,1,0:T(8,128)(2,1)S(1)} %collective-permute-done.2.refs_2_), channel_id=1, source_target_pairs={{0,16},{16,0},{32,48},{48,32},{64,80},{80,64},{96,112},{112,96},{1... | collective-permute-start | bytes 884744 | tf_op jit(solution)/shard_map/ppermute | solution.py:276
  24.4 1.9 %copy-start.5 = (bf16[8,9,16,128]{3,2,1,0:T(8,128)(2,1)}, bf16[8,9,16,128]{3,2,1,0:T(8,128)(2,1)S(1)}, u32[]{:S(2)}) copy-start(bf16[8,9,16,128]{3,2,1,0:T(8,128)(2,1)S(1)} %collective-permute-done.refs_3_) | copy-start | bytes 884740
  24.4 1.9 %copy-start.9 = (bf16[8,9,16,128]{3,2,1,0:T(8,128)(2,1)}, bf16[8,9,16,128]{3,2,1,0:T(8,128)(2,1)S(1)}, u32[]{:S(2)}) copy-start(bf16[8,9,16,128]{3,2,1,0:T(8,128)(2,1)S(1)} %collective-permute-done.4.refs_1_) | copy-start | bytes 884740
  24.4 1.9 %copy-start.10 = (bf16[8,9,16,128]{3,2,1,0:T(8,128)(2,1)}, bf16[8,9,16,128]{3,2,1,0:T(8,128)(2,1)S(1)}, u32[]{:S(2)}) copy-start(bf16[8,9,16,128]{3,2,1,0:T(8,128)(2,1)S(1)} %collective-permute-done.5.refs_2_) | copy-start | bytes 884740
  24.4 1.9 %collective-permute-start.6 = (bf16[8,9,16,128]{3,2,1,0:T(8,128)(2,1)S(1)}, bf16[8,9,16,128]{3,2,1,0:T(8,128)(2,1)S(1)}, u32[]{:S(2)}, u32[]{:S(2)}) collective-permute-start(bf16[8,9,16,128]{3,2,1,0:T(8,128)(2,1)S(1)} %collective-permute-done.refs_3_), channel_id=1, source_target_pairs={{0,16},{16,0},{32,48},{48,32},{64,80},{80,64},{96,112},{112,96},{1... | collective-permute-start | bytes 884744 | tf_op jit(solution)/shard_map/ppermute | solution.py:276
  26.3 0.7 copy-start.11
  39.4 27.0 %all-to-all-start = ((f32[16,8,16,128]{3,2,1,0:T(8,128)}), f32[16,8,16,128]{3,2,1,0:T(8,128)S(1)}, u32[]{:S(2)}, u32[]{:S(2)}) async-start(f32[16,8,16,128]{3,2,1,0:T(8,128)} %last.1), calls=%async_computation | async-start | bytes 2097152 | tf_op jit(solution)/shard_map/all_to_all | solution.py:297
  50.2 0.6 copy-start.4
  66.4 1.0 %copy-start = (f32[16,8,16,128]{3,2,1,0:T(8,128)}, f32[16,8,16,128]{3,2,1,0:T(8,128)S(1)}, u32[]{:S(2)}) copy-start(f32[16,8,16,128]{3,2,1,0:T(8,128)S(1)} %all-to-all-done) | copy-start | bytes 3145732
  72.0 7.2 %collective-permute-start.7 = (f32[64,128]{1,0:T(8,128)}, f32[64,128]{1,0:T(8,128)S(1)}, u32[]{:S(2)}, u32[]{:S(2)}) collective-permute-start(f32[64,128]{1,0:T(8,128)} %get-tuple-element.22), channel_id=1, source_target_pairs={{0,112},{16,96},{32,80},{48,64},{64,48},{80,32},{96,16},{112,0},{1... | collective-permute-start | bytes 98312 | tf_op jit(solution)/shard_map/ppermute | solution.py:300
  79.2 0.6 copy-start.3

commit v4 on v3

--- a/solution.py
+++ b/solution.py
@@ -16,8 +16,14 @@
 ATOMS = 16384
 FRAMES = 128
 HALF = 16
+LINK = jnp.bfloat16
 ROWS = 59
 SINE = (6.28318516, -41.3416550, 81.6010040, -76.5498338, 39.5367090)
+
+
+def place():
+    a, t = lax.axis_index("atom"), lax.axis_index("tm")
+    return jnp.maximum(a, 7 - a), (a >= 4).astype(jnp.int32), t
 
 
 def sine(u):
@@ -111,13 +117,14 @@
     return total
 
 
-def modes_kernel(number, frames, more, last, waves, *refs):
+def modes_kernel(number, frames, more, last, *refs):
     if more:
         before, refs = refs[0], refs[1:]
     data, out = refs[:number], refs[number]
     table_a, table_b, blocks, *rest = refs[number + 1 :]
     totals = rest[0] if last else out
-    first, odd = waves[0], waves[1]
+    pair, upper, _ = place()
+    first, odd = (4 * pair - 15).astype(jnp.float32), upper.astype(jnp.float32)
     steps = number * frames
     for g in range(number):
         for f in range(frames):
@@ -142,24 +149,24 @@
     if not last:
         return
     for f in range(frames):
-        total = totals[f]
+        total = totals[f].astype(LINK)
         for i in range(4):
             for b in range(4):
-                minus, upper = b < 2, b in (0, 3)
-                here = 32 * i + 16 * minus + 4 * upper
-                there = 32 * (3 - i) + 16 * (not minus) + 4 * upper
-                out[i * 4 + b, f] = jnp.concatenate(
-                    [total[at + k : at + k + 4] for k in (0, 8) for at in (here, there)], 0
-                )
-
-
-def modes(waves, blocks, before=None, last=False):
+                minus, outer = b < 2, b in (0, 3)
+                here = 32 * i + 16 * minus + 4 * outer
+                there = 32 * (3 - i) + 16 * (not minus) + 4 * outer
+                for side, at in enumerate((there, here)):
+                    out[side * 16 + i * 4 + b, f] = jnp.concatenate(
+                        [total[at : at + 4], total[at + 8 : at + 12]], 0
+                    )
+
+
+def modes(blocks, before=None, last=False):
     frames = blocks[0].shape[0]
     number, more = len(blocks), before is not None
-    smem = pl.BlockSpec(memory_space=pltpu.SMEM)
     data = pl.BlockSpec((frames, 9, 16, 128), lambda _: (0, 0, 0, 0))
     sums = pl.BlockSpec((frames, 128, 128), lambda _: (0, 0, 0))
-    owned = (16, frames, 16, 128)
+    owned = (32, frames, 8, 128)
     scratch = [
         pltpu.VMEM((16 * ROWS, 128), jnp.float32),
         pltpu.VMEM((16 * ROWS, 128), jnp.float32),
@@ -169,25 +176,29 @@
     return pl.pallas_call(
         functools.partial(modes_kernel, number, frames, more, last),
         grid=(1,),
-        out_shape=jax.ShapeDtypeStruct(owned if last else (frames, 128, 128), jnp.float32),
-        in_specs=[smem] + [sums] * more + [data] * number,
+        out_shape=jax.ShapeDtypeStruct(owned, LINK)
+        if last
+        else jax.ShapeDtypeStruct((frames, 128, 128), jnp.float32),
+        in_specs=[sums] * more + [data] * number,
         out_specs=pl.BlockSpec(owned, lambda _: (0, 0, 0, 0)) if last else sums,
         scratch_shapes=scratch + [pltpu.VMEM((frames, 128, 128), jnp.float32)] * last,
         cost_estimate=pl.CostEstimate(
             flops=work * 128 * 128 * 2, bytes_accessed=work * 18, transcendentals=0
         ),
         name="last" if last else f"nearby{int(more)}",
-    )(waves, *([before] * more), *blocks)
-
-
-def correlate_kernel(flags, series, keep, send, d, e):
+    )(*([before] * more), *blocks)
+
+
+def correlate_kernel(series, out, d, e, rows):
     frames = FRAMES
     d[frames:, :, :] = jnp.zeros((LAGS, 8, 128), jnp.float32)
     e[frames:, :, :] = jnp.zeros((LAGS, 8, 128), jnp.float32)
+    lower = lax.broadcasted_iota(jnp.int32, (8, 128), 0) < 4
 
     def split(t, carry):
-        values = series[t].astype(jnp.float32)
-        real, imag = values[:8], pltpu.roll(values[8:], 64, 1)
+        even, odd = (series[side, t].astype(jnp.float32) for side in range(2))
+        real = jnp.where(lower, odd, pltpu.roll(even, 4, 0))
+        imag = pltpu.roll(jnp.where(lower, pltpu.roll(odd, 4, 0), even), 64, 1)
         d[t] = real - imag
         e[t] = real + imag
         return carry
@@ -203,39 +214,24 @@
         return lax.fori_loop(0, frames, step, (zero,) * LAGS, unroll=4)
 
     sums_d, sums_e = lags(d), lags(e)
-    mirrored = flags[1] == 1
     for lag in range(LAGS):
         value = (sums_d[lag] + pltpu.roll(sums_e[lag], 64, 1)) * (1.0 / (ATOMS * (frames - lag)))
-        value = jnp.where(mirrored, pltpu.roll(value, 4, 0), value)
-        keep[lag * 4 : lag * 4 + 4, :] = value[:4]
-        send[lag * 4 : lag * 4 + 4, :] = value[4:]
-
-
-def correlate(flags, series):
-    vmem = pl.BlockSpec(memory_space=pltpu.VMEM)
-    return pl.pallas_call(
-        correlate_kernel,
-        out_shape=[jax.ShapeDtypeStruct((4 * LAGS, 128), jnp.float32)] * 2,
-        in_specs=[pl.BlockSpec(memory_space=pltpu.SMEM), vmem],
-        out_specs=[vmem, vmem],
-        scratch_shapes=[pltpu.VMEM((FRAMES + LAGS, 8, 128), jnp.float32)] * 2,
-        name="correlate",
-    )(flags, series)
-
-
-def arrange_kernel(flags, keep, received, pick, out, rows):
-    mirrored = flags[1] == 1
-    kept, other = keep[...], received[...]
-    rows[:64, :] = jnp.where(mirrored, other, kept)
-    rows[64:, :] = jnp.where(mirrored, kept, other)
+        rows[lag * 8 : lag * 8 + 8, :] = value
+
+    _, upper, t = place()
+    lane = lax.broadcasted_iota(jnp.int32, (128, 128), 1)
+    comp, q = (lane // 32) * 16, lane % 32
+    falling, rising = comp + 15 - q, comp + q - 16
+    source = jnp.where(q < 16, 64 * upper + falling, 64 * (1 - upper) + rising)
+    pick = (lax.broadcasted_iota(jnp.int32, (128, 128), 0) == source).astype(jnp.float32)
     rows[...] = jnp.dot(
-        rows[...], pick[...], precision=lax.Precision.HIGHEST, preferred_element_type=jnp.float32
+        rows[...], pick, precision=lax.Precision.HIGHEST, preferred_element_type=jnp.float32
     )
-    flip = flags[0] == 1
-    lane = lax.broadcasted_iota(jnp.int32, (LAGS, 128), 1) // 32
+    flip = t % 4 < 2
+    group = lax.broadcasted_iota(jnp.int32, (LAGS, 128), 1) // 32
 
     def wave(w):
-        return rows[pl.ds(64 * (w % 2) + w // 2, LAGS, stride=4), :]
+        return rows[pl.ds(4 * (w % 2) + w // 2, LAGS, stride=8), :]
 
     for half in range(2):
         totals = [jnp.zeros((LAGS, 128), jnp.float32) for _ in range(4)]
@@ -245,27 +241,25 @@
             for comp in range(4):
                 by = (32 * (part - comp)) % 128
                 moved = pltpu.roll(value, by, 1) if by else value
-                totals[comp] = jnp.where(lane == part, moved, totals[comp])
+                totals[comp] = jnp.where(group == part, moved, totals[comp])
         for comp in range(4):
             out[comp, :, half * 128 : half * 128 + 128] = totals[comp]
 
 
-def arrange(flags, keep, received):
-    lane = jnp.arange(128)
-    comp, q = lane // 32, lane % 32
-    falling, rising = comp * 16 + 15 - q, comp * 16 + q - 16
-    side = 64 * flags[1]
-    source = jnp.where(q < 16, 64 - side + falling, side + rising)
-    pick = (lane[:, None] == source[None, :]).astype(jnp.float32)
+def correlate(series):
     vmem = pl.BlockSpec(memory_space=pltpu.VMEM)
     return pl.pallas_call(
-        arrange_kernel,
+        correlate_kernel,
         out_shape=jax.ShapeDtypeStruct((4, LAGS, 256), jnp.float32),
-        in_specs=[pl.BlockSpec(memory_space=pltpu.SMEM), vmem, vmem, vmem],
+        in_specs=[vmem],
         out_specs=vmem,
-        scratch_shapes=[pltpu.VMEM((128, 128), jnp.float32)],
-        name="arrange",
-    )(flags, keep, received, pick)
+        scratch_shapes=[
+            pltpu.VMEM((FRAMES + LAGS, 8, 128), jnp.float32),
+            pltpu.VMEM((FRAMES + LAGS, 8, 128), jnp.float32),
+            pltpu.VMEM((128, 128), jnp.float32),
+        ],
+        name="correlate",
+    )(series)
 
 
 def shift(block, by):
@@ -276,29 +270,27 @@
     return lax.ppermute(block, "atom", [(i, i ^ 1) for i in range(8)])
 
 
+def exchange(local):
+    groups = [[a * 16 + t for a in (lower, 7 - lower) for t in range(16)] for lower in range(4)]
+    series = lax.all_to_all(
+        local, ("atom", "tm"), 0, 0, tiled=True, axis_index_groups=groups
+    )
+    return series.reshape(2, FRAMES, 8, 128)
+
+
 def per_device(positions, velocity):
-    a = lax.axis_index("atom")
-    t = lax.axis_index("tm")
     frames = positions.shape[0]
     low = ((positions + 256) & 511) - 256
     high = (positions - low) >> 9
     parts = jnp.stack([high, low], 2).reshape(frames, 6, 16, 128).astype(jnp.bfloat16)
     own = jnp.concatenate([parts, velocity.reshape(frames, 3, 16, 128)], 1)
-    positive = a >= 4
-    first = 4 * jnp.maximum(a, 7 - a) - 15
-    waves = jnp.stack([first, positive.astype(jnp.int32)]).astype(jnp.float32)
     left, right, across = shift(own, 2), shift(own, 6), shift(own, 4)
-    sums = modes(waves, [own, swap(own)])
+    sums = modes([own, swap(own)])
     left, right, sums = lax.optimization_barrier((left, right, sums))
     far = [swap(left), swap(right)]
-    sums = modes(waves, [left, right], sums)
+    sums = modes([left, right], sums)
     across, sums, *far = lax.optimization_barrier((across, sums, *far))
-    local = modes(waves, far + [across, swap(across)], sums, True)
-    series = lax.all_to_all(local, "tm", split_axis=0, concat_axis=0, tiled=True)
-    flags = jnp.stack([t % 4 < 2, ~positive]).astype(jnp.int32)
-    keep, send = correlate(flags, series.reshape(FRAMES, 16, 128))
-    received = lax.ppermute(send, "atom", [(i, 7 - i) for i in range(8)])
-    return arrange(flags, keep, received)
+    return correlate(exchange(modes(far + [across, swap(across)], sums, True)))
 
 
 def solution(mesh):

time: 82 us -> 71.8 us (0.88)
  blocking collectives: 0 us -> 21.4 us
  starting transfers between devices: 23.6 us -> 7.79 us
  waiting for transfers between devices: 17.4 us -> 7.63 us
  local copies, waits for them, and re-layouts: 4.9 us -> 2.7 us
  Pallas kernels: 32.7 us -> 30.8 us
  other arithmetic: 2.26 us -> 1 us
    all_to_all x0 -> x1, blocking collectives: none -> 21.4 us  [exchange(): lax.all_to_all(local, ('atom', 'tm'), 0, 0, tiled=True, axis_index_groups...]
    all_to_all x1 -> x0, waiting for transfers between devices: 15 us -> none  [per_device(): lax.all_to_all(local, 'tm', split_axis=0, concat_axis=0, tiled=True)]
    all_to_all x1 -> x0, starting transfers between devices: 10.6 us -> none  [per_device(): lax.all_to_all(local, 'tm', split_axis=0, concat_axis=0, tiled=True)]
    ppermute x3, waiting for transfers between devices: 0.01 us -> 6.42 us  [shift(): return lax.ppermute(block, 'atom', [(i, (i + by) % 8) for i in range(8)])]
    ppermute x1 -> x0, starting transfers between devices: 5.38 us -> none  [per_device(): received = lax.ppermute(send, 'atom', [(i, 7 - i) for i in range(8)])]
    pallas_call x2 -> x1, Pallas kernels: 6.44 us -> 4.76 us  [correlate(): pl.pallas_call(correlate_kernel, out_shape=jax.ShapeDtypeStruct((4, LAGS,...]
    unnamed x25 -> x19, local copies, waits for them, and re-layouts: 3.95 us -> 2.34 us
    convert_element_type x3 -> x0, other arithmetic: 1.25 us -> none  [the longest x1 0.63 us: arrange(): pick = (lane[:, None] == source[None, :]).astype(jnp.float32)]
  transfers between devices with their start and end apart: 9 -> 7, of which waited for: 3 -> 3; matrix products, arithmetic and copies ran while one was open for 2% -> 0% of each run, Pallas kernels for 17% -> 19%
where the time goes in v4:
time: 71.8 us; the launch traced here: 71.4 us
  Pallas kernels  30.8 us (43%)
  blocking collectives  21.4 us (30%)
  starting transfers between devices  7.79 us (11%)
  waiting for transfers between devices  7.63 us (11%)
  local copies, waits for them, and re-layouts  2.7 us (4%)
  other arithmetic  1 us (1%)
    pallas_call x3, Pallas kernels, modes(): pl.pallas_call(functools.partial(modes_kernel, number, frames, more, last...  26.1 us
    all_to_all x1, blocking collectives, exchange(): lax.all_to_all(local, ('atom', 'tm'), 0, 0, tiled=True, axis_index_groups...  21.4 us
    ppermute x3, waiting for transfers between devices, shift(): return lax.ppermute(block, 'atom', [(i, (i + by) % 8) for i in range(8)])  6.42 us
    pallas_call x1, Pallas kernels, correlate(): pl.pallas_call(correlate_kernel, out_shape=jax.ShapeDtypeStruct((4, LAGS,...  4.76 us
    ppermute x3, starting transfers between devices, shift(): return lax.ppermute(block, 'atom', [(i, (i + by) % 8) for i in range(8)])  4.32 us
    ppermute x4, starting transfers between devices, swap(): return lax.ppermute(block, 'atom', [(i, i ^ 1) for i in range(8)])  3.47 us
    unnamed x19, local copies, waits for them, and re-layouts  2.34 us
  transfers between devices with their start and end apart: 7, of which 3 were waited for; matrix products, arithmetic and copies ran while one was open for 0% of the time, Pallas kernels for 19%

profile of v4, /device:TPU:1, one launch (start us, length us, event | category | flops | bytes accessed | tf_op | source)
XLA Modules:
  0.0 71.4 jit_solution(8605906947562094749)
XLA Ops:
  0.0 1.0 %fusion.2 = (bf16[8,3,1,2048]{3,0,1,2:T(8,128)(2,1)S(1)}, bf16[8,3,1,2048]{3,0,1,2:T(8,128)(2,1)S(1)}) fusion(s32[8,3,2048]{2,0,1:T(8,128)} %param.2), kind=kLoop, calls=%fused_computation.5 | loop fusion | flops 344064 | bytes 393216 | tf_op jit(solution)/shard_map/stack | solution.py:285
  1.0 0.2 copy.5
  1.2 0.1 convert_element_type.4
  1.4 0.0 copy-start.1
  1.4 0.9 %copy-done.1 = bf16[8,3,2048]{2,0,1:T(8,128)(2,1)S(1)} copy-done((bf16[8,3,2048]{2,0,1:T(8,128)(2,1)S(1)}, bf16[8,3,2048]{2,0,1:T(8,128)(2,1)}, u32[]{:S(2)}) %copy-start.1) | copy-done | bytes 98328
  2.3 0.0 copy-start
  2.3 1.5 %collective-permute-start.3 = (bf16[8,9,16,128]{3,2,1,0:T(8,128)(2,1)S(1)}, bf16[8,9,16,128]{3,2,1,0:T(8,128)(2,1)S(1)}, u32[]{:S(2)}, u32[]{:S(2)}) collective-permute-start(bf16[8,9,16,128]{3,2,1,0:T(8,128)(2,1)S(1)} %copy_dynamic-update-slice_fusion.refs_0_), channel_id=1, source_target_pairs={{0,16},{16,0},{32,48},{48,32},{64,80},{80,64},{96,112},{112,96},{1... | collective-permute-start | bytes 884744 | tf_op jit(solution)/shard_map/ppermute | solution.py:270
  3.8 2.6 %collective-permute-start.2 = (bf16[8,9,16,128]{3,2,1,0:T(8,128)(2,1)S(1)}, bf16[8,9,16,128]{3,2,1,0:T(8,128)(2,1)S(1)}, u32[]{:S(2)}, u32[]{:S(2)}) collective-permute-start(bf16[8,9,16,128]{3,2,1,0:T(8,128)(2,1)S(1)} %copy_dynamic-update-slice_fusion.refs_0_), channel_id=1, source_target_pairs={{0,96},{16,112},{32,0},{48,16},{64,32},{80,48},{96,64},{112,80},{1... | collective-permute-start | bytes 884744 | tf_op jit(solution)/shard_map/ppermute | solution.py:266
  6.3 0.0 collective-permute-start.1
  6.3 1.7 %collective-permute-start = (bf16[8,9,16,128]{3,2,1,0:T(8,128)(2,1)S(1)}, bf16[8,9,16,128]{3,2,1,0:T(8,128)(2,1)S(1)}, u32[]{:S(2)}, u32[]{:S(2)}) collective-permute-start(bf16[8,9,16,128]{3,2,1,0:T(8,128)(2,1)S(1)} %copy_dynamic-update-slice_fusion.refs_0_), channel_id=1, source_target_pairs={{0,64},{16,80},{32,96},{48,112},{64,0},{80,16},{96,32},{112,48},{1... | collective-permute-start | bytes 884744 | tf_op jit(solution)/shard_map/ppermute | solution.py:266
  8.1 0.0 collective-permute-done.3.refs_1_
  8.1 0.0 copy-done
  8.1 0.0 copy-start.7
  8.1 0.7 %copy-done.7 = bf16[8,9,16,128]{3,2,1,0:T(8,128)(2,1)} copy-done((bf16[8,9,16,128]{3,2,1,0:T(8,128)(2,1)}, bf16[8,9,16,128]{3,2,1,0:T(8,128)(2,1)S(1)}, u32[]{:S(2)}) %copy-start.7) | copy-done | bytes 294936
  8.8 6.9 %nearby0.1.refs_0_ = f32[8,128,128]{2,1,0:T(8,128)} custom-call(bf16[8,9,16,128]{3,2,1,0:T(8,128)(2,1)} %copy-done, bf16[8,9,16,128]{3,2,1,0:T(8,128)(2,1)} %copy-done.7), custom_call_target="tpu_custom_call" | custom-call | flops 1073741824 | bytes 589824 | tf_op jit(solution)/shard_map/nearby0/pallas_call | solution.py:176
  15.7 3.1 %collective-permute-done.2.refs_2_ = bf16[8,9,16,128]{3,2,1,0:T(8,128)(2,1)S(1)} collective-permute-done((bf16[8,9,16,128]{3,2,1,0:T(8,128)(2,1)S(1)}, bf16[8,9,16,128]{3,2,1,0:T(8,128)(2,1)S(1)}, u32[]{:S(2)}, u32[]{:S(2)}) %collective-permute-start.2) | collective-permute-done | bytes 294944 | tf_op jit(solution)/shard_map/ppermute | solution.py:266
  18.8 0.0 copy-start.3
  18.8 3.3 %collective-permute-done.1.refs_1_ = bf16[8,9,16,128]{3,2,1,0:T(8,128)(2,1)S(1)} collective-permute-done((bf16[8,9,16,128]{3,2,1,0:T(8,128)(2,1)S(1)}, bf16[8,9,16,128]{3,2,1,0:T(8,128)(2,1)S(1)}, u32[]{:S(2)}, u32[]{:S(2)}) %collective-permute-start.1) | collective-permute-done | bytes 294944 | tf_op jit(solution)/shard_map/ppermute | solution.py:266
  22.1 0.0 copy-start.4
  22.1 1.2 %collective-permute-start.4 = (bf16[8,9,16,128]{3,2,1,0:T(8,128)(2,1)S(1)}, bf16[8,9,16,128]{3,2,1,0:T(8,128)(2,1)S(1)}, u32[]{:S(2)}, u32[]{:S(2)}) collective-permute-start(bf16[8,9,16,128]{3,2,1,0:T(8,128)(2,1)S(1)} %collective-permute-done.1.refs_1_), channel_id=1, source_target_pairs={{0,16},{16,0},{32,48},{48,32},{64,80},{80,64},{96,112},{112,96},{1... | collective-permute-start | bytes 884744 | tf_op jit(solution)/shard_map/ppermute | solution.py:270
  23.3 0.0 collective-permute-start.5
  23.3 0.0 copy-done.3
  23.3 0.0 copy-done.4
  23.3 7.0 %nearby1.1.refs_0_ = f32[8,128,128]{2,1,0:T(8,128)} custom-call(f32[8,128,128]{2,1,0:T(8,128)} %nearby0.1.refs_0_, bf16[8,9,16,128]{3,2,1,0:T(8,128)(2,1)} %copy-done.4, bf16[8,9,16,128]{3,2,1,0:T(8,128)(2,1)} %copy-done.3), custom_call_target="tpu_custom_call" | custom-call | flops 1073741824 | bytes 589824 | tf_op jit(solution)/shard_map/nearby1/pallas_call | solution.py:176
  30.3 0.0 collective-permute-done.refs_3_
  30.3 0.0 copy-start.2
  30.3 0.0 collective-permute-done.4.refs_1_
  30.3 0.0 copy-start.5
  30.4 0.0 collective-permute-done.5.refs_2_
  30.4 0.0 copy-start.6
  30.4 0.8 %collective-permute-start.6 = (bf16[8,9,16,128]{3,2,1,0:T(8,128)(2,1)S(1)}, bf16[8,9,16,128]{3,2,1,0:T(8,128)(2,1)S(1)}, u32[]{:S(2)}, u32[]{:S(2)}) collective-permute-start(bf16[8,9,16,128]{3,2,1,0:T(8,128)(2,1)S(1)} %collective-permute-done.refs_3_), channel_id=1, source_target_pairs={{0,16},{16,0},{32,48},{48,32},{64,80},{80,64},{96,112},{112,96},{1... | collective-permute-start | bytes 884744 | tf_op jit(solution)/shard_map/ppermute | solution.py:270
  31.2 1.2 %collective-permute-done.6.refs_4_ = bf16[8,9,16,128]{3,2,1,0:T(8,128)(2,1)S(1)} collective-permute-done((bf16[8,9,16,128]{3,2,1,0:T(8,128)(2,1)S(1)}, bf16[8,9,16,128]{3,2,1,0:T(8,128)(2,1)S(1)}, u32[]{:S(2)}, u32[]{:S(2)}) %collective-permute-start.6) | collective-permute-done | bytes 294944 | tf_op jit(solution)/shard_map/ppermute | solution.py:270
  32.4 0.0 copy-done.2
  32.4 0.0 copy-done.5
  32.4 0.0 copy-done.6
  32.4 0.0 copy-start.8
  32.4 0.7 copy-done.8
  33.1 12.2 %last.1 = bf16[32,8,8,128]{3,2,1,0:T(8,128)(2,1)} custom-call(f32[8,128,128]{2,1,0:T(8,128)} %nearby1.1.refs_0_, bf16[8,9,16,128]{3,2,1,0:T(8,128)(2,1)} %copy-done.5, bf16[8,9,16,128]{3,2,1,0:T(8,128)(2,1)} %copy-done.6, bf16[8,9,16,128]{3,2,1,0:T(8,128)(2,1)} %copy-done.2, bf16[8,9,16,128]{3,2,1,0:T(8,128)(2,1)} %copy-done.8), custom_call_target="tpu_custom_call" | custom-call | flops 2147483648 | bytes 1179648 | tf_op jit(solution)/shard_map/last/pallas_call | solution.py:176
  45.3 21.4 %all_to_all.5 = bf16[32,8,8,128]{3,2,1,0:T(8,128)(2,1)} all-to-all(bf16[32,8,8,128]{3,2,1,0:T(8,128)(2,1)} %last.1), channel_id=1, replica_groups={{0,1,2,3,4,5,6,7,8,9,10,11,12,13,14,15,112,113,114,115,116,117,118,119,..., dimensions={0} | all-to-all | bytes 1048576 | tf_op jit(solution)/shard_map/all_to_all | solution.py:275
  66.7 4.8 %correlate.1 = f32[4,16,256]{2,1,0:T(8,128)} custom-call(bf16[2,128,8,128]{3,2,1,0:T(8,128)(2,1)} %bitcast.13), custom_call_target="tpu_custom_call" | custom-call | tf_op jit(solution)/shard_map/correlate/pallas_call | solution.py:251
  (3 shorter events, 0.1 us)
Async XLA Ops:
  1.4 0.9 %copy-start.1 = (bf16[8,3,2048]{2,0,1:T(8,128)(2,1)S(1)}, bf16[8,3,2048]{2,0,1:T(8,128)(2,1)}, u32[]{:S(2)}) copy-start(bf16[8,3,2048]{2,0,1:T(8,128)(2,1)} %param.3) | copy-start | bytes 294916
  2.3 5.8 %copy-start = (bf16[8,9,16,128]{3,2,1,0:T(8,128)(2,1)}, bf16[8,9,16,128]{3,2,1,0:T(8,128)(2,1)S(1)}, u32[]{:S(2)}) copy-start(bf16[8,9,16,128]{3,2,1,0:T(8,128)(2,1)S(1)} %copy_dynamic-update-slice_fusion.refs_0_) | copy-start | bytes 884740
  2.3 5.8 %collective-permute-start.3 = (bf16[8,9,16,128]{3,2,1,0:T(8,128)(2,1)S(1)}, bf16[8,9,16,128]{3,2,1,0:T(8,128)(2,1)S(1)}, u32[]{:S(2)}, u32[]{:S(2)}) collective-permute-start(bf16[8,9,16,128]{3,2,1,0:T(8,128)(2,1)S(1)} %copy_dynamic-update-slice_fusion.refs_0_), channel_id=1, source_target_pairs={{0,16},{16,0},{32,48},{48,32},{64,80},{80,64},{96,112},{112,96},{1... | collective-permute-start | bytes 884744 | tf_op jit(solution)/shard_map/ppermute | solution.py:270
  3.8 15.1 %collective-permute-start.2 = (bf16[8,9,16,128]{3,2,1,0:T(8,128)(2,1)S(1)}, bf16[8,9,16,128]{3,2,1,0:T(8,128)(2,1)S(1)}, u32[]{:S(2)}, u32[]{:S(2)}) collective-permute-start(bf16[8,9,16,128]{3,2,1,0:T(8,128)(2,1)S(1)} %copy_dynamic-update-slice_fusion.refs_0_), channel_id=1, source_target_pairs={{0,96},{16,112},{32,0},{48,16},{64,32},{80,48},{96,64},{112,80},{1... | collective-permute-start | bytes 884744 | tf_op jit(solution)/shard_map/ppermute | solution.py:266
  6.3 15.7 %collective-permute-start.1 = (bf16[8,9,16,128]{3,2,1,0:T(8,128)(2,1)S(1)}, bf16[8,9,16,128]{3,2,1,0:T(8,128)(2,1)S(1)}, u32[]{:S(2)}, u32[]{:S(2)}) collective-permute-start(bf16[8,9,16,128]{3,2,1,0:T(8,128)(2,1)S(1)} %copy_dynamic-update-slice_fusion.refs_0_), channel_id=1, source_target_pairs={{0,32},{16,48},{32,64},{48,80},{64,96},{80,112},{96,0},{112,16},{1... | collective-permute-start | bytes 884744 | tf_op jit(solution)/shard_map/ppermute | solution.py:266
  6.3 24.0 %collective-permute-start = (bf16[8,9,16,128]{3,2,1,0:T(8,128)(2,1)S(1)}, bf16[8,9,16,128]{3,2,1,0:T(8,128)(2,1)S(1)}, u32[]{:S(2)}, u32[]{:S(2)}) collective-permute-start(bf16[8,9,16,128]{3,2,1,0:T(8,128)(2,1)S(1)} %copy_dynamic-update-slice_fusion.refs_0_), channel_id=1, source_target_pairs={{0,64},{16,80},{32,96},{48,112},{64,0},{80,16},{96,32},{112,48},{1... | collective-permute-start | bytes 884744 | tf_op jit(solution)/shard_map/ppermute | solution.py:266
  8.1 0.7 %copy-start.7 = (bf16[8,9,16,128]{3,2,1,0:T(8,128)(2,1)}, bf16[8,9,16,128]{3,2,1,0:T(8,128)(2,1)S(1)}, u32[]{:S(2)}) copy-start(bf16[8,9,16,128]{3,2,1,0:T(8,128)(2,1)S(1)} %collective-permute-done.3.refs_1_) | copy-start | bytes 884740
  18.8 4.5 %copy-start.3 = (bf16[8,9,16,128]{3,2,1,0:T(8,128)(2,1)}, bf16[8,9,16,128]{3,2,1,0:T(8,128)(2,1)S(1)}, u32[]{:S(2)}) copy-start(bf16[8,9,16,128]{3,2,1,0:T(8,128)(2,1)S(1)} %collective-permute-done.2.refs_2_) | copy-start | bytes 884740
  22.1 1.2 %copy-start.4 = (bf16[8,9,16,128]{3,2,1,0:T(8,128)(2,1)}, bf16[8,9,16,128]{3,2,1,0:T(8,128)(2,1)S(1)}, u32[]{:S(2)}) copy-start(bf16[8,9,16,128]{3,2,1,0:T(8,128)(2,1)S(1)} %collective-permute-done.1.refs_1_) | copy-start | bytes 884740
  22.1 8.3 %collective-permute-start.4 = (bf16[8,9,16,128]{3,2,1,0:T(8,128)(2,1)S(1)}, bf16[8,9,16,128]{3,2,1,0:T(8,128)(2,1)S(1)}, u32[]{:S(2)}, u32[]{:S(2)}) collective-permute-start(bf16[8,9,16,128]{3,2,1,0:T(8,128)(2,1)S(1)} %collective-permute-done.1.refs_1_), channel_id=1, source_target_pairs={{0,16},{16,0},{32,48},{48,32},{64,80},{80,64},{96,112},{112,96},{1... | collective-permute-start | bytes 884744 | tf_op jit(solution)/shard_map/ppermute | solution.py:270
  23.3 7.1 %collective-permute-start.5 = (bf16[8,9,16,128]{3,2,1,0:T(8,128)(2,1)S(1)}, bf16[8,9,16,128]{3,2,1,0:T(8,128)(2,1)S(1)}, u32[]{:S(2)}, u32[]{:S(2)}) collective-permute-start(bf16[8,9,16,128]{3,2,1,0:T(8,128)(2,1)S(1)} %collective-permute-done.2.refs_2_), channel_id=1, source_target_pairs={{0,16},{16,0},{32,48},{48,32},{64,80},{80,64},{96,112},{112,96},{1... | collective-permute-start | bytes 884744 | tf_op jit(solution)/shard_map/ppermute | solution.py:270
  30.3 2.0 %copy-start.2 = (bf16[8,9,16,128]{3,2,1,0:T(8,128)(2,1)}, bf16[8,9,16,128]{3,2,1,0:T(8,128)(2,1)S(1)}, u32[]{:S(2)}) copy-start(bf16[8,9,16,128]{3,2,1,0:T(8,128)(2,1)S(1)} %collective-permute-done.refs_3_) | copy-start | bytes 884740
  30.3 2.0 %copy-start.5 = (bf16[8,9,16,128]{3,2,1,0:T(8,128)(2,1)}, bf16[8,9,16,128]{3,2,1,0:T(8,128)(2,1)S(1)}, u32[]{:S(2)}) copy-start(bf16[8,9,16,128]{3,2,1,0:T(8,128)(2,1)S(1)} %collective-permute-done.4.refs_1_) | copy-start | bytes 884740
  30.4 2.0 %copy-start.6 = (bf16[8,9,16,128]{3,2,1,0:T(8,128)(2,1)}, bf16[8,9,16,128]{3,2,1,0:T(8,128)(2,1)S(1)}, u32[]{:S(2)}) copy-start(bf16[8,9,16,128]{3,2,1,0:T(8,128)(2,1)S(1)} %collective-permute-done.5.refs_2_) | copy-start | bytes 884740
  30.4 2.0 %collective-permute-start.6 = (bf16[8,9,16,128]{3,2,1,0:T(8,128)(2,1)S(1)}, bf16[8,9,16,128]{3,2,1,0:T(8,128)(2,1)S(1)}, u32[]{:S(2)}, u32[]{:S(2)}) collective-permute-start(bf16[8,9,16,128]{3,2,1,0:T(8,128)(2,1)S(1)} %collective-permute-done.refs_3_), channel_id=1, source_target_pairs={{0,16},{16,0},{32,48},{48,32},{64,80},{80,64},{96,112},{112,96},{1... | collective-permute-start | bytes 884744 | tf_op jit(solution)/shard_map/ppermute | solution.py:270
  32.4 0.7 copy-start.8

commit v5 on v4

--- a/solution.py
+++ b/solution.py
@@ -17,7 +17,7 @@
 FRAMES = 128
 HALF = 16
 LINK = jnp.bfloat16
-ROWS = 59
+ROWS = 75
 SINE = (6.28318516, -41.3416550, 81.6010040, -76.5498338, 39.5367090)
 
 
@@ -41,10 +41,6 @@
     return c, s
 
 
-def double(c, s):
-    return 2.0 * c * c - 1.0, 2.0 * s * c
-
-
 def harmonics(here, before, twice, number):
     values = [here]
     for _ in range(number - 1):
@@ -53,7 +49,7 @@
     return values
 
 
-def fill(data, first, odd, table):
+def fill(data, first, table):
     def put(row, values):
         for k, value in enumerate(values):
             table[pl.ds(row + k, 16, stride=ROWS), :] = value
@@ -69,15 +65,11 @@
         put(2 * i, [c, s])
         if i < 3:
             c, s = c * c1 - s * s1, c * s1 + s * c1
-    c1, s1 = cos_sin(y)
-    c2, s2 = double(c1, s1)
-    even = 1.0 - odd
-    put(8, harmonics(odd * c1 + even * c2, odd * c1 + even, c2 + c2, 8))
-    put(16, harmonics(odd * s1 + even * s2, -odd * s1, c2 + c2, 8))
-    c1, s1 = cos_sin(z)
-    put(24, harmonics(c1, jnp.ones_like(c1), c1 + c1, HALF))
-    put(40, harmonics(s1, jnp.zeros_like(s1), c1 + c1, HALF))
-    put(56, [data[6 + comp].astype(jnp.float32) for comp in range(3)])
+    for row, angle in ((8, y), (40, z)):
+        c1, s1 = cos_sin(angle)
+        put(row, harmonics(c1, jnp.ones_like(c1), c1 + c1, HALF))
+        put(row + HALF, harmonics(s1, jnp.zeros_like(s1), c1 + c1, HALF))
+    put(72, [data[6 + comp].astype(jnp.float32) for comp in range(3)])
 
 
 def multiply(table, total):
@@ -90,23 +82,25 @@
         def wide(parts):
             return jnp.concatenate([p.astype(jnp.bfloat16) for p in parts], 1)
 
-        yc, ys = rows(8, 8), rows(16, 8)
+        yc = [rows(8 + 8 * b, 8) for b in range(2)]
+        ys = [rows(24 + 8 * b, 8) for b in range(2)]
         left = []
         for i in range(4):
             cx, sx = rows(2 * i, 1), rows(2 * i + 1, 1)
-            plus, minus = [], []
-            for k in range(2):
-                cc, sn = cx[k] * yc[k], sx[k] * ys[k]
-                cn, sc = cx[k] * ys[k], sx[k] * yc[k]
-                plus.append(jnp.concatenate([cc - sn, cn + sc], 0))
-                minus.append(jnp.concatenate([cc + sn, sc - cn], 0))
-            left += [wide(plus), wide(minus)]
+            for b in range(2):
+                plus, minus = [], []
+                for k in range(2):
+                    cc, sn = cx[k] * yc[b][k], sx[k] * ys[b][k]
+                    cn, sc = cx[k] * ys[b][k], sx[k] * yc[b][k]
+                    plus.append(jnp.concatenate([cc - sn, cn + sc], 0))
+                    minus.append(jnp.concatenate([cc + sn, sc - cn], 0))
+                left += [wide(plus), wide(minus)]
         right = []
         for part in range(2):
-            z = rows(24 + 16 * part, 16)
+            z = rows(40 + 16 * part, 16)
             right.append(wide(z))
             for comp in range(3):
-                u = rows(56 + comp, 1)
+                u = rows(72 + comp, 1)
                 right.append(wide([z[k] * u[k] for k in range(2)]))
         total = total + lax.dot_general(
             jnp.concatenate(left, 0),
@@ -123,8 +117,7 @@
     data, out = refs[:number], refs[number]
     table_a, table_b, blocks, *rest = refs[number + 1 :]
     totals = rest[0] if last else out
-    pair, upper, _ = place()
-    first, odd = (4 * pair - 15).astype(jnp.float32), upper.astype(jnp.float32)
+    first = (4 * place()[0] - 15).astype(jnp.float32)
     steps = number * frames
     for g in range(number):
         for f in range(frames):
@@ -134,14 +127,14 @@
         return [blocks[index, k] for k in range(9)]
 
     totals[...] = before[...] if more else jnp.zeros_like(totals)
-    fill(block(0), first, odd, table_a)
+    fill(block(0), first, table_a)
 
     def step(half, carry):
         now = 2 * half
         frame = now // number
-        fill(block(now + 1), first, odd, table_b)
+        fill(block(now + 1), first, table_b)
         total = multiply(table_a, totals[frame])
-        fill(block(jnp.minimum(now + 2, steps - 1)), first, odd, table_a)
+        fill(block(jnp.minimum(now + 2, steps - 1)), first, table_a)
         totals[frame] = multiply(table_b, total)
         return carry
 
@@ -153,20 +146,18 @@
         for i in range(4):
             for b in range(4):
                 minus, outer = b < 2, b in (0, 3)
-                here = 32 * i + 16 * minus + 4 * outer
-                there = 32 * (3 - i) + 16 * (not minus) + 4 * outer
-                for side, at in enumerate((there, here)):
-                    out[side * 16 + i * 4 + b, f] = jnp.concatenate(
-                        [total[at : at + 4], total[at + 8 : at + 12]], 0
-                    )
+                here = 64 * i + 32 * outer + 16 * minus
+                there = 64 * (3 - i) + 32 * outer + 16 * (not minus)
+                out[i * 4 + b, f] = total[there : there + 16]
+                out[16 + i * 4 + b, f] = total[here : here + 16]
 
 
 def modes(blocks, before=None, last=False):
     frames = blocks[0].shape[0]
     number, more = len(blocks), before is not None
     data = pl.BlockSpec((frames, 9, 16, 128), lambda _: (0, 0, 0, 0))
-    sums = pl.BlockSpec((frames, 128, 128), lambda _: (0, 0, 0))
-    owned = (32, frames, 8, 128)
+    sums = pl.BlockSpec((frames, 256, 128), lambda _: (0, 0, 0))
+    owned = (32, frames, 16, 128)
     scratch = [
         pltpu.VMEM((16 * ROWS, 128), jnp.float32),
         pltpu.VMEM((16 * ROWS, 128), jnp.float32),
@@ -178,12 +169,12 @@
         grid=(1,),
         out_shape=jax.ShapeDtypeStruct(owned, LINK)
         if last
-        else jax.ShapeDtypeStruct((frames, 128, 128), jnp.float32),
+        else jax.ShapeDtypeStruct((frames, 256, 128), jnp.float32),
         in_specs=[sums] * more + [data] * number,
         out_specs=pl.BlockSpec(owned, lambda _: (0, 0, 0, 0)) if last else sums,
-        scratch_shapes=scratch + [pltpu.VMEM((frames, 128, 128), jnp.float32)] * last,
+        scratch_shapes=scratch + [pltpu.VMEM((frames, 256, 128), jnp.float32)] * last,
         cost_estimate=pl.CostEstimate(
-            flops=work * 128 * 128 * 2, bytes_accessed=work * 18, transcendentals=0
+            flops=work * 256 * 128 * 2, bytes_accessed=work * 18, transcendentals=0
         ),
         name="last" if last else f"nearby{int(more)}",
     )(*([before] * more), *blocks)
@@ -193,12 +184,10 @@
     frames = FRAMES
     d[frames:, :, :] = jnp.zeros((LAGS, 8, 128), jnp.float32)
     e[frames:, :, :] = jnp.zeros((LAGS, 8, 128), jnp.float32)
-    lower = lax.broadcasted_iota(jnp.int32, (8, 128), 0) < 4
 
     def split(t, carry):
-        even, odd = (series[side, t].astype(jnp.float32) for side in range(2))
-        real = jnp.where(lower, odd, pltpu.roll(even, 4, 0))
-        imag = pltpu.roll(jnp.where(lower, pltpu.roll(odd, 4, 0), even), 64, 1)
+        values = series[0, t].astype(jnp.float32) + series[1, t].astype(jnp.float32)
+        real, imag = values[:8], pltpu.roll(values[8:], 64, 1)
         d[t] = real - imag
         e[t] = real + imag
         return carry
@@ -231,7 +220,7 @@
     group = lax.broadcasted_iota(jnp.int32, (LAGS, 128), 1) // 32
 
     def wave(w):
-        return rows[pl.ds(4 * (w % 2) + w // 2, LAGS, stride=8), :]
+        return rows[pl.ds(w, LAGS, stride=8), :]
 
     for half in range(2):
         totals = [jnp.zeros((LAGS, 128), jnp.float32) for _ in range(4)]
@@ -262,8 +251,8 @@
     )(series)
 
 
-def shift(block, by):
-    return lax.ppermute(block, "atom", [(i, (i + by) % 8) for i in range(8)])
+def across(block):
+    return lax.ppermute(block, "atom", [(i, i ^ 2) for i in range(8)])
 
 
 def swap(block):
@@ -275,7 +264,7 @@
     series = lax.all_to_all(
         local, ("atom", "tm"), 0, 0, tiled=True, axis_index_groups=groups
     )
-    return series.reshape(2, FRAMES, 8, 128)
+    return series.reshape(2, FRAMES, 16, 128)
 
 
 def per_device(positions, velocity):
@@ -284,13 +273,10 @@
     high = (positions - low) >> 9
     parts = jnp.stack([high, low], 2).reshape(frames, 6, 16, 128).astype(jnp.bfloat16)
     own = jnp.concatenate([parts, velocity.reshape(frames, 3, 16, 128)], 1)
-    left, right, across = shift(own, 2), shift(own, 6), shift(own, 4)
+    other = across(own)
     sums = modes([own, swap(own)])
-    left, right, sums = lax.optimization_barrier((left, right, sums))
-    far = [swap(left), swap(right)]
-    sums = modes([left, right], sums)
-    across, sums, *far = lax.optimization_barrier((across, sums, *far))
-    return correlate(exchange(modes(far + [across, swap(across)], sums, True)))
+    other, sums = lax.optimization_barrier((other, sums))
+    return correlate(exchange(modes([other, swap(other)], sums, True)))
 
 
 def solution(mesh):

time: 71.8 us -> 60.1 us (0.84)
  Pallas kernels: 30.8 us -> 23.5 us
  blocking collectives: 21.4 us -> 28.1 us
  waiting for transfers between devices: 7.63 us -> 1.21 us
  starting transfers between devices: 7.79 us -> 3.16 us
    pallas_call x3 -> x2, Pallas kernels: 26.1 us -> 18.6 us  [modes(): pl.pallas_call(functools.partial(modes_kernel, number, frames, more, last...]
    all_to_all x1, blocking collectives: 21.4 us -> 28.1 us  [exchange(): lax.all_to_all(local, ('atom', 'tm'), 0, 0, tiled=True, axis_index_groups...]
    ppermute x3 -> x1, waiting for transfers between devices: 6.42 us -> 0.01 us  [across(): return lax.ppermute(block, 'atom', [(i, i ^ 2) for i in range(8)])]
    ppermute x3 -> x1, starting transfers between devices: 4.32 us -> 1.32 us  [across(): return lax.ppermute(block, 'atom', [(i, i ^ 2) for i in range(8)])]
    ppermute x4 -> x2, starting transfers between devices: 3.47 us -> 1.83 us  [swap(): return lax.ppermute(block, 'atom', [(i, i ^ 1) for i in range(8)])]
    unnamed x19 -> x11, local copies, waits for them, and re-layouts: 2.34 us -> 2.32 us
  transfers between devices with their start and end apart: 7 -> 3, of which waited for: 3 -> 1; matrix products, arithmetic and copies ran while one was open for 0% -> 0% of each run, Pallas kernels for 19% -> 15%
where the time goes in v5:
time: 60.1 us; the launch traced here: 59.8 us
  blocking collectives  28.1 us (47%)
  Pallas kernels  23.5 us (39%)
  starting transfers between devices  3.16 us (5%)
  local copies, waits for them, and re-layouts  2.68 us (4%)
  waiting for transfers between devices  1.21 us (2%)
  other arithmetic  1 us (2%)
    all_to_all x1, blocking collectives, exchange(): lax.all_to_all(local, ('atom', 'tm'), 0, 0, tiled=True, axis_index_groups...  28.1 us
    pallas_call x2, Pallas kernels, modes(): pl.pallas_call(functools.partial(modes_kernel, number, frames, more, last...  18.6 us
    pallas_call x1, Pallas kernels, correlate(): pl.pallas_call(correlate_kernel, out_shape=jax.ShapeDtypeStruct((4, LAGS,...  4.96 us
    unnamed x11, local copies, waits for them, and re-layouts  2.32 us
    ppermute x2, starting transfers between devices, swap(): return lax.ppermute(block, 'atom', [(i, i ^ 1) for i in range(8)])  1.83 us
    ppermute x1, starting transfers between devices, across(): return lax.ppermute(block, 'atom', [(i, i ^ 2) for i in range(8)])  1.32 us
    ppermute x2, waiting for transfers between devices, swap(): return lax.ppermute(block, 'atom', [(i, i ^ 1) for i in range(8)])  1.21 us
  transfers between devices with their start and end apart: 3, of which 1 were waited for; matrix products, arithmetic and copies ran while one was open for 0% of the time, Pallas kernels for 15%

profile of v5, /device:TPU:1, one launch (start us, length us, event | category | flops | bytes accessed | tf_op | source)
XLA Modules:
  0.0 59.8 jit_solution(12351296067864615478)
XLA Ops:
  0.0 1.0 %fusion.2 = (bf16[8,3,1,2048]{3,0,1,2:T(8,128)(2,1)S(1)}, bf16[8,3,1,2048]{3,0,1,2:T(8,128)(2,1)S(1)}) fusion(s32[8,3,2048]{2,0,1:T(8,128)} %param.2), kind=kLoop, calls=%fused_computation.5 | loop fusion | flops 344064 | bytes 393216 | tf_op jit(solution)/shard_map/stack | solution.py:274
  1.0 0.2 copy.5
  1.2 0.1 convert_element_type.4
  1.4 0.0 copy-start.1
  1.4 0.9 %copy-done.1 = bf16[8,3,2048]{2,0,1:T(8,128)(2,1)S(1)} copy-done((bf16[8,3,2048]{2,0,1:T(8,128)(2,1)S(1)}, bf16[8,3,2048]{2,0,1:T(8,128)(2,1)}, u32[]{:S(2)}) %copy-start.1) | copy-done | bytes 98328
  2.3 0.0 copy-start
  2.3 1.5 %collective-permute-start.1 = (bf16[8,9,16,128]{3,2,1,0:T(8,128)(2,1)S(1)}, bf16[8,9,16,128]{3,2,1,0:T(8,128)(2,1)S(1)}, u32[]{:S(2)}, u32[]{:S(2)}) collective-permute-start(bf16[8,9,16,128]{3,2,1,0:T(8,128)(2,1)S(1)} %copy_dynamic-update-slice_fusion.refs_0_), channel_id=1, source_target_pairs={{0,16},{16,0},{32,48},{48,32},{64,80},{80,64},{96,112},{112,96},{1... | collective-permute-start | bytes 884744 | tf_op jit(solution)/shard_map/ppermute | solution.py:259
  3.8 1.3 %collective-permute-start = (bf16[8,9,16,128]{3,2,1,0:T(8,128)(2,1)S(1)}, bf16[8,9,16,128]{3,2,1,0:T(8,128)(2,1)S(1)}, u32[]{:S(2)}, u32[]{:S(2)}) collective-permute-start(bf16[8,9,16,128]{3,2,1,0:T(8,128)(2,1)S(1)} %copy_dynamic-update-slice_fusion.refs_0_), channel_id=1, source_target_pairs={{0,32},{16,48},{32,0},{48,16},{64,96},{80,112},{96,64},{112,80},{1... | collective-permute-start | bytes 884744 | tf_op jit(solution)/shard_map/ppermute | solution.py:255
  5.1 0.0 collective-permute-done.1.refs_1_
  5.1 0.0 copy-done
  5.1 0.0 copy-start.3
  5.1 0.7 %copy-done.3 = bf16[8,9,16,128]{3,2,1,0:T(8,128)(2,1)} copy-done((bf16[8,9,16,128]{3,2,1,0:T(8,128)(2,1)}, bf16[8,9,16,128]{3,2,1,0:T(8,128)(2,1)S(1)}, u32[]{:S(2)}) %copy-start.3) | copy-done | bytes 294936
  5.8 9.0 %nearby0.1.refs_0_ = f32[8,256,128]{2,1,0:T(8,128)} custom-call(bf16[8,9,16,128]{3,2,1,0:T(8,128)(2,1)} %copy-done, bf16[8,9,16,128]{3,2,1,0:T(8,128)(2,1)} %copy-done.3), custom_call_target="tpu_custom_call" | custom-call | flops 2147483648 | bytes 589824 | tf_op jit(solution)/shard_map/nearby0/pallas_call | solution.py:167
  14.8 0.0 collective-permute-done.refs_1_
  14.8 0.0 copy-start.2
  14.8 0.4 collective-permute-start.2
  15.2 1.2 %collective-permute-done.2.refs_2_ = bf16[8,9,16,128]{3,2,1,0:T(8,128)(2,1)S(1)} collective-permute-done((bf16[8,9,16,128]{3,2,1,0:T(8,128)(2,1)S(1)}, bf16[8,9,16,128]{3,2,1,0:T(8,128)(2,1)S(1)}, u32[]{:S(2)}, u32[]{:S(2)}) %collective-permute-start.2) | collective-permute-done | bytes 294944 | tf_op jit(solution)/shard_map/ppermute | solution.py:259
  16.4 0.0 copy-done.2
  16.4 0.0 copy-start.4
  16.4 0.7 %copy-done.4 = bf16[8,9,16,128]{3,2,1,0:T(8,128)(2,1)} copy-done((bf16[8,9,16,128]{3,2,1,0:T(8,128)(2,1)}, bf16[8,9,16,128]{3,2,1,0:T(8,128)(2,1)S(1)}, u32[]{:S(2)}) %copy-start.4) | copy-done | bytes 294936
  17.1 9.6 %last.1 = bf16[32,8,16,128]{3,2,1,0:T(8,128)(2,1)} custom-call(f32[8,256,128]{2,1,0:T(8,128)} %nearby0.1.refs_0_, bf16[8,9,16,128]{3,2,1,0:T(8,128)(2,1)} %copy-done.2, bf16[8,9,16,128]{3,2,1,0:T(8,128)(2,1)} %copy-done.4), custom_call_target="tpu_custom_call" | custom-call | flops 2147483648 | bytes 589824 | tf_op jit(solution)/shard_map/last/pallas_call | solution.py:167
  26.7 28.1 %all_to_all.5 = bf16[32,8,16,128]{3,2,1,0:T(8,128)(2,1)} all-to-all(bf16[32,8,16,128]{3,2,1,0:T(8,128)(2,1)} %last.1), channel_id=1, replica_groups={{0,1,2,3,4,5,6,7,8,9,10,11,12,13,14,15,112,113,114,115,116,117,118,119,..., dimensions={0} | all-to-all | bytes 2097152 | tf_op jit(solution)/shard_map/all_to_all | solution.py:264
  54.8 5.0 %correlate.1 = f32[4,16,256]{2,1,0:T(8,128)} custom-call(bf16[2,128,16,128]{3,2,1,0:T(8,128)(2,1)} %bitcast.13), custom_call_target="tpu_custom_call" | custom-call | tf_op jit(solution)/shard_map/correlate/pallas_call | solution.py:240
  (3 shorter events, 0.1 us)
Async XLA Ops:
  1.4 0.9 %copy-start.1 = (bf16[8,3,2048]{2,0,1:T(8,128)(2,1)S(1)}, bf16[8,3,2048]{2,0,1:T(8,128)(2,1)}, u32[]{:S(2)}) copy-start(bf16[8,3,2048]{2,0,1:T(8,128)(2,1)} %param.3) | copy-start | bytes 294916
  2.3 2.8 %copy-start = (bf16[8,9,16,128]{3,2,1,0:T(8,128)(2,1)}, bf16[8,9,16,128]{3,2,1,0:T(8,128)(2,1)S(1)}, u32[]{:S(2)}) copy-start(bf16[8,9,16,128]{3,2,1,0:T(8,128)(2,1)S(1)} %copy_dynamic-update-slice_fusion.refs_0_) | copy-start | bytes 884740
  2.3 2.8 %collective-permute-start.1 = (bf16[8,9,16,128]{3,2,1,0:T(8,128)(2,1)S(1)}, bf16[8,9,16,128]{3,2,1,0:T(8,128)(2,1)S(1)}, u32[]{:S(2)}, u32[]{:S(2)}) collective-permute-start(bf16[8,9,16,128]{3,2,1,0:T(8,128)(2,1)S(1)} %copy_dynamic-update-slice_fusion.refs_0_), channel_id=1, source_target_pairs={{0,16},{16,0},{32,48},{48,32},{64,80},{80,64},{96,112},{112,96},{1... | collective-permute-start | bytes 884744 | tf_op jit(solution)/shard_map/ppermute | solution.py:259
  3.8 11.1 %collective-permute-start = (bf16[8,9,16,128]{3,2,1,0:T(8,128)(2,1)S(1)}, bf16[8,9,16,128]{3,2,1,0:T(8,128)(2,1)S(1)}, u32[]{:S(2)}, u32[]{:S(2)}) collective-permute-start(bf16[8,9,16,128]{3,2,1,0:T(8,128)(2,1)S(1)} %copy_dynamic-update-slice_fusion.refs_0_), channel_id=1, source_target_pairs={{0,32},{16,48},{32,0},{48,16},{64,96},{80,112},{96,64},{112,80},{1... | collective-permute-start | bytes 884744 | tf_op jit(solution)/shard_map/ppermute | solution.py:255
  5.1 0.7 %copy-start.3 = (bf16[8,9,16,128]{3,2,1,0:T(8,128)(2,1)}, bf16[8,9,16,128]{3,2,1,0:T(8,128)(2,1)S(1)}, u32[]{:S(2)}) copy-start(bf16[8,9,16,128]{3,2,1,0:T(8,128)(2,1)S(1)} %collective-permute-done.1.refs_1_) | copy-start | bytes 884740
  14.8 1.6 %copy-start.2 = (bf16[8,9,16,128]{3,2,1,0:T(8,128)(2,1)}, bf16[8,9,16,128]{3,2,1,0:T(8,128)(2,1)S(1)}, u32[]{:S(2)}) copy-start(bf16[8,9,16,128]{3,2,1,0:T(8,128)(2,1)S(1)} %collective-permute-done.refs_1_) | copy-start | bytes 884740
  14.8 1.6 %collective-permute-start.2 = (bf16[8,9,16,128]{3,2,1,0:T(8,128)(2,1)S(1)}, bf16[8,9,16,128]{3,2,1,0:T(8,128)(2,1)S(1)}, u32[]{:S(2)}, u32[]{:S(2)}) collective-permute-start(bf16[8,9,16,128]{3,2,1,0:T(8,128)(2,1)S(1)} %collective-permute-done.refs_1_), channel_id=1, source_target_pairs={{0,16},{16,0},{32,48},{48,32},{64,80},{80,64},{96,112},{112,96},{1... | collective-permute-start | bytes 884744 | tf_op jit(solution)/shard_map/ppermute | solution.py:259
  16.4 0.7 %copy-start.4 = (bf16[8,9,16,128]{3,2,1,0:T(8,128)(2,1)}, bf16[8,9,16,128]{3,2,1,0:T(8,128)(2,1)S(1)}, u32[]{:S(2)}) copy-start(bf16[8,9,16,128]{3,2,1,0:T(8,128)(2,1)S(1)} %collective-permute-done.2.refs_2_) | copy-start | bytes 884740

commit v6 on v5

--- a/solution.py
+++ b/solution.py
@@ -17,6 +17,8 @@
 FRAMES = 128
 HALF = 16
 LINK = jnp.bfloat16
+WIDTH = 2
+GRANT = 16 << 20
 ROWS = 75
 SINE = (6.28318516, -41.3416550, 81.6010040, -76.5498338, 39.5367090)
 
@@ -73,8 +75,8 @@
 
 
 def multiply(table, total):
-    for pair in range(8):
-        bases = [(2 * pair + k) * ROWS for k in range(2)]
+    for start in range(0, 16, WIDTH):
+        bases = [(start + k) * ROWS for k in range(WIDTH)]
 
         def rows(start, number):
             return [table[pl.ds(base + start, number), :] for base in bases]
@@ -89,7 +91,7 @@
             cx, sx = rows(2 * i, 1), rows(2 * i + 1, 1)
             for b in range(2):
                 plus, minus = [], []
-                for k in range(2):
+                for k in range(WIDTH):
                     cc, sn = cx[k] * yc[b][k], sx[k] * ys[b][k]
                     cn, sc = cx[k] * ys[b][k], sx[k] * yc[b][k]
                     plus.append(jnp.concatenate([cc - sn, cn + sc], 0))
@@ -101,7 +103,7 @@
             right.append(wide(z))
             for comp in range(3):
                 u = rows(72 + comp, 1)
-                right.append(wide([z[k] * u[k] for k in range(2)]))
+                right.append(wide([z[k] * u[k] for k in range(WIDTH)]))
         total = total + lax.dot_general(
             jnp.concatenate(left, 0),
             jnp.concatenate(right, 0),
@@ -112,16 +114,16 @@
 
 
 def modes_kernel(number, frames, more, last, *refs):
+    data, refs = refs[:number], refs[number:]
     if more:
         before, refs = refs[0], refs[1:]
-    data, out = refs[:number], refs[number]
-    table_a, table_b, blocks, *rest = refs[number + 1 :]
+    out, table_a, table_b, blocks, *rest = refs
     totals = rest[0] if last else out
     first = (4 * place()[0] - 15).astype(jnp.float32)
     steps = number * frames
     for g in range(number):
         for f in range(frames):
-            blocks[f * number + g] = data[g][f]
+            blocks[g * frames + f] = data[g][f]
 
     def block(index):
         return [blocks[index, k] for k in range(9)]
@@ -131,11 +133,11 @@
 
     def step(half, carry):
         now = 2 * half
-        frame = now // number
+        frame = now % frames
         fill(block(now + 1), first, table_b)
-        total = multiply(table_a, totals[frame])
+        totals[frame] = multiply(table_a, totals[frame])
         fill(block(jnp.minimum(now + 2, steps - 1)), first, table_a)
-        totals[frame] = multiply(table_b, total)
+        totals[frame + 1] = multiply(table_b, totals[frame + 1])
         return carry
 
     lax.fori_loop(0, steps // 2, step, 0)
@@ -155,29 +157,29 @@
 def modes(blocks, before=None, last=False):
     frames = blocks[0].shape[0]
     number, more = len(blocks), before is not None
-    data = pl.BlockSpec((frames, 9, 16, 128), lambda _: (0, 0, 0, 0))
-    sums = pl.BlockSpec((frames, 256, 128), lambda _: (0, 0, 0))
-    owned = (32, frames, 16, 128)
-    scratch = [
-        pltpu.VMEM((16 * ROWS, 128), jnp.float32),
-        pltpu.VMEM((16 * ROWS, 128), jnp.float32),
-        pltpu.VMEM((number * frames, 9, 16, 128), jnp.bfloat16),
-    ]
+    vmem = pl.BlockSpec(memory_space=pltpu.VMEM)
+    sums = (frames, 256, 128)
     work = number * frames * 2048
     return pl.pallas_call(
         functools.partial(modes_kernel, number, frames, more, last),
-        grid=(1,),
-        out_shape=jax.ShapeDtypeStruct(owned, LINK)
+        out_shape=jax.ShapeDtypeStruct((32, frames, 16, 128), LINK)
         if last
-        else jax.ShapeDtypeStruct((frames, 256, 128), jnp.float32),
-        in_specs=[sums] * more + [data] * number,
-        out_specs=pl.BlockSpec(owned, lambda _: (0, 0, 0, 0)) if last else sums,
-        scratch_shapes=scratch + [pltpu.VMEM((frames, 256, 128), jnp.float32)] * last,
+        else jax.ShapeDtypeStruct(sums, jnp.float32),
+        in_specs=[vmem] * (number + more),
+        out_specs=vmem,
+        scratch_shapes=[
+            pltpu.VMEM((16 * ROWS, 128), jnp.float32),
+            pltpu.VMEM((16 * ROWS, 128), jnp.float32),
+            pltpu.VMEM((number * frames, 9, 16, 128), jnp.bfloat16),
+        ]
+        + [pltpu.VMEM(sums, jnp.float32)] * last,
+        input_output_aliases={number: 0} if more and not last else {},
         cost_estimate=pl.CostEstimate(
             flops=work * 256 * 128 * 2, bytes_accessed=work * 18, transcendentals=0
         ),
+        compiler_params=pltpu.CompilerParams(vmem_limit_bytes=GRANT),
         name="last" if last else f"nearby{int(more)}",
-    )(*([before] * more), *blocks)
+    )(*blocks, *([before] * more))
 
 
 def correlate_kernel(series, out, d, e, rows):
@@ -247,6 +249,7 @@
             pltpu.VMEM((FRAMES + LAGS, 8, 128), jnp.float32),
             pltpu.VMEM((128, 128), jnp.float32),
         ],
+        compiler_params=pltpu.CompilerParams(vmem_limit_bytes=GRANT),
         name="correlate",
     )(series)
 
@@ -276,7 +279,9 @@
     other = across(own)
     sums = modes([own, swap(own)])
     other, sums = lax.optimization_barrier((other, sums))
-    return correlate(exchange(modes([other, swap(other)], sums, True)))
+    behind = swap(other)
+    sums = modes([other], sums)
+    return correlate(exchange(modes([behind], sums, True)))
 
 
 def solution(mesh):

time: 60.1 us -> 52.4 us (0.87)
  Pallas kernels: 23.5 us -> 18.1 us
  local copies, waits for them, and re-layouts: 2.68 us -> 1.24 us
  waiting for transfers between devices: 1.21 us -> 0.14 us
    pallas_call x2 -> x3, Pallas kernels: 18.6 us -> 14.4 us  [modes(): pl.pallas_call(functools.partial(modes_kernel, number, frames, more, last...]
    unnamed x11 -> x3, local copies, waits for them, and re-layouts: 2.32 us -> 0.88 us
    pallas_call x1, Pallas kernels: 4.96 us -> 3.74 us  [correlate(): pl.pallas_call(correlate_kernel, out_shape=jax.ShapeDtypeStruct((4, LAGS,...]
    ppermute x2, waiting for transfers between devices: 1.21 us -> 0.01 us  [swap(): return lax.ppermute(block, 'atom', [(i, i ^ 1) for i in range(8)])]
  transfers between devices with their start and end apart: 3 -> 3, of which waited for: 1 -> 1; matrix products, arithmetic and copies ran while one was open for 0% -> 0% of each run, Pallas kernels for 15% -> 20%
where the time goes in v6:
time: 52.4 us; the launch traced here: 52.2 us
  blocking collectives  27.9 us (53%)
  Pallas kernels  18.1 us (35%)
  starting transfers between devices  3.73 us (7%)
  local copies, waits for them, and re-layouts  1.24 us (2%)
  other arithmetic  1 us (2%)
    all_to_all x1, blocking collectives, exchange(): lax.all_to_all(local, ('atom', 'tm'), 0, 0, tiled=True, axis_index_groups...  27.9 us
    pallas_call x3, Pallas kernels, modes(): pl.pallas_call(functools.partial(modes_kernel, number, frames, more, last...  14.4 us
    pallas_call x1, Pallas kernels, correlate(): pl.pallas_call(correlate_kernel, out_shape=jax.ShapeDtypeStruct((4, LAGS,...  3.74 us
    ppermute x2, starting transfers between devices, swap(): return lax.ppermute(block, 'atom', [(i, i ^ 1) for i in range(8)])  2.41 us
    ppermute x1, starting transfers between devices, across(): return lax.ppermute(block, 'atom', [(i, i ^ 2) for i in range(8)])  1.32 us
  transfers between devices with their start and end apart: 3, of which 1 were waited for; matrix products, arithmetic and copies ran while one was open for 0% of the time, Pallas kernels for 20%

profile of v6, /device:TPU:1, one launch (start us, length us, event | category | flops | bytes accessed | tf_op | source)
XLA Modules:
  0.0 52.2 jit_solution(2958288425432593397)
XLA Ops:
  0.0 1.0 %fusion.2 = (bf16[8,3,1,2048]{3,0,1,2:T(8,128)(2,1)S(1)}, bf16[8,3,1,2048]{3,0,1,2:T(8,128)(2,1)S(1)}) fusion(s32[8,3,2048]{2,0,1:T(8,128)} %param.2), kind=kLoop, calls=%fused_computation.5 | loop fusion | flops 344064 | bytes 393216 | tf_op jit(solution)/shard_map/stack | solution.py:277
  1.0 0.2 copy.6
  1.2 0.1 convert_element_type.4
  1.4 0.0 copy-start
  1.4 0.9 %copy-done = bf16[8,3,2048]{2,0,1:T(8,128)(2,1)S(1)} copy-done((bf16[8,3,2048]{2,0,1:T(8,128)(2,1)S(1)}, bf16[8,3,2048]{2,0,1:T(8,128)(2,1)}, u32[]{:S(2)}) %copy-start) | copy-done | bytes 98328
  2.3 1.5 %collective-permute-start.1 = (bf16[8,9,16,128]{3,2,1,0:T(8,128)(2,1)S(1)}, bf16[8,9,16,128]{3,2,1,0:T(8,128)(2,1)S(1)}, u32[]{:S(2)}, u32[]{:S(2)}) collective-permute-start(bf16[8,9,16,128]{3,2,1,0:T(8,128)(2,1)S(1)} %copy_dynamic-update-slice_fusion.refs_0_), channel_id=1, source_target_pairs={{0,16},{16,0},{32,48},{48,32},{64,80},{80,64},{96,112},{112,96},{1... | collective-permute-start | bytes 884744 | tf_op jit(solution)/shard_map/ppermute | solution.py:262
  3.7 1.3 %collective-permute-start = (bf16[8,9,16,128]{3,2,1,0:T(8,128)(2,1)S(1)}, bf16[8,9,16,128]{3,2,1,0:T(8,128)(2,1)S(1)}, u32[]{:S(2)}, u32[]{:S(2)}) collective-permute-start(bf16[8,9,16,128]{3,2,1,0:T(8,128)(2,1)S(1)} %copy_dynamic-update-slice_fusion.refs_0_), channel_id=1, source_target_pairs={{0,32},{16,48},{32,0},{48,16},{64,96},{80,112},{96,64},{112,80},{1... | collective-permute-start | bytes 884744 | tf_op jit(solution)/shard_map/ppermute | solution.py:258
  5.1 0.0 collective-permute-done.1.refs_1_
  5.1 7.0 %nearby0.1.refs_1_ = f32[8,256,128]{2,1,0:T(8,128)S(1)} custom-call(bf16[8,9,16,128]{3,2,1,0:T(8,128)(2,1)S(1)} %copy_dynamic-update-slice_fusion.refs_0_, bf16[8,9,16,128]{3,2,1,0:T(8,128)(2,1)S(1)} %collective-permute-done.1.refs_1_), custom_call_target="tpu_custom_call" | custom-call | flops 2147483648 | bytes 589824 | tf_op jit(solution)/shard_map/nearby0/pallas_call | solution.py:163
  12.1 0.1 collective-permute-done.refs_0_
  12.2 0.9 %collective-permute-start.2 = (bf16[8,9,16,128]{3,2,1,0:T(8,128)(2,1)S(1)}, bf16[8,9,16,128]{3,2,1,0:T(8,128)(2,1)S(1)}, u32[]{:S(2)}, u32[]{:S(2)}) collective-permute-start(bf16[8,9,16,128]{3,2,1,0:T(8,128)(2,1)S(1)} %collective-permute-done.refs_0_), channel_id=1, source_target_pairs={{0,16},{16,0},{32,48},{48,32},{64,80},{80,64},{96,112},{112,96},{1... | collective-permute-start | bytes 884744 | tf_op jit(solution)/shard_map/ppermute | solution.py:262
  13.2 3.6 %nearby1.1.refs_1_ = f32[8,256,128]{2,1,0:T(8,128)S(1)} custom-call(bf16[8,9,16,128]{3,2,1,0:T(8,128)(2,1)S(1)} %collective-permute-done.refs_0_, f32[8,256,128]{2,1,0:T(8,128)S(1)} %nearby0.1.refs_1_), custom_call_target="tpu_custom_call", output_to_operand_aliasing={{}: (1, {})} | custom-call | flops 1073741824 | bytes 294912 | tf_op jit(solution)/shard_map/nearby1/pallas_call | solution.py:163
  16.8 0.0 collective-permute-done.2.refs_0_
  16.8 3.7 %last.1 = bf16[32,8,16,128]{3,2,1,0:T(8,128)(2,1)S(1)} custom-call(bf16[8,9,16,128]{3,2,1,0:T(8,128)(2,1)S(1)} %collective-permute-done.2.refs_0_, f32[8,256,128]{2,1,0:T(8,128)S(1)} %nearby1.1.refs_1_), custom_call_target="tpu_custom_call" | custom-call | flops 1073741824 | bytes 294912 | tf_op jit(solution)/shard_map/last/pallas_call | solution.py:163
  20.6 27.9 %all_to_all.5 = bf16[32,8,16,128]{3,2,1,0:T(8,128)(2,1)S(1)} all-to-all(bf16[32,8,16,128]{3,2,1,0:T(8,128)(2,1)S(1)} %last.1), channel_id=1, replica_groups={{0,1,2,3,4,5,6,7,8,9,10,11,12,13,14,15,112,113,114,115,116,117,118,119,..., dimensions={0} | all-to-all | bytes 2097152 | tf_op jit(solution)/shard_map/all_to_all | solution.py:267
  48.4 3.7 %correlate.1 = f32[4,16,256]{2,1,0:T(8,128)} custom-call(bf16[2,128,16,128]{3,2,1,0:T(8,128)(2,1)S(1)} %bitcast.13), custom_call_target="tpu_custom_call" | custom-call | tf_op jit(solution)/shard_map/correlate/pallas_call | solution.py:242
  (3 shorter events, 0.1 us)
Async XLA Ops:
  1.4 0.9 %copy-start = (bf16[8,3,2048]{2,0,1:T(8,128)(2,1)S(1)}, bf16[8,3,2048]{2,0,1:T(8,128)(2,1)}, u32[]{:S(2)}) copy-start(bf16[8,3,2048]{2,0,1:T(8,128)(2,1)} %param.3) | copy-start | bytes 294916
  2.3 2.8 %collective-permute-start.1 = (bf16[8,9,16,128]{3,2,1,0:T(8,128)(2,1)S(1)}, bf16[8,9,16,128]{3,2,1,0:T(8,128)(2,1)S(1)}, u32[]{:S(2)}, u32[]{:S(2)}) collective-permute-start(bf16[8,9,16,128]{3,2,1,0:T(8,128)(2,1)S(1)} %copy_dynamic-update-slice_fusion.refs_0_), channel_id=1, source_target_pairs={{0,16},{16,0},{32,48},{48,32},{64,80},{80,64},{96,112},{112,96},{1... | collective-permute-start | bytes 884744 | tf_op jit(solution)/shard_map/ppermute | solution.py:262
  3.7 8.5 %collective-permute-start = (bf16[8,9,16,128]{3,2,1,0:T(8,128)(2,1)S(1)}, bf16[8,9,16,128]{3,2,1,0:T(8,128)(2,1)S(1)}, u32[]{:S(2)}, u32[]{:S(2)}) collective-permute-start(bf16[8,9,16,128]{3,2,1,0:T(8,128)(2,1)S(1)} %copy_dynamic-update-slice_fusion.refs_0_), channel_id=1, source_target_pairs={{0,32},{16,48},{32,0},{48,16},{64,96},{80,112},{96,64},{112,80},{1... | collective-permute-start | bytes 884744 | tf_op jit(solution)/shard_map/ppermute | solution.py:258
  12.2 4.6 %collective-permute-start.2 = (bf16[8,9,16,128]{3,2,1,0:T(8,128)(2,1)S(1)}, bf16[8,9,16,128]{3,2,1,0:T(8,128)(2,1)S(1)}, u32[]{:S(2)}, u32[]{:S(2)}) collective-permute-start(bf16[8,9,16,128]{3,2,1,0:T(8,128)(2,1)S(1)} %collective-permute-done.refs_0_), channel_id=1, source_target_pairs={{0,16},{16,0},{32,48},{48,32},{64,80},{80,64},{96,112},{112,96},{1... | collective-permute-start | bytes 884744 | tf_op jit(solution)/shard_map/ppermute | solution.py:262

commit v7 on v6

--- a/solution.py
+++ b/solution.py
@@ -18,6 +18,7 @@
 HALF = 16
 LINK = jnp.bfloat16
 WIDTH = 2
+SPREAD = 136
 GRANT = 16 << 20
 ROWS = 75
 SINE = (6.28318516, -41.3416550, 81.6010040, -76.5498338, 39.5367090)
@@ -72,6 +73,55 @@
         put(row, harmonics(c1, jnp.ones_like(c1), c1 + c1, HALF))
         put(row + HALF, harmonics(s1, jnp.zeros_like(s1), c1 + c1, HALF))
     put(72, [data[6 + comp].astype(jnp.float32) for comp in range(3)])
+
+
+def prepare_kernel(far_positions, far_velocity, out, positions, velocity, spread, sem):
+    frames = positions.shape[1]
+    copies = [
+        pltpu.make_async_copy(far_positions, positions, sem.at[0]),
+        pltpu.make_async_copy(far_velocity, velocity, sem.at[1]),
+    ]
+    for copy in copies:
+        copy.start()
+    for copy in copies:
+        copy.wait()
+    for g in range(16):
+        lanes = slice(g * 128, (g + 1) * 128)
+        for a in range(3):
+            whole = positions[a, :, lanes]
+            low = ((whole + 256) & 511) - 256
+            high = (whole - low) >> 9
+            parts = (high, low, velocity[a, :, lanes])
+            for k, part in zip((2 * a, 2 * a + 1, 6 + a), parts):
+                spread[pl.ds(k * SPREAD + g, frames, stride=17), :] = part.astype(jnp.float32)
+    for f in range(frames):
+        for k in range(9):
+            at = k * SPREAD + 17 * f
+            out[f, k] = spread[at : at + 16, :].astype(jnp.bfloat16)
+
+
+def prepare(positions, velocity):
+    frames = positions.shape[0]
+    vmem = pl.BlockSpec(memory_space=pltpu.VMEM)
+    return pl.pallas_call(
+        prepare_kernel,
+        out_shape=jax.ShapeDtypeStruct((frames, 9, 16, 128), jnp.bfloat16),
+        in_specs=[pl.BlockSpec(memory_space=pltpu.HBM)] * 2,
+        out_specs=vmem,
+        scratch_shapes=[
+            pltpu.VMEM((3, frames, 2048), jnp.int32),
+            pltpu.VMEM((3, frames, 2048), jnp.bfloat16),
+            pltpu.VMEM((9 * SPREAD, 128), jnp.float32),
+            pltpu.SemaphoreType.DMA((2,)),
+        ],
+        compiler_params=pltpu.CompilerParams(vmem_limit_bytes=GRANT),
+        name="prepare",
+    )(
+        *(
+            pltpu.with_memory_space_constraint(jnp.transpose(x, (1, 0, 2)), pltpu.HBM)
+            for x in (positions, velocity)
+        )
+    )
 
 
 def multiply(table, total):
@@ -196,15 +246,14 @@
 
     lax.fori_loop(0, frames, split, 0, unroll=8)
 
-    def lags(source):
-        def step(t, sums):
-            here = source[t]
-            return tuple(sums[lag] + here * source[t + lag] for lag in range(LAGS))
-
-        zero = jnp.zeros((8, 128), jnp.float32)
-        return lax.fori_loop(0, frames, step, (zero,) * LAGS, unroll=4)
-
-    sums_d, sums_e = lags(d), lags(e)
+    def step(t, sums):
+        return tuple(
+            tuple(part[lag] + source[t] * source[t + lag] for lag in range(LAGS))
+            for part, source in zip(sums, (d, e))
+        )
+
+    zero = (jnp.zeros((8, 128), jnp.float32),) * LAGS
+    sums_d, sums_e = lax.fori_loop(0, frames, step, (zero, zero), unroll=8)
     for lag in range(LAGS):
         value = (sums_d[lag] + pltpu.roll(sums_e[lag], 64, 1)) * (1.0 / (ATOMS * (frames - lag)))
         rows[lag * 8 : lag * 8 + 8, :] = value
@@ -214,10 +263,7 @@
     comp, q = (lane // 32) * 16, lane % 32
     falling, rising = comp + 15 - q, comp + q - 16
     source = jnp.where(q < 16, 64 * upper + falling, 64 * (1 - upper) + rising)
-    pick = (lax.broadcasted_iota(jnp.int32, (128, 128), 0) == source).astype(jnp.float32)
-    rows[...] = jnp.dot(
-        rows[...], pick, precision=lax.Precision.HIGHEST, preferred_element_type=jnp.float32
-    )
+    rows[...] = jnp.take_along_axis(rows[...], source, axis=1)
     flip = t % 4 < 2
     group = lax.broadcasted_iota(jnp.int32, (LAGS, 128), 1) // 32
 
@@ -271,11 +317,7 @@
 
 
 def per_device(positions, velocity):
-    frames = positions.shape[0]
-    low = ((positions + 256) & 511) - 256
-    high = (positions - low) >> 9
-    parts = jnp.stack([high, low], 2).reshape(frames, 6, 16, 128).astype(jnp.bfloat16)
-    own = jnp.concatenate([parts, velocity.reshape(frames, 3, 16, 128)], 1)
+    own = prepare(positions, velocity)
     other = across(own)
     sums = modes([own, swap(own)])
     other, sums = lax.optimization_barrier((other, sums))

time: 52.4 us -> 50.9 us (0.971)
  local copies, waits for them, and re-layouts: 1.24 us -> 0 us
  other arithmetic: 1 us -> 0 us
  Pallas kernels: 18.1 us -> 18.9 us
    pallas_call x0 -> x1, Pallas kernels: none -> 1.09 us  [prepare(): pl.pallas_call(prepare_kernel, out_shape=jax.ShapeDtypeStruct((frames, 9,...]
    another operation x2 -> x0, other arithmetic: 1 us -> none  [per_device(): jnp.stack([high, low], 2).reshape(frames, 6, 16, 128).astype(jnp.bfloat16)]
    unnamed x3 -> x0, local copies, waits for them, and re-layouts: 0.88 us -> none
  transfers between devices with their start and end apart: 3 -> 3, of which waited for: 1 -> 1; matrix products, arithmetic and copies ran while one was open for 0% -> 0% of each run, Pallas kernels for 20% -> 21%
where the time goes in v7:
time: 50.9 us; the launch traced here: 50.7 us
  blocking collectives  27.9 us (55%)
  Pallas kernels  18.9 us (37%)
  starting transfers between devices  3.73 us (7%)
    all_to_all x1, blocking collectives, exchange(): lax.all_to_all(local, ('atom', 'tm'), 0, 0, tiled=True, axis_index_groups...  27.9 us
    pallas_call x3, Pallas kernels, modes(): pl.pallas_call(functools.partial(modes_kernel, number, frames, more, last...  14.4 us
    pallas_call x1, Pallas kernels, correlate(): pl.pallas_call(correlate_kernel, out_shape=jax.ShapeDtypeStruct((4, LAGS,...  3.48 us
    ppermute x2, starting transfers between devices, swap(): return lax.ppermute(block, 'atom', [(i, i ^ 1) for i in range(8)])  2.41 us
    ppermute x1, starting transfers between devices, across(): return lax.ppermute(block, 'atom', [(i, i ^ 2) for i in range(8)])  1.32 us
    pallas_call x1, Pallas kernels, prepare(): pl.pallas_call(prepare_kernel, out_shape=jax.ShapeDtypeStruct((frames, 9,...  1.09 us
  transfers between devices with their start and end apart: 3, of which 1 were waited for; matrix products, arithmetic and copies ran while one was open for 0% of the time, Pallas kernels for 21%

profile of v7, /device:TPU:1, one launch (start us, length us, event | category | flops | bytes accessed | tf_op | source)
XLA Modules:
  0.0 50.7 jit_solution(5439307126826191244)
XLA Ops:
  0.0 1.1 %prepare.1.refs_0_ = bf16[8,9,16,128]{3,2,1,0:T(8,128)(2,1)S(1)} custom-call(s32[3,8,2048]{2,1,0:T(8,128)} %bitcast.4, bf16[3,8,2048]{2,1,0:T(8,128)(2,1)} %bitcast.5), custom_call_target="tpu_custom_call" | custom-call | tf_op jit(solution)/shard_map/prepare/pallas_call | solution.py:106
  1.1 1.5 %collective-permute-start.1 = (bf16[8,9,16,128]{3,2,1,0:T(8,128)(2,1)S(1)}, bf16[8,9,16,128]{3,2,1,0:T(8,128)(2,1)S(1)}, u32[]{:S(2)}, u32[]{:S(2)}) collective-permute-start(bf16[8,9,16,128]{3,2,1,0:T(8,128)(2,1)S(1)} %prepare.1.refs_0_), channel_id=1, source_target_pairs={{0,16},{16,0},{32,48},{48,32},{64,80},{80,64},{96,112},{112,96},{1... | collective-permute-start | bytes 884744 | tf_op jit(solution)/shard_map/ppermute | solution.py:308
  2.6 1.3 %collective-permute-start = (bf16[8,9,16,128]{3,2,1,0:T(8,128)(2,1)S(1)}, bf16[8,9,16,128]{3,2,1,0:T(8,128)(2,1)S(1)}, u32[]{:S(2)}, u32[]{:S(2)}) collective-permute-start(bf16[8,9,16,128]{3,2,1,0:T(8,128)(2,1)S(1)} %prepare.1.refs_0_), channel_id=1, source_target_pairs={{0,32},{16,48},{32,0},{48,16},{64,96},{80,112},{96,64},{112,80},{1... | collective-permute-start | bytes 884744 | tf_op jit(solution)/shard_map/ppermute | solution.py:304
  3.9 0.0 collective-permute-done.1.refs_1_
  3.9 7.0 %nearby0.1.refs_1_ = f32[8,256,128]{2,1,0:T(8,128)S(1)} custom-call(bf16[8,9,16,128]{3,2,1,0:T(8,128)(2,1)S(1)} %prepare.1.refs_0_, bf16[8,9,16,128]{3,2,1,0:T(8,128)(2,1)S(1)} %collective-permute-done.1.refs_1_), custom_call_target="tpu_custom_call" | custom-call | flops 2147483648 | bytes 589824 | tf_op jit(solution)/shard_map/nearby0/pallas_call | solution.py:213
  10.9 0.1 collective-permute-done.refs_0_
  11.0 0.9 %collective-permute-start.2 = (bf16[8,9,16,128]{3,2,1,0:T(8,128)(2,1)S(1)}, bf16[8,9,16,128]{3,2,1,0:T(8,128)(2,1)S(1)}, u32[]{:S(2)}, u32[]{:S(2)}) collective-permute-start(bf16[8,9,16,128]{3,2,1,0:T(8,128)(2,1)S(1)} %collective-permute-done.refs_0_), channel_id=1, source_target_pairs={{0,16},{16,0},{32,48},{48,32},{64,80},{80,64},{96,112},{112,96},{1... | collective-permute-start | bytes 884744 | tf_op jit(solution)/shard_map/ppermute | solution.py:308
  12.0 3.6 %nearby1.1.refs_1_ = f32[8,256,128]{2,1,0:T(8,128)S(1)} custom-call(bf16[8,9,16,128]{3,2,1,0:T(8,128)(2,1)S(1)} %collective-permute-done.refs_0_, f32[8,256,128]{2,1,0:T(8,128)S(1)} %nearby0.1.refs_1_), custom_call_target="tpu_custom_call", output_to_operand_aliasing={{}: (1, {})} | custom-call | flops 1073741824 | bytes 294912 | tf_op jit(solution)/shard_map/nearby1/pallas_call | solution.py:213
  15.6 0.0 collective-permute-done.2.refs_0_
  15.7 3.7 %last.1 = bf16[32,8,16,128]{3,2,1,0:T(8,128)(2,1)S(1)} custom-call(bf16[8,9,16,128]{3,2,1,0:T(8,128)(2,1)S(1)} %collective-permute-done.2.refs_0_, f32[8,256,128]{2,1,0:T(8,128)S(1)} %nearby1.1.refs_1_), custom_call_target="tpu_custom_call" | custom-call | flops 1073741824 | bytes 294912 | tf_op jit(solution)/shard_map/last/pallas_call | solution.py:213
  19.4 27.9 %all_to_all.5 = bf16[32,8,16,128]{3,2,1,0:T(8,128)(2,1)S(1)} all-to-all(bf16[32,8,16,128]{3,2,1,0:T(8,128)(2,1)S(1)} %last.1), channel_id=1, replica_groups={{0,1,2,3,4,5,6,7,8,9,10,11,12,13,14,15,112,113,114,115,116,117,118,119,..., dimensions={0} | all-to-all | bytes 2097152 | tf_op jit(solution)/shard_map/all_to_all | solution.py:313
  47.2 3.5 %correlate.1 = f32[4,16,256]{2,1,0:T(8,128)} custom-call(bf16[2,128,16,128]{3,2,1,0:T(8,128)(2,1)S(1)} %bitcast.3), custom_call_target="tpu_custom_call" | custom-call | tf_op jit(solution)/shard_map/correlate/pallas_call | solution.py:288
Async XLA Ops:
  1.1 2.8 %collective-permute-start.1 = (bf16[8,9,16,128]{3,2,1,0:T(8,128)(2,1)S(1)}, bf16[8,9,16,128]{3,2,1,0:T(8,128)(2,1)S(1)}, u32[]{:S(2)}, u32[]{:S(2)}) collective-permute-start(bf16[8,9,16,128]{3,2,1,0:T(8,128)(2,1)S(1)} %prepare.1.refs_0_), channel_id=1, source_target_pairs={{0,16},{16,0},{32,48},{48,32},{64,80},{80,64},{96,112},{112,96},{1... | collective-permute-start | bytes 884744 | tf_op jit(solution)/shard_map/ppermute | solution.py:308
  2.6 8.5 %collective-permute-start = (bf16[8,9,16,128]{3,2,1,0:T(8,128)(2,1)S(1)}, bf16[8,9,16,128]{3,2,1,0:T(8,128)(2,1)S(1)}, u32[]{:S(2)}, u32[]{:S(2)}) collective-permute-start(bf16[8,9,16,128]{3,2,1,0:T(8,128)(2,1)S(1)} %prepare.1.refs_0_), channel_id=1, source_target_pairs={{0,32},{16,48},{32,0},{48,16},{64,96},{80,112},{96,64},{112,80},{1... | collective-permute-start | bytes 884744 | tf_op jit(solution)/shard_map/ppermute | solution.py:304
  11.0 4.6 %collective-permute-start.2 = (bf16[8,9,16,128]{3,2,1,0:T(8,128)(2,1)S(1)}, bf16[8,9,16,128]{3,2,1,0:T(8,128)(2,1)S(1)}, u32[]{:S(2)}, u32[]{:S(2)}) collective-permute-start(bf16[8,9,16,128]{3,2,1,0:T(8,128)(2,1)S(1)} %collective-permute-done.refs_0_), channel_id=1, source_target_pairs={{0,16},{16,0},{32,48},{48,32},{64,80},{80,64},{96,112},{112,96},{1... | collective-permute-start | bytes 884744 | tf_op jit(solution)/shard_map/ppermute | solution.py:308

commit v8 on v7

--- a/solution.py
+++ b/solution.py
@@ -244,7 +244,7 @@
         e[t] = real + imag
         return carry
 
-    lax.fori_loop(0, frames, split, 0, unroll=8)
+    lax.fori_loop(0, frames, split, 0, unroll=64)
 
     def step(t, sums):
         return tuple(
@@ -253,7 +253,7 @@
         )
 
     zero = (jnp.zeros((8, 128), jnp.float32),) * LAGS
-    sums_d, sums_e = lax.fori_loop(0, frames, step, (zero, zero), unroll=8)
+    sums_d, sums_e = lax.fori_loop(0, frames, step, (zero, zero), unroll=16)
     for lag in range(LAGS):
         value = (sums_d[lag] + pltpu.roll(sums_e[lag], 64, 1)) * (1.0 / (ATOMS * (frames - lag)))
         rows[lag * 8 : lag * 8 + 8, :] = value

time: 50.9 us -> 49.8 us (0.978)
  Pallas kernels: 18.9 us -> 17.8 us
    pallas_call x1, Pallas kernels: 3.48 us -> 2.37 us  [correlate(): pl.pallas_call(correlate_kernel, out_shape=jax.ShapeDtypeStruct((4, LAGS,...]
where the time goes in v8:
time: 49.8 us; the launch traced here: 49.6 us
  blocking collectives  27.9 us (56%)
  Pallas kernels  17.8 us (36%)
  starting transfers between devices  3.73 us (7%)
    all_to_all x1, blocking collectives, exchange(): lax.all_to_all(local, ('atom', 'tm'), 0, 0, tiled=True, axis_index_groups...  27.9 us
    pallas_call x3, Pallas kernels, modes(): pl.pallas_call(functools.partial(modes_kernel, number, frames, more, last...  14.4 us
    ppermute x2, starting transfers between devices, swap(): return lax.ppermute(block, 'atom', [(i, i ^ 1) for i in range(8)])  2.41 us
    pallas_call x1, Pallas kernels, correlate(): pl.pallas_call(correlate_kernel, out_shape=jax.ShapeDtypeStruct((4, LAGS,...  2.37 us
    ppermute x1, starting transfers between devices, across(): return lax.ppermute(block, 'atom', [(i, i ^ 2) for i in range(8)])  1.32 us
    pallas_call x1, Pallas kernels, prepare(): pl.pallas_call(prepare_kernel, out_shape=jax.ShapeDtypeStruct((frames, 9,...  1.09 us
  transfers between devices with their start and end apart: 3, of which 1 were waited for; matrix products, arithmetic and copies ran while one was open for 0% of the time, Pallas kernels for 21%

profile of v8, /device:TPU:1, one launch (start us, length us, event | category | flops | bytes accessed | tf_op | source)
XLA Modules:
  0.0 49.6 jit_solution(5880628995002336444)
XLA Ops:
  0.0 1.1 %prepare.1.refs_0_ = bf16[8,9,16,128]{3,2,1,0:T(8,128)(2,1)S(1)} custom-call(s32[3,8,2048]{2,1,0:T(8,128)} %bitcast.4, bf16[3,8,2048]{2,1,0:T(8,128)(2,1)} %bitcast.5), custom_call_target="tpu_custom_call" | custom-call | tf_op jit(solution)/shard_map/prepare/pallas_call | solution.py:106
  1.1 1.5 %collective-permute-start.1 = (bf16[8,9,16,128]{3,2,1,0:T(8,128)(2,1)S(1)}, bf16[8,9,16,128]{3,2,1,0:T(8,128)(2,1)S(1)}, u32[]{:S(2)}, u32[]{:S(2)}) collective-permute-start(bf16[8,9,16,128]{3,2,1,0:T(8,128)(2,1)S(1)} %prepare.1.refs_0_), channel_id=1, source_target_pairs={{0,16},{16,0},{32,48},{48,32},{64,80},{80,64},{96,112},{112,96},{1... | collective-permute-start | bytes 884744 | tf_op jit(solution)/shard_map/ppermute | solution.py:308
  2.6 1.3 %collective-permute-start = (bf16[8,9,16,128]{3,2,1,0:T(8,128)(2,1)S(1)}, bf16[8,9,16,128]{3,2,1,0:T(8,128)(2,1)S(1)}, u32[]{:S(2)}, u32[]{:S(2)}) collective-permute-start(bf16[8,9,16,128]{3,2,1,0:T(8,128)(2,1)S(1)} %prepare.1.refs_0_), channel_id=1, source_target_pairs={{0,32},{16,48},{32,0},{48,16},{64,96},{80,112},{96,64},{112,80},{1... | collective-permute-start | bytes 884744 | tf_op jit(solution)/shard_map/ppermute | solution.py:304
  3.9 0.0 collective-permute-done.1.refs_1_
  3.9 7.0 %nearby0.1.refs_1_ = f32[8,256,128]{2,1,0:T(8,128)S(1)} custom-call(bf16[8,9,16,128]{3,2,1,0:T(8,128)(2,1)S(1)} %prepare.1.refs_0_, bf16[8,9,16,128]{3,2,1,0:T(8,128)(2,1)S(1)} %collective-permute-done.1.refs_1_), custom_call_target="tpu_custom_call" | custom-call | flops 2147483648 | bytes 589824 | tf_op jit(solution)/shard_map/nearby0/pallas_call | solution.py:213
  10.9 0.1 collective-permute-done.refs_0_
  11.0 0.9 %collective-permute-start.2 = (bf16[8,9,16,128]{3,2,1,0:T(8,128)(2,1)S(1)}, bf16[8,9,16,128]{3,2,1,0:T(8,128)(2,1)S(1)}, u32[]{:S(2)}, u32[]{:S(2)}) collective-permute-start(bf16[8,9,16,128]{3,2,1,0:T(8,128)(2,1)S(1)} %collective-permute-done.refs_0_), channel_id=1, source_target_pairs={{0,16},{16,0},{32,48},{48,32},{64,80},{80,64},{96,112},{112,96},{1... | collective-permute-start | bytes 884744 | tf_op jit(solution)/shard_map/ppermute | solution.py:308
  12.0 3.6 %nearby1.1.refs_1_ = f32[8,256,128]{2,1,0:T(8,128)S(1)} custom-call(bf16[8,9,16,128]{3,2,1,0:T(8,128)(2,1)S(1)} %collective-permute-done.refs_0_, f32[8,256,128]{2,1,0:T(8,128)S(1)} %nearby0.1.refs_1_), custom_call_target="tpu_custom_call", output_to_operand_aliasing={{}: (1, {})} | custom-call | flops 1073741824 | bytes 294912 | tf_op jit(solution)/shard_map/nearby1/pallas_call | solution.py:213
  15.6 0.0 collective-permute-done.2.refs_0_
  15.7 3.7 %last.1 = bf16[32,8,16,128]{3,2,1,0:T(8,128)(2,1)S(1)} custom-call(bf16[8,9,16,128]{3,2,1,0:T(8,128)(2,1)S(1)} %collective-permute-done.2.refs_0_, f32[8,256,128]{2,1,0:T(8,128)S(1)} %nearby1.1.refs_1_), custom_call_target="tpu_custom_call" | custom-call | flops 1073741824 | bytes 294912 | tf_op jit(solution)/shard_map/last/pallas_call | solution.py:213
  19.4 27.9 %all_to_all.5 = bf16[32,8,16,128]{3,2,1,0:T(8,128)(2,1)S(1)} all-to-all(bf16[32,8,16,128]{3,2,1,0:T(8,128)(2,1)S(1)} %last.1), channel_id=1, replica_groups={{0,1,2,3,4,5,6,7,8,9,10,11,12,13,14,15,112,113,114,115,116,117,118,119,..., dimensions={0} | all-to-all | bytes 2097152 | tf_op jit(solution)/shard_map/all_to_all | solution.py:313
  47.2 2.4 %correlate.1 = f32[4,16,256]{2,1,0:T(8,128)} custom-call(bf16[2,128,16,128]{3,2,1,0:T(8,128)(2,1)S(1)} %bitcast.3), custom_call_target="tpu_custom_call" | custom-call | tf_op jit(solution)/shard_map/correlate/pallas_call | solution.py:288
Async XLA Ops:
  1.1 2.8 %collective-permute-start.1 = (bf16[8,9,16,128]{3,2,1,0:T(8,128)(2,1)S(1)}, bf16[8,9,16,128]{3,2,1,0:T(8,128)(2,1)S(1)}, u32[]{:S(2)}, u32[]{:S(2)}) collective-permute-start(bf16[8,9,16,128]{3,2,1,0:T(8,128)(2,1)S(1)} %prepare.1.refs_0_), channel_id=1, source_target_pairs={{0,16},{16,0},{32,48},{48,32},{64,80},{80,64},{96,112},{112,96},{1... | collective-permute-start | bytes 884744 | tf_op jit(solution)/shard_map/ppermute | solution.py:308
  2.6 8.5 %collective-permute-start = (bf16[8,9,16,128]{3,2,1,0:T(8,128)(2,1)S(1)}, bf16[8,9,16,128]{3,2,1,0:T(8,128)(2,1)S(1)}, u32[]{:S(2)}, u32[]{:S(2)}) collective-permute-start(bf16[8,9,16,128]{3,2,1,0:T(8,128)(2,1)S(1)} %prepare.1.refs_0_), channel_id=1, source_target_pairs={{0,32},{16,48},{32,0},{48,16},{64,96},{80,112},{96,64},{112,80},{1... | collective-permute-start | bytes 884744 | tf_op jit(solution)/shard_map/ppermute | solution.py:304
  11.0 4.6 %collective-permute-start.2 = (bf16[8,9,16,128]{3,2,1,0:T(8,128)(2,1)S(1)}, bf16[8,9,16,128]{3,2,1,0:T(8,128)(2,1)S(1)}, u32[]{:S(2)}, u32[]{:S(2)}) collective-permute-start(bf16[8,9,16,128]{3,2,1,0:T(8,128)(2,1)S(1)} %collective-permute-done.refs_0_), channel_id=1, source_target_pairs={{0,16},{16,0},{32,48},{48,32},{64,80},{80,64},{96,112},{112,96},{1... | collective-permute-start | bytes 884744 | tf_op jit(solution)/shard_map/ppermute | solution.py:308

commit v9 on v8

--- a/solution.py
+++ b/solution.py
@@ -16,6 +16,7 @@
 ATOMS = 16384
 FRAMES = 128
 HALF = 16
+ORDER = (26, 17, 11, 10, 28, 1, 5, 4, 7, 16, 9, 19, 30, 13, 22, 0, 21, 29, 6, 12, 20, 23, 14, 15, 3, 31, 2, 24, 25, 27, 18, 8)
 LINK = jnp.bfloat16
 WIDTH = 2
 SPREAD = 136
@@ -200,8 +201,8 @@
                 minus, outer = b < 2, b in (0, 3)
                 here = 64 * i + 32 * outer + 16 * minus
                 there = 64 * (3 - i) + 32 * outer + 16 * (not minus)
-                out[i * 4 + b, f] = total[there : there + 16]
-                out[16 + i * 4 + b, f] = total[here : here + 16]
+                out[ORDER.index(i * 4 + b), f] = total[there : there + 16]
+                out[ORDER.index(16 + i * 4 + b), f] = total[here : here + 16]
 
 
 def modes(blocks, before=None, last=False):
@@ -237,14 +238,14 @@
     d[frames:, :, :] = jnp.zeros((LAGS, 8, 128), jnp.float32)
     e[frames:, :, :] = jnp.zeros((LAGS, 8, 128), jnp.float32)
 
-    def split(t, carry):
-        values = series[0, t].astype(jnp.float32) + series[1, t].astype(jnp.float32)
+    for t in range(frames):
+        source, f = divmod(t, series.shape[1])
+        values = sum(
+            series[ORDER.index(side * 16 + source), f].astype(jnp.float32) for side in range(2)
+        )
         real, imag = values[:8], pltpu.roll(values[8:], 64, 1)
         d[t] = real - imag
         e[t] = real + imag
-        return carry
-
-    lax.fori_loop(0, frames, split, 0, unroll=64)
 
     def step(t, sums):
         return tuple(
@@ -309,11 +310,10 @@
 
 
 def exchange(local):
-    groups = [[a * 16 + t for a in (lower, 7 - lower) for t in range(16)] for lower in range(4)]
-    series = lax.all_to_all(
-        local, ("atom", "tm"), 0, 0, tiled=True, axis_index_groups=groups
-    )
-    return series.reshape(2, FRAMES, 16, 128)
+    groups = [
+        [(7 - lower if at // 16 else lower) * 16 + at % 16 for at in ORDER] for lower in range(4)
+    ]
+    return lax.all_to_all(local, ("atom", "tm"), 0, 0, tiled=True, axis_index_groups=groups)
 
 
 def per_device(positions, velocity):

time: 49.8 us -> 47.3 us (0.950)
  blocking collectives: 27.9 us -> 25.5 us
    all_to_all x1, blocking collectives: 27.9 us -> 25.5 us  [exchange(): lax.all_to_all(local, ('atom', 'tm'), 0, 0, tiled=True, axis_index_groups...]
  transfers between devices with their start and end apart: 3 -> 3, of which waited for: 1 -> 1; matrix products, arithmetic and copies ran while one was open for 0% -> 0% of each run, Pallas kernels for 21% -> 23%
where the time goes in v9:
time: 47.3 us; the launch traced here: 47.2 us
  blocking collectives  25.5 us (54%)
  Pallas kernels  17.7 us (37%)
  starting transfers between devices  3.73 us (8%)
    all_to_all x1, blocking collectives, exchange(): lax.all_to_all(local, ('atom', 'tm'), 0, 0, tiled=True, axis_index_groups...  25.5 us
    pallas_call x3, Pallas kernels, modes(): pl.pallas_call(functools.partial(modes_kernel, number, frames, more, last...  14.4 us
    ppermute x2, starting transfers between devices, swap(): return lax.ppermute(block, 'atom', [(i, i ^ 1) for i in range(8)])  2.41 us
    pallas_call x1, Pallas kernels, correlate(): pl.pallas_call(correlate_kernel, out_shape=jax.ShapeDtypeStruct((4, LAGS,...  2.28 us
    ppermute x1, starting transfers between devices, across(): return lax.ppermute(block, 'atom', [(i, i ^ 2) for i in range(8)])  1.32 us
    pallas_call x1, Pallas kernels, prepare(): pl.pallas_call(prepare_kernel, out_shape=jax.ShapeDtypeStruct((frames, 9,...  1.09 us
  transfers between devices with their start and end apart: 3, of which 1 were waited for; matrix products, arithmetic and copies ran while one was open for 0% of the time, Pallas kernels for 23%

profile of v9, /device:TPU:1, one launch (start us, length us, event | category | flops | bytes accessed | tf_op | source)
XLA Modules:
  0.0 47.2 jit_solution(4972790717371130962)
XLA Ops:
  0.0 1.1 %prepare.1.refs_0_ = bf16[8,9,16,128]{3,2,1,0:T(8,128)(2,1)S(1)} custom-call(s32[3,8,2048]{2,1,0:T(8,128)} %bitcast.2, bf16[3,8,2048]{2,1,0:T(8,128)(2,1)} %bitcast.3), custom_call_target="tpu_custom_call" | custom-call | tf_op jit(solution)/shard_map/prepare/pallas_call | solution.py:107
  1.1 1.5 %collective-permute-start.1 = (bf16[8,9,16,128]{3,2,1,0:T(8,128)(2,1)S(1)}, bf16[8,9,16,128]{3,2,1,0:T(8,128)(2,1)S(1)}, u32[]{:S(2)}, u32[]{:S(2)}) collective-permute-start(bf16[8,9,16,128]{3,2,1,0:T(8,128)(2,1)S(1)} %prepare.1.refs_0_), channel_id=1, source_target_pairs={{0,16},{16,0},{32,48},{48,32},{64,80},{80,64},{96,112},{112,96},{1... | collective-permute-start | bytes 884744 | tf_op jit(solution)/shard_map/ppermute | solution.py:309
  2.6 1.3 %collective-permute-start = (bf16[8,9,16,128]{3,2,1,0:T(8,128)(2,1)S(1)}, bf16[8,9,16,128]{3,2,1,0:T(8,128)(2,1)S(1)}, u32[]{:S(2)}, u32[]{:S(2)}) collective-permute-start(bf16[8,9,16,128]{3,2,1,0:T(8,128)(2,1)S(1)} %prepare.1.refs_0_), channel_id=1, source_target_pairs={{0,32},{16,48},{32,0},{48,16},{64,96},{80,112},{96,64},{112,80},{1... | collective-permute-start | bytes 884744 | tf_op jit(solution)/shard_map/ppermute | solution.py:305
  3.9 0.0 collective-permute-done.1.refs_1_
  3.9 7.0 %nearby0.1.refs_1_ = f32[8,256,128]{2,1,0:T(8,128)S(1)} custom-call(bf16[8,9,16,128]{3,2,1,0:T(8,128)(2,1)S(1)} %prepare.1.refs_0_, bf16[8,9,16,128]{3,2,1,0:T(8,128)(2,1)S(1)} %collective-permute-done.1.refs_1_), custom_call_target="tpu_custom_call" | custom-call | flops 2147483648 | bytes 589824 | tf_op jit(solution)/shard_map/nearby0/pallas_call | solution.py:214
  10.9 0.1 collective-permute-done.refs_0_
  11.0 0.9 %collective-permute-start.2 = (bf16[8,9,16,128]{3,2,1,0:T(8,128)(2,1)S(1)}, bf16[8,9,16,128]{3,2,1,0:T(8,128)(2,1)S(1)}, u32[]{:S(2)}, u32[]{:S(2)}) collective-permute-start(bf16[8,9,16,128]{3,2,1,0:T(8,128)(2,1)S(1)} %collective-permute-done.refs_0_), channel_id=1, source_target_pairs={{0,16},{16,0},{32,48},{48,32},{64,80},{80,64},{96,112},{112,96},{1... | collective-permute-start | bytes 884744 | tf_op jit(solution)/shard_map/ppermute | solution.py:309
  12.0 3.6 %nearby1.1.refs_1_ = f32[8,256,128]{2,1,0:T(8,128)S(1)} custom-call(bf16[8,9,16,128]{3,2,1,0:T(8,128)(2,1)S(1)} %collective-permute-done.refs_0_, f32[8,256,128]{2,1,0:T(8,128)S(1)} %nearby0.1.refs_1_), custom_call_target="tpu_custom_call", output_to_operand_aliasing={{}: (1, {})} | custom-call | flops 1073741824 | bytes 294912 | tf_op jit(solution)/shard_map/nearby1/pallas_call | solution.py:214
  15.6 0.0 collective-permute-done.2.refs_0_
  15.7 3.7 %last.1 = bf16[32,8,16,128]{3,2,1,0:T(8,128)(2,1)S(1)} custom-call(bf16[8,9,16,128]{3,2,1,0:T(8,128)(2,1)S(1)} %collective-permute-done.2.refs_0_, f32[8,256,128]{2,1,0:T(8,128)S(1)} %nearby1.1.refs_1_), custom_call_target="tpu_custom_call" | custom-call | flops 1073741824 | bytes 294912 | tf_op jit(solution)/shard_map/last/pallas_call | solution.py:214
  19.4 25.5 %all_to_all.5.series = bf16[32,8,16,128]{3,2,1,0:T(8,128)(2,1)S(1)} all-to-all(bf16[32,8,16,128]{3,2,1,0:T(8,128)(2,1)S(1)} %last.1), channel_id=1, replica_groups={{122,113,11,10,124,1,5,4,7,112,9,115,126,13,118,0,117,125,6,12,116,119,..., dimensions={0} | all-to-all | bytes 2097152 | tf_op jit(solution)/shard_map/all_to_all | solution.py:316
  44.9 2.3 %correlate.1 = f32[4,16,256]{2,1,0:T(8,128)} custom-call(bf16[32,8,16,128]{3,2,1,0:T(8,128)(2,1)S(1)} %all_to_all.5.series), custom_call_target="tpu_custom_call" | custom-call | tf_op jit(solution)/shard_map/correlate/pallas_call | solution.py:289
Async XLA Ops:
  1.1 2.8 %collective-permute-start.1 = (bf16[8,9,16,128]{3,2,1,0:T(8,128)(2,1)S(1)}, bf16[8,9,16,128]{3,2,1,0:T(8,128)(2,1)S(1)}, u32[]{:S(2)}, u32[]{:S(2)}) collective-permute-start(bf16[8,9,16,128]{3,2,1,0:T(8,128)(2,1)S(1)} %prepare.1.refs_0_), channel_id=1, source_target_pairs={{0,16},{16,0},{32,48},{48,32},{64,80},{80,64},{96,112},{112,96},{1... | collective-permute-start | bytes 884744 | tf_op jit(solution)/shard_map/ppermute | solution.py:309
  2.6 8.5 %collective-permute-start = (bf16[8,9,16,128]{3,2,1,0:T(8,128)(2,1)S(1)}, bf16[8,9,16,128]{3,2,1,0:T(8,128)(2,1)S(1)}, u32[]{:S(2)}, u32[]{:S(2)}) collective-permute-start(bf16[8,9,16,128]{3,2,1,0:T(8,128)(2,1)S(1)} %prepare.1.refs_0_), channel_id=1, source_target_pairs={{0,32},{16,48},{32,0},{48,16},{64,96},{80,112},{96,64},{112,80},{1... | collective-permute-start | bytes 884744 | tf_op jit(solution)/shard_map/ppermute | solution.py:305
  11.0 4.6 %collective-permute-start.2 = (bf16[8,9,16,128]{3,2,1,0:T(8,128)(2,1)S(1)}, bf16[8,9,16,128]{3,2,1,0:T(8,128)(2,1)S(1)}, u32[]{:S(2)}, u32[]{:S(2)}) collective-permute-start(bf16[8,9,16,128]{3,2,1,0:T(8,128)(2,1)S(1)} %collective-permute-done.refs_0_), channel_id=1, source_target_pairs={{0,16},{16,0},{32,48},{48,32},{64,80},{80,64},{96,112},{112,96},{1... | collective-permute-start | bytes 884744 | tf_op jit(solution)/shard_map/ppermute | solution.py:309

commit v10 on v9

--- a/solution.py
+++ b/solution.py
@@ -16,7 +16,7 @@
 ATOMS = 16384
 FRAMES = 128
 HALF = 16
-ORDER = (26, 17, 11, 10, 28, 1, 5, 4, 7, 16, 9, 19, 30, 13, 22, 0, 21, 29, 6, 12, 20, 23, 14, 15, 3, 31, 2, 24, 25, 27, 18, 8)
+ORDER = (27, 11, 0, 13, 29, 25, 31, 18, 17, 10, 5, 3, 4, 1, 15, 26, 12, 30, 21, 14, 2, 9, 28, 23, 8, 7, 16, 20, 24, 22, 19, 6)
 LINK = jnp.bfloat16
 WIDTH = 2
 SPREAD = 136

time: 47.3 us -> 46.5 us (0.983)
  blocking collectives: 25.5 us -> 24.7 us
    all_to_all x1, blocking collectives: 25.5 us -> 24.7 us  [exchange(): lax.all_to_all(local, ('atom', 'tm'), 0, 0, tiled=True, axis_index_groups...]
where the time goes in v10:
time: 46.5 us; the launch traced here: 46.3 us
  blocking collectives  24.7 us (53%)
  Pallas kernels  17.7 us (38%)
  starting transfers between devices  3.73 us (8%)
    all_to_all x1, blocking collectives, exchange(): lax.all_to_all(local, ('atom', 'tm'), 0, 0, tiled=True, axis_index_groups...  24.7 us
    pallas_call x3, Pallas kernels, modes(): pl.pallas_call(functools.partial(modes_kernel, number, frames, more, last...  14.4 us
    ppermute x2, starting transfers between devices, swap(): return lax.ppermute(block, 'atom', [(i, i ^ 1) for i in range(8)])  2.41 us
    pallas_call x1, Pallas kernels, correlate(): pl.pallas_call(correlate_kernel, out_shape=jax.ShapeDtypeStruct((4, LAGS,...  2.28 us
    ppermute x1, starting transfers between devices, across(): return lax.ppermute(block, 'atom', [(i, i ^ 2) for i in range(8)])  1.32 us
    pallas_call x1, Pallas kernels, prepare(): pl.pallas_call(prepare_kernel, out_shape=jax.ShapeDtypeStruct((frames, 9,...  1.09 us
  transfers between devices with their start and end apart: 3, of which 1 were waited for; matrix products, arithmetic and copies ran while one was open for 0% of the time, Pallas kernels for 23%

profile of v10, /device:TPU:1, one launch (start us, length us, event | category | flops | bytes accessed | tf_op | source)
XLA Modules:
  0.0 46.3 jit_solution(8423800460726764382)
XLA Ops:
  0.0 1.1 %prepare.1.refs_0_ = bf16[8,9,16,128]{3,2,1,0:T(8,128)(2,1)S(1)} custom-call(s32[3,8,2048]{2,1,0:T(8,128)} %bitcast.2, bf16[3,8,2048]{2,1,0:T(8,128)(2,1)} %bitcast.3), custom_call_target="tpu_custom_call" | custom-call | tf_op jit(solution)/shard_map/prepare/pallas_call | solution.py:107
  1.1 1.5 %collective-permute-start.1 = (bf16[8,9,16,128]{3,2,1,0:T(8,128)(2,1)S(1)}, bf16[8,9,16,128]{3,2,1,0:T(8,128)(2,1)S(1)}, u32[]{:S(2)}, u32[]{:S(2)}) collective-permute-start(bf16[8,9,16,128]{3,2,1,0:T(8,128)(2,1)S(1)} %prepare.1.refs_0_), channel_id=1, source_target_pairs={{0,16},{16,0},{32,48},{48,32},{64,80},{80,64},{96,112},{112,96},{1... | collective-permute-start | bytes 884744 | tf_op jit(solution)/shard_map/ppermute | solution.py:309
  2.6 1.3 %collective-permute-start = (bf16[8,9,16,128]{3,2,1,0:T(8,128)(2,1)S(1)}, bf16[8,9,16,128]{3,2,1,0:T(8,128)(2,1)S(1)}, u32[]{:S(2)}, u32[]{:S(2)}) collective-permute-start(bf16[8,9,16,128]{3,2,1,0:T(8,128)(2,1)S(1)} %prepare.1.refs_0_), channel_id=1, source_target_pairs={{0,32},{16,48},{32,0},{48,16},{64,96},{80,112},{96,64},{112,80},{1... | collective-permute-start | bytes 884744 | tf_op jit(solution)/shard_map/ppermute | solution.py:305
  3.9 0.0 collective-permute-done.1.refs_1_
  3.9 7.0 %nearby0.1.refs_1_ = f32[8,256,128]{2,1,0:T(8,128)S(1)} custom-call(bf16[8,9,16,128]{3,2,1,0:T(8,128)(2,1)S(1)} %prepare.1.refs_0_, bf16[8,9,16,128]{3,2,1,0:T(8,128)(2,1)S(1)} %collective-permute-done.1.refs_1_), custom_call_target="tpu_custom_call" | custom-call | flops 2147483648 | bytes 589824 | tf_op jit(solution)/shard_map/nearby0/pallas_call | solution.py:214
  10.9 0.1 collective-permute-done.refs_0_
  11.0 0.9 %collective-permute-start.2 = (bf16[8,9,16,128]{3,2,1,0:T(8,128)(2,1)S(1)}, bf16[8,9,16,128]{3,2,1,0:T(8,128)(2,1)S(1)}, u32[]{:S(2)}, u32[]{:S(2)}) collective-permute-start(bf16[8,9,16,128]{3,2,1,0:T(8,128)(2,1)S(1)} %collective-permute-done.refs_0_), channel_id=1, source_target_pairs={{0,16},{16,0},{32,48},{48,32},{64,80},{80,64},{96,112},{112,96},{1... | collective-permute-start | bytes 884744 | tf_op jit(solution)/shard_map/ppermute | solution.py:309
  12.0 3.6 %nearby1.1.refs_1_ = f32[8,256,128]{2,1,0:T(8,128)S(1)} custom-call(bf16[8,9,16,128]{3,2,1,0:T(8,128)(2,1)S(1)} %collective-permute-done.refs_0_, f32[8,256,128]{2,1,0:T(8,128)S(1)} %nearby0.1.refs_1_), custom_call_target="tpu_custom_call", output_to_operand_aliasing={{}: (1, {})} | custom-call | flops 1073741824 | bytes 294912 | tf_op jit(solution)/shard_map/nearby1/pallas_call | solution.py:214
  15.6 0.0 collective-permute-done.2.refs_0_
  15.7 3.7 %last.1 = bf16[32,8,16,128]{3,2,1,0:T(8,128)(2,1)S(1)} custom-call(bf16[8,9,16,128]{3,2,1,0:T(8,128)(2,1)S(1)} %collective-permute-done.2.refs_0_, f32[8,256,128]{2,1,0:T(8,128)S(1)} %nearby1.1.refs_1_), custom_call_target="tpu_custom_call" | custom-call | flops 1073741824 | bytes 294912 | tf_op jit(solution)/shard_map/last/pallas_call | solution.py:214
  19.4 24.7 %all_to_all.5.series = bf16[32,8,16,128]{3,2,1,0:T(8,128)(2,1)S(1)} all-to-all(bf16[32,8,16,128]{3,2,1,0:T(8,128)(2,1)S(1)} %last.1), channel_id=1, replica_groups={{123,11,0,13,125,121,127,114,113,10,5,3,4,1,15,122,12,126,117,14,2,9,12..., dimensions={0} | all-to-all | bytes 2097152 | tf_op jit(solution)/shard_map/all_to_all | solution.py:316
  44.1 2.3 %correlate.1 = f32[4,16,256]{2,1,0:T(8,128)} custom-call(bf16[32,8,16,128]{3,2,1,0:T(8,128)(2,1)S(1)} %all_to_all.5.series), custom_call_target="tpu_custom_call" | custom-call | tf_op jit(solution)/shard_map/correlate/pallas_call | solution.py:289
Async XLA Ops:
  1.1 2.8 %collective-permute-start.1 = (bf16[8,9,16,128]{3,2,1,0:T(8,128)(2,1)S(1)}, bf16[8,9,16,128]{3,2,1,0:T(8,128)(2,1)S(1)}, u32[]{:S(2)}, u32[]{:S(2)}) collective-permute-start(bf16[8,9,16,128]{3,2,1,0:T(8,128)(2,1)S(1)} %prepare.1.refs_0_), channel_id=1, source_target_pairs={{0,16},{16,0},{32,48},{48,32},{64,80},{80,64},{96,112},{112,96},{1... | collective-permute-start | bytes 884744 | tf_op jit(solution)/shard_map/ppermute | solution.py:309
  2.6 8.5 %collective-permute-start = (bf16[8,9,16,128]{3,2,1,0:T(8,128)(2,1)S(1)}, bf16[8,9,16,128]{3,2,1,0:T(8,128)(2,1)S(1)}, u32[]{:S(2)}, u32[]{:S(2)}) collective-permute-start(bf16[8,9,16,128]{3,2,1,0:T(8,128)(2,1)S(1)} %prepare.1.refs_0_), channel_id=1, source_target_pairs={{0,32},{16,48},{32,0},{48,16},{64,96},{80,112},{96,64},{112,80},{1... | collective-permute-start | bytes 884744 | tf_op jit(solution)/shard_map/ppermute | solution.py:305
  11.0 4.6 %collective-permute-start.2 = (bf16[8,9,16,128]{3,2,1,0:T(8,128)(2,1)S(1)}, bf16[8,9,16,128]{3,2,1,0:T(8,128)(2,1)S(1)}, u32[]{:S(2)}, u32[]{:S(2)}) collective-permute-start(bf16[8,9,16,128]{3,2,1,0:T(8,128)(2,1)S(1)} %collective-permute-done.refs_0_), channel_id=1, source_target_pairs={{0,16},{16,0},{32,48},{48,32},{64,80},{80,64},{96,112},{112,96},{1... | collective-permute-start | bytes 884744 | tf_op jit(solution)/shard_map/ppermute | solution.py:309
